TPU v7x, 32 devices: a whole 2x2x4 slice. The times are simulated.
32 devices in a mesh: row: 4 (over z), col: 8 (over y, x, core).
Axes of the slice: x: 2, y: 2, z: 4, core: 2. Of those that a mesh axis runs over, the one named last changes fastest.
Arguments:
- rhs_window: float32 [4, 4096, 256], P(None, 'row'), may hold values from -6 to 6
- rhs_below: float32 [32768, 256], P(('row', 'col')), may hold values from -6 to 6
- dinv: bfloat16 [4, 4096, 4096], P(None, 'col', 'row'), as said below
- couple: bfloat16 [6, 4096, 4096], P(None, 'row', 'col'), may hold values from -0.0546875 to 0.0546875
- window_mask: int32 [6, 32], P(None, 'row'), may hold values 0 or 1
- below_factor: bfloat16 [4, 32768, 4096], P(None, 'row', 'col'), may hold values from -0.0625 to 0.0625
- below_mask: int32 [4, 256], P(None, 'row'), may hold values 0 or 1
Outputs:
- solution: float32 [4, 4096, 256], P(None, 'col')
- below_rhs: float32 [32768, 256], P(('row', 'col'))
Inputs may be any that keep to these rules, and one draw needn't show every extreme that they name: Each block of dinv is lower triangular with a positive diagonal.
All inputs are finite; a program needn't handle non-finite values. No bound on the sum of `window_mask` or of `below_mask` on one device may be relied on, other than what follows from the above.
Results may differ from a plain program's by a relative error of at most 0.0065.
Values sent between devices are 32-bit elements; how exact they have to be, the bound alone decides.
No kernel may reach another device: no remote copies, remote signals or barrier semaphores. Data moves between devices by JAX's collectives and lax.ppermute only.
A program may use at most 128 MiB of HBM per device.

v0:
```python
import jax
import jax.numpy as jnp
from jax import lax
from jax.sharding import PartitionSpec as P

BLK = 128
PANELS = 4


def local(rhs_window, rhs_below, dinv, couple, window_mask, below_factor, below_mask):
    window_gain = jnp.repeat(window_mask.astype(jnp.float32), BLK, axis=1)
    below_gain = jnp.repeat(below_mask.astype(jnp.float32), BLK, axis=1)
    own_rows = rhs_below.shape[0]
    solutions = []
    solved_list = []
    for target in range(PANELS):
        right_part = rhs_window[target]
        if target > 0:
            partial_value = jnp.zeros(right_part.shape, jnp.float32)
            for source in range(target):
                pair_index = target * (target - 1) // 2 + source
                product = jnp.dot(
                    couple[pair_index], solved_list[source], preferred_element_type=jnp.float32
                )
                partial_value = partial_value + window_gain[pair_index][:, None] * product
            partial_value = lax.psum(partial_value, "col")
            right_part = right_part - partial_value
        reduced = right_part.astype(jnp.bfloat16)
        local_part = jnp.dot(dinv[target], reduced, preferred_element_type=jnp.float32)
        solved = lax.psum(local_part, "row")
        solved_bf = solved.astype(jnp.bfloat16)
        solutions.append(solved)
        solved_list.append(solved_bf)
    term = jnp.zeros((lax.axis_size("col") * own_rows, rhs_below.shape[1]), jnp.float32)
    for panel in range(PANELS):
        factor_rows = below_factor[panel]
        row_gain = below_gain[panel]
        product = jnp.dot(factor_rows, solved_list[panel], preferred_element_type=jnp.float32)
        term = term + row_gain[:, None] * product
    below_sum = lax.psum_scatter(term, "col", scatter_dimension=0, tiled=True)
    return (jnp.stack(solutions), rhs_below - below_sum)


def solution(mesh):
    return jax.shard_map(
        local,
        mesh=mesh,
        in_specs=(
            P(None, "row", None),
            P(("row", "col"), None),
            P(None, "col", "row"),
            P(None, "row", "col"),
            P(None, "row"),
            P(None, "row", "col"),
            P(None, "row"),
        ),
        out_specs=(P(None, "col", None), P(("row", "col"), None)),
        check_vma=False,
    )
```

profile of v0, /device:TPU:0, one launch (start us, length us, event | category | flops | bytes accessed | tf_op | source)
XLA Modules:
  0.0 447.2 jit_solution(3852811574136104066)
XLA Ops:
  7.2 0.0 all-reduce.8.cloned.1.call-start
  7.2 2.8 fusion.30
  10.0 0.0 all-reduce.8.cloned.1.call-update
  10.0 0.0 all-reduce.10.cloned.1.call-start
  10.1 0.7 convert_element_type.32
  10.8 0.1 broadcast_bitcast_fusion.9
  10.8 0.7 convert_element_type.39
  11.5 0.1 broadcast_bitcast_fusion.6
  11.6 0.1 broadcast_bitcast_fusion.7
  11.7 40.3 %all-reduce.8.cloned.1.call-done = f32[512,256]{1,0:T(8,128)} async-done(((f32[512,256]{1,0:T(8,128)}), f32[512,256]{1,0:T(8,128)}) %all-reduce.8.cloned.1.call-update) | async-done | bytes 524304 | tf_op jit(solution)/shard_map/psum | solution.py:30
  51.9 1.1 convert_element_type.33
  53.0 2.6 fusion.17
  55.6 0.0 all-reduce.10.cloned.1.call-update
  55.7 0.0 all-reduce.12.cloned.1.call-start
  55.7 0.1 broadcast_bitcast_fusion.2
  55.8 0.1 broadcast_bitcast_fusion.3
  55.9 56.5 %all-reduce.10.cloned.1.call-done = f32[1024,256]{1,0:T(8,128)} async-done(((f32[1024,256]{1,0:T(8,128)}), f32[1024,256]{1,0:T(8,128)}) %all-reduce.10.cloned.1.call-update) | async-done | bytes 1048592 | tf_op jit(solution)/shard_map/psum | solution.py:26
  112.4 3.1 convolution_bitcast_fusion.2
  115.5 0.0 all-reduce.14.cloned.1.call-start
  115.6 0.1 broadcast_bitcast_fusion.5
  115.7 0.1 broadcast_bitcast_fusion.1
  115.7 1.7 convolution_multiply_fusion.8
  117.4 35.6 %all-reduce.12.cloned.1.call-done = f32[512,256]{1,0:T(8,128)} async-done(((f32[512,256]{1,0:T(8,128)}), f32[512,256]{1,0:T(8,128)}) %all-reduce.12.cloned.1.call-update) | async-done | bytes 524304 | tf_op jit(solution)/shard_map/psum | solution.py:30
  153.0 2.8 fusion.16
  155.9 0.0 all-reduce.16.cloned.1.call-start
  155.9 0.1 broadcast_bitcast_fusion.4
  156.0 0.1 broadcast_bitcast_fusion
  156.1 1.7 convolution_multiply_fusion.6
  157.7 55.5 %all-reduce.14.cloned.1.call-done = f32[1024,256]{1,0:T(8,128)} async-done(((f32[1024,256]{1,0:T(8,128)}), f32[1024,256]{1,0:T(8,128)}) %all-reduce.14.cloned.1.call-update) | async-done | bytes 1048592 | tf_op jit(solution)/shard_map/psum | solution.py:26
  213.2 3.1 convolution_bitcast_fusion.1
  216.4 0.0 all-reduce.18.cloned.1.call-start
  216.4 9.0 %convolution_multiply_fusion.2 = f32[256,8192]{1,0:T(8,128)} fusion(bf16[4,8192,512]{2,1,0:T(8,128)(2,1)} %param.12, f32[8192]{0:T(1024)S(1)} %broadcast_bitcast_fusion.2, f32[512,256]{1,0:T(8,128)S(1)} %copy-done.1), kind=kOutput, calls=%fused_computation.2 | convolution fusion | flops 2149711872 | bytes 17334272 | tf_op jit(solution)/shard_map/dot_general | solution.py:38
  225.4 1.7 fusion.14
  227.1 26.7 %all-reduce.16.cloned.1.call-done = f32[512,256]{1,0:T(8,128)} async-done(((f32[512,256]{1,0:T(8,128)}), f32[512,256]{1,0:T(8,128)}) %all-reduce.16.cloned.1.call-update) | async-done | bytes 524304 | tf_op jit(solution)/shard_map/psum | solution.py:30
  253.8 2.8 fusion.13
  256.6 0.0 all-reduce.20.cloned.1.call-start
  256.7 11.5 %fusion = f32[256,8192]{1,0:T(8,128)} fusion(f32[256,8192]{1,0:T(8,128)} %convolution_multiply_fusion.2, bf16[512,256]{1,0:T(8,128)(2,1)S(1)} %convert_element_type.33, bf16[4,8192,512]{2,1,0:T(8,128)(2,1)} %param.12, f32[8192]{0:T(1024)S(1)} %broadcast_bitcast_fusion.3), kind=kOutput, calls=%fused_computation.4 | convolution fusion | flops 2151677952 | bytes 25460736 | tf_op jit(solution)/shard_map/dot_general | solution.py:38
  268.2 45.9 %all-reduce.18.cloned.1.call-done = f32[1024,256]{1,0:T(8,128)} async-done(((f32[1024,256]{1,0:T(8,128)}), f32[1024,256]{1,0:T(8,128)}) %all-reduce.18.cloned.1.call-update) | async-done | bytes 1048592 | tf_op jit(solution)/shard_map/psum | solution.py:26
  314.0 3.1 convolution_bitcast_fusion
  317.2 0.2 reduce-scatter.2.cloned.1.call-start
  317.4 11.5 %fusion.1 = f32[256,8192]{1,0:T(8,128)} fusion(f32[256,8192]{1,0:T(8,128)} %fusion, bf16[4,8192,512]{2,1,0:T(8,128)(2,1)} %param.12, f32[8192]{0:T(1024)S(1)} %broadcast_bitcast_fusion.1, f32[512,256]{1,0:T(8,128)S(1)} %copy-done), kind=kOutput, calls=%fused_computation.5 | convolution fusion | flops 2151809024 | bytes 25722880 | tf_op jit(solution)/shard_map/dot_general | solution.py:38
  329.0 25.7 %all-reduce.20.cloned.1.call-done = f32[512,256]{1,0:T(8,128)} async-done(((f32[512,256]{1,0:T(8,128)}), f32[512,256]{1,0:T(8,128)}) %all-reduce.20.cloned.1.call-update) | async-done | bytes 524304 | tf_op jit(solution)/shard_map/psum | solution.py:30
  354.7 11.6 %fusion.3 = f32[8192,256]{0,1:T(8,128)} fusion(f32[256,8192]{1,0:T(8,128)} %fusion.1, bf16[4,8192,512]{2,1,0:T(8,128)(2,1)} %param.12, f32[8192]{0:T(1024)S(1)} %broadcast_bitcast_fusion, f32[512,256]{1,0:T(8,128)} %all-reduce.20.cloned.1.call-done), kind=kOutput, calls=%fused_computation.7 | convolution fusion | flops 2151809024 | bytes 25722880 | tf_op jit(solution)/shard_map/dot_general | solution.py:38
  366.3 1.6 copy.12
  367.9 1.5 pad_maximum_fusion
  369.4 68.3 %reduce-scatter.2.cloned.1.call-done = f32[1024,256]{0,1:T(8,128)} async-done(((f32[8192,256]{0,1:T(8,128)}), f32[1024,256]{0,1:T(8,128)}) %reduce-scatter.2.cloned.1.call-update) | async-done | bytes 1048592 | tf_op jit(solution)/shard_map/reduce_scatter | solution.py:40
  437.7 1.4 sub.15
  439.1 1.3 copy.13
  (16 shorter events, 0.1 us)
Async XLA Ops:
  7.2 44.8 %all-reduce.8.cloned.1.call-start = ((), (), s32[]{:S(2)}) async-start(), calls=%async_computation.1 | async-start | bytes 1048576 | tf_op jit(solution)/shard_map/psum | solution.py:30
  10.0 102.4 %all-reduce.10.cloned.1.call-start = ((), (), s32[]{:S(2)}) async-start(), calls=%async_computation.2 | async-start | bytes 2097152 | tf_op jit(solution)/shard_map/psum | solution.py:26
  55.7 97.4 %all-reduce.12.cloned.1.call-start = ((), (), s32[]{:S(2)}) async-start(), calls=%async_computation.3 | async-start | bytes 1048576 | tf_op jit(solution)/shard_map/psum | solution.py:30
  115.5 97.7 %all-reduce.14.cloned.1.call-start = ((), (), s32[]{:S(2)}) async-start(), calls=%async_computation.4 | async-start | bytes 2097152 | tf_op jit(solution)/shard_map/psum | solution.py:26
  153.0 63.4 %copy-start.1 = (f32[512,256]{1,0:T(8,128)S(1)}, f32[512,256]{1,0:T(8,128)}, u32[]{:S(2)}) copy-start(f32[512,256]{1,0:T(8,128)} %all-reduce.12.cloned.1.call-done) | copy-start | bytes 1572868
  155.9 98.0 %all-reduce.16.cloned.1.call-start = ((), (), s32[]{:S(2)}) async-start(), calls=%async_computation.5 | async-start | bytes 1048576 | tf_op jit(solution)/shard_map/psum | solution.py:30
  216.4 97.7 %all-reduce.18.cloned.1.call-start = ((), (), s32[]{:S(2)}) async-start(), calls=%async_computation.6 | async-start | bytes 2097152 | tf_op jit(solution)/shard_map/psum | solution.py:26
  256.6 60.8 %copy-start = (f32[512,256]{1,0:T(8,128)S(1)}, f32[512,256]{1,0:T(8,128)}, u32[]{:S(2)}) copy-start(f32[512,256]{1,0:T(8,128)} %all-reduce.16.cloned.1.call-done) | copy-start | bytes 1572868
  256.6 98.0 %all-reduce.20.cloned.1.call-start = ((), (), s32[]{:S(2)}) async-start(), calls=%async_computation.7 | async-start | bytes 1048576 | tf_op jit(solution)/shard_map/psum | solution.py:30
  317.2 120.5 %reduce-scatter.2.cloned.1.call-start = ((), (), s32[]{:S(2)}) async-start(), calls=%async_computation.8 | async-start | bytes 9437184 | tf_op jit(solution)/shard_map/reduce_scatter | solution.py:40
  366.2 1.7 copy-start.2
  366.2 1.7 copy-start.3
Sparse Core Ops, SparseCore 0:
  10.9 40.9 all-reduce.7
  55.8 56.5 all-reduce.9
  115.7 37.3 all-reduce.11
  156.6 56.5 all-reduce.13
  216.5 37.3 all-reduce.15
  257.4 56.5 all-reduce.17
  317.3 37.3 all-reduce.19
  366.4 71.2 reduce-scatter.1
where the time goes:
time: 448 us; the launch traced here: 447 us
  waiting for transfers between devices  355 us (79%)
  matrix products  68.9 us (15%)
  between operations  14.2 us (3%)
  other arithmetic  5.28 us (1%)
    psum x3, waiting for transfers between devices, local(): partial_value = lax.psum(partial_value, 'col')  158 us
    psum x4, waiting for transfers between devices, local(): solved = lax.psum(local_part, 'row')  128 us
    reduce_scatter x1, waiting for transfers between devices, local(): below_sum = lax.psum_scatter(term, 'col', scatter_dimension=0, tiled=True)  68.3 us
    dot_general x4, matrix products, local(): jnp.dot(factor_rows, solved_list[panel], preferred_element_type=jnp.float32)  43.6 us
    dot_general x6, matrix products, local(): jnp.dot(couple[pair_index], solved_list[source], preferred_element_type=j...  13.2 us
    dot_general x4, matrix products, local(): jnp.dot(dinv[target], reduced, preferred_element_type=jnp.float32)  12.1 us
  transfers between devices with their start and end apart: 8, of which 8 were waited for; matrix products, arithmetic and copies ran while one was open for 9% of the time, Pallas kernels for 0%

commit v1 on v0

v1 whole, which is shorter than its diff:
```python
import functools

import jax
import jax.numpy as jnp
from jax import lax
from jax.experimental import pallas as pl
from jax.experimental.pallas import tpu as pltpu
from jax.sharding import PartitionSpec as P

BLK = 128
PANELS = 4
F32 = jnp.float32


def swap(x, axis, mask):
    n = lax.axis_size(axis)
    return lax.ppermute(x, axis, [(i, i ^ mask) for i in range(n)])


def sum_parts(parts, axis, masks):
    parts = list(parts)
    for step in range(len(masks)):
        got = [swap(p, axis, masks[(step + j) % len(masks)]) for j, p in enumerate(parts)]
        parts = [p + g for p, g in zip(parts, got)]
    return parts


def halves(x):
    rows = x.shape[0] // 2
    return [x[:rows], x[rows:]]


def sum_rest(x, axis, masks):
    return jnp.concatenate(sum_parts(halves(x), axis, masks), axis=0)


def sum_paired(x, axis, masks):
    bit = lax.axis_index(axis) & 1
    rows = x.shape[0] // 2
    mine = lax.dynamic_slice_in_dim(x, bit * rows, rows, 0)
    other = lax.dynamic_slice_in_dim(x, (1 - bit) * rows, rows, 0)
    total = sum_rest(mine + swap(other, axis, 1), axis, masks)
    back = swap(total, axis, 1)
    low = jnp.where(bit == 0, total, back)
    high = jnp.where(bit == 0, back, total)
    return jnp.concatenate([low, high], axis=0)


def sum_row(x):
    n = lax.axis_size("row")
    return sum_rest(x, "row", (1, 3)) if n == 4 else sum_paired(x, "row", (2, 6))


def sum_col(x):
    n = lax.axis_size("col")
    return sum_paired(x, "col", tuple(2 << b for b in range(n.bit_length() - 2)))


def early_kernel(mask, f_ref, x_ref, o_ref):
    tile = o_ref.shape[0]
    base = pl.program_id(0) * (tile // BLK)
    for sub in range(tile // BLK):
        rows = pl.ds(sub * BLK, BLK)
        total = None
        for p in range(PANELS - 1):
            part = jnp.dot(f_ref[p, rows, :], x_ref[p], preferred_element_type=F32)
            part = part * mask[p, base + sub].astype(F32)
            total = part if total is None else total + part
        o_ref[rows, :] = total


def early_below(mask, factor, solved):
    _, rows, depth = factor.shape
    cols = solved.shape[-1]
    tile = min(1024, rows)
    return pl.pallas_call(
        early_kernel,
        out_shape=jax.ShapeDtypeStruct((rows, cols), F32),
        grid_spec=pltpu.PrefetchScalarGridSpec(
            num_scalar_prefetch=1,
            grid=(rows // tile,),
            in_specs=[
                pl.BlockSpec((PANELS - 1, tile, depth), lambda i, m: (0, i, 0)),
                pl.BlockSpec((PANELS - 1, depth, cols), lambda i, m: (0, 0, 0)),
            ],
            out_specs=pl.BlockSpec((tile, cols), lambda i, m: (i, 0)),
        ),
        cost_estimate=pl.CostEstimate(
            flops=2 * 3 * rows * depth * cols,
            bytes_accessed=6 * rows * depth + 4 * rows * cols,
            transcendentals=0,
        ),
        name="early_below",
    )(mask, factor, solved)


def last_kernel(part, mask, sel, f_ref, x_ref, a_ref, o_ref):
    tile = o_ref.shape[0]
    block = (2 * pl.program_id(0) + sel[0]) * 2 + part
    base = block * (tile // BLK)
    for sub in range(tile // BLK):
        rows = pl.ds(sub * BLK, BLK)
        term = jnp.dot(f_ref[0, rows, :], x_ref[...], preferred_element_type=F32)
        o_ref[rows, :] = a_ref[rows, :] + term * mask[PANELS - 1, base + sub].astype(F32)


def last_below(part, mask, sel, factor, solved, early, n):
    _, rows, depth = factor.shape
    cols = solved.shape[-1]
    tile = rows // n // 2

    def at(i, m, s):
        return (2 * i + s[0]) * 2 + part

    return pl.pallas_call(
        functools.partial(last_kernel, part),
        out_shape=jax.ShapeDtypeStruct((rows // 4, cols), F32),
        grid_spec=pltpu.PrefetchScalarGridSpec(
            num_scalar_prefetch=2,
            grid=(n // 2,),
            in_specs=[
                pl.BlockSpec((1, tile, depth), lambda i, m, s: (PANELS - 1, at(i, m, s), 0)),
                pl.BlockSpec((depth, cols), lambda i, m, s: (0, 0)),
                pl.BlockSpec((tile, cols), lambda i, m, s: (at(i, m, s), 0)),
            ],
            out_specs=pl.BlockSpec((tile, cols), lambda i, m, s: (i, 0)),
        ),
        cost_estimate=pl.CostEstimate(
            flops=rows * depth * cols // 2,
            bytes_accessed=rows * depth // 2 + 2 * rows * cols,
            transcendentals=0,
        ),
        name="last_below",
    )(mask, sel, factor, solved, early)


def scatter_rest(kept, order):
    me = lax.axis_index("col")
    left = list(range(kept.ndim - 2, 0, -1))
    for bit in order:
        dim = left.index(bit)
        mine = (me >> bit) & 1
        send = lax.dynamic_index_in_dim(kept, 1 - mine, dim, keepdims=False)
        keep = lax.dynamic_index_in_dim(kept, mine, dim, keepdims=False)
        left.remove(bit)
        kept = keep + swap(send, "col", 1 << bit)
    return kept


def local(rhs_window, rhs_below, dinv, couple, window_mask, below_factor, below_mask):
    window_gain = jnp.repeat(window_mask.astype(F32), BLK, axis=1)
    n = lax.axis_size("col")
    bits = n.bit_length() - 1
    me = lax.axis_index("col")
    solutions, solved = [], []
    for target in range(PANELS):
        right = rhs_window[target]
        if target > 0:
            partial = None
            for source in range(target):
                pair = target * (target - 1) // 2 + source
                product = jnp.dot(couple[pair], solved[source], preferred_element_type=F32)
                product = window_gain[pair][:, None] * product
                partial = product if partial is None else partial + product
            right = right - sum_col(partial)
        reduced = right.astype(jnp.bfloat16)
        total = sum_row(jnp.dot(dinv[target], reduced, preferred_element_type=F32))
        solutions.append(total)
        solved.append(total.astype(jnp.bfloat16))
    early = early_below(below_mask, below_factor, jnp.stack(solved[:-1]))
    mine = (me & 1).astype(jnp.int32)[None]
    sends = [
        swap(last_below(j, below_mask, 1 - mine, below_factor, solved[-1], early, n), "col", 1)
        for j in range(2)
    ]
    keeps = [last_below(j, below_mask, mine, below_factor, solved[-1], early, n) for j in range(2)]
    done = []
    for j in range(2):
        kept = keeps[j] + sends[j]
        kept = kept.reshape((2,) * (bits - 1) + (-1, kept.shape[-1]))
        order = list(range(1, bits))
        done.append(scatter_rest(kept, order[j:] + order[:j]))
    return (jnp.stack(solutions), rhs_below - jnp.concatenate(done, axis=0))


def solution(mesh):
    return jax.shard_map(
        local,
        mesh=mesh,
        in_specs=(
            P(None, "row", None),
            P(("row", "col"), None),
            P(None, "col", "row"),
            P(None, "row", "col"),
            P(None, "row"),
            P(None, "row", "col"),
            P(None, "row"),
        ),
        out_specs=(P(None, "col", None), P(("row", "col"), None)),
        check_vma=False,
    )
```

time: 448 us -> 292 us (0.65)
  waiting for transfers between devices: 355 us -> 152 us
  matrix products: 68.9 us -> 17.6 us
  starting transfers between devices: 0.51 us -> 43.9 us
  Pallas kernels: 0 us -> 38.9 us
  other arithmetic: 5.28 us -> 22.9 us
  between operations: 14.2 us -> 1.2 us
  local copies, waits for them, and re-layouts: 3.61 us -> 13.3 us
    psum x7 -> x0, waiting for transfers between devices: 286 us -> none  [the longest x3 158 us: local(): partial_value = lax.psum(partial_value, 'col')]
    ppermute x0 -> x40, waiting for transfers between devices: none -> 152 us  [swap(): return lax.ppermute(x, axis, [(i, i ^ mask) for i in range(n)])]
    reduce_scatter x1 -> x0, waiting for transfers between devices: 68.3 us -> none  [local(): below_sum = lax.psum_scatter(term, 'col', scatter_dimension=0, tiled=True)]
    dot_general x14 -> x10, matrix products: 68.9 us -> 17.6 us  [the longest x6 10.4 us: local(): product = jnp.dot(couple[pair], solved[source], preferred_element_type=F32)]
    ppermute x0 -> x40, starting transfers between devices: none -> 43.9 us  [swap(): return lax.ppermute(x, axis, [(i, i ^ mask) for i in range(n)])]
    pallas_call x0 -> x5, Pallas kernels: none -> 38.9 us  [the longest x4 21.9 us: last_below(): pl.pallas_call(functools.partial(last_kernel, part), out_shape=jax.ShapeD...]
    concatenate x0 -> x12, other arithmetic: none -> 9.7 us  [the longest x9 6.05 us: sum_rest(): return jnp.concatenate(sum_parts(halves(x), axis, masks), axis=0)]
    add x0 -> x24, other arithmetic: none -> 8.84 us  [the longest x2 4.98 us: local(): kept = keeps[j] + sends[j]]
  transfers between devices with their start and end apart: 8 -> 40, of which waited for: 8 -> 35; matrix products, arithmetic and copies ran while one was open for 9% -> 9% of each run, Pallas kernels for 0% -> 12%
where the time goes in v1:
time: 292 us; the launch traced here: 290 us
  waiting for transfers between devices  152 us (52%)
  starting transfers between devices  43.9 us (15%)
  Pallas kernels  38.9 us (13%)
  other arithmetic  22.9 us (8%)
  matrix products  17.6 us (6%)
  local copies, waits for them, and re-layouts  13.3 us (5%)
    ppermute x40, waiting for transfers between devices, swap(): return lax.ppermute(x, axis, [(i, i ^ mask) for i in range(n)])  152 us
    ppermute x40, starting transfers between devices, swap(): return lax.ppermute(x, axis, [(i, i ^ mask) for i in range(n)])  43.9 us
    pallas_call x4, Pallas kernels, last_below(): pl.pallas_call(functools.partial(last_kernel, part), out_shape=jax.ShapeD...  21.9 us
    pallas_call x1, Pallas kernels, early_below(): pl.pallas_call(early_kernel, out_shape=jax.ShapeDtypeStruct((rows, cols),...  17 us
    dot_general x6, matrix products, local(): product = jnp.dot(couple[pair], solved[source], preferred_element_type=F32)  10.4 us
    dot_general x4, matrix products, local(): total = sum_row(jnp.dot(dinv[target], reduced, preferred_element_type=F32))  7.22 us
    unnamed x39, local copies, waits for them, and re-layouts  7.03 us
    concatenate x9, other arithmetic, sum_rest(): return jnp.concatenate(sum_parts(halves(x), axis, masks), axis=0)  6.05 us
  transfers between devices with their start and end apart: 40, of which 35 were waited for; matrix products, arithmetic and copies ran while one was open for 9% of the time, Pallas kernels for 12%

profile of v1, /device:TPU:0, one launch (start us, length us, event | category | flops | bytes accessed | tf_op | source)
XLA Modules:
  0.0 290.2 jit_solution(8950333938747812282)
XLA Ops:
  0.6 2.0 fusion.15
  2.7 3.1 %collective-permute-start = (f32[256,256]{1,0:T(8,128)S(1)}, f32[256,256]{1,0:T(8,128)S(1)}, u32[]{:S(2)}, u32[]{:S(2)}) collective-permute-start(f32[256,256]{1,0:T(8,128)S(1)} %get-tuple-element.49), channel_id=1, source_target_pairs={{0,8},{8,0},{16,24},{24,16},{1,9},{9,1},{17,25},{25,17},{2,10},{10... | collective-permute-start | bytes 786440 | tf_op jit(solution)/shard_map/ppermute | solution.py:17
  5.8 2.5 collective-permute-start.2
  8.2 4.2 %collective-permute-done = f32[256,256]{1,0:T(8,128)S(1)} collective-permute-done((f32[256,256]{1,0:T(8,128)S(1)}, f32[256,256]{1,0:T(8,128)S(1)}, u32[]{:S(2)}, u32[]{:S(2)}) %collective-permute-start) | collective-permute-done | bytes 262176 | tf_op jit(solution)/shard_map/ppermute | solution.py:17
  12.5 7.5 %collective-permute-done.2 = f32[256,256]{1,0:T(8,128)S(1)} collective-permute-done((f32[256,256]{1,0:T(8,128)S(1)}, f32[256,256]{1,0:T(8,128)S(1)}, u32[]{:S(2)}, u32[]{:S(2)}) %collective-permute-start.2) | collective-permute-done | bytes 262176 | tf_op jit(solution)/shard_map/ppermute | solution.py:17
  21.6 2.1 collective-permute-start.3
  23.8 7.5 %collective-permute-done.1 = f32[256,256]{1,0:T(8,128)S(1)} collective-permute-done((f32[256,256]{1,0:T(8,128)S(1)}, f32[256,256]{1,0:T(8,128)S(1)}, u32[]{:S(2)}, u32[]{:S(2)}) %collective-permute-start.1) | collective-permute-done | bytes 262176 | tf_op jit(solution)/shard_map/ppermute | solution.py:17
  31.3 2.6 collective-permute-done.3
  36.5 1.9 collective-permute-done.4
  41.6 5.3 %collective-permute-done.5 = f32[256,256]{0,1:T(8,128)S(1)} collective-permute-done((f32[256,256]{0,1:T(8,128)S(1)}, f32[256,256]{0,1:T(8,128)S(1)}, u32[]{:S(2)}, u32[]{:S(2)}) %collective-permute-start.5) | collective-permute-done | bytes 262176 | tf_op jit(solution)/shard_map/ppermute | solution.py:17
  50.3 5.1 %collective-permute-done.6 = f32[256,256]{0,1:T(8,128)S(1)} collective-permute-done((f32[256,256]{0,1:T(8,128)S(1)}, f32[256,256]{0,1:T(8,128)S(1)}, u32[]{:S(2)}, u32[]{:S(2)}) %collective-permute-start.6) | collective-permute-done | bytes 262176 | tf_op jit(solution)/shard_map/ppermute | solution.py:17
  57.6 3.4 %fusion.55 = (f32[1,1024,256]{2,1,0:T(8,128)}, f32[1,1024,256]{2,1,0:T(8,128)}, f32[1,1024,256]{2,1,0:T(8,128)S(1)}) fusion(f32[4,1024,256]{2,1,0:T(8,128)} %param.7), kind=kLoop, calls=%fused_computation.120 | loop fusion | bytes 6291456 | tf_op jit(solution)/shard_map/slice | solution.py:157
  65.9 2.5 collective-permute-start.12
  68.5 5.7 %collective-permute-done.10 = f32[256,256]{1,0:T(8,128)S(1)} collective-permute-done((f32[256,256]{1,0:T(8,128)S(1)}, f32[256,256]{1,0:T(8,128)S(1)}, u32[]{:S(2)}, u32[]{:S(2)}) %collective-permute-start.10) | collective-permute-done | bytes 262176 | tf_op jit(solution)/shard_map/ppermute | solution.py:17
  74.3 6.5 %collective-permute-done.12 = f32[256,256]{1,0:T(8,128)S(1)} collective-permute-done((f32[256,256]{1,0:T(8,128)S(1)}, f32[256,256]{1,0:T(8,128)S(1)}, u32[]{:S(2)}, u32[]{:S(2)}) %collective-permute-start.12) | collective-permute-done | bytes 262176 | tf_op jit(solution)/shard_map/ppermute | solution.py:17
  84.8 7.2 %collective-permute-done.11 = f32[256,256]{1,0:T(8,128)S(1)} collective-permute-done((f32[256,256]{1,0:T(8,128)S(1)}, f32[256,256]{1,0:T(8,128)S(1)}, u32[]{:S(2)}, u32[]{:S(2)}) %collective-permute-start.11) | collective-permute-done | bytes 262176 | tf_op jit(solution)/shard_map/ppermute | solution.py:17
  92.7 2.9 collective-permute-done.13
  98.0 1.9 collective-permute-done.14
  101.3 7.2 %collective-permute-done.15 = f32[256,256]{0,1:T(8,128)S(1)} collective-permute-done((f32[256,256]{0,1:T(8,128)S(1)}, f32[256,256]{0,1:T(8,128)S(1)}, u32[]{:S(2)}, u32[]{:S(2)}) %collective-permute-start.15) | collective-permute-done | bytes 262176 | tf_op jit(solution)/shard_map/ppermute | solution.py:17
  110.9 5.3 %collective-permute-done.16 = f32[256,256]{0,1:T(8,128)S(1)} collective-permute-done((f32[256,256]{0,1:T(8,128)S(1)}, f32[256,256]{0,1:T(8,128)S(1)}, u32[]{:S(2)}, u32[]{:S(2)}) %collective-permute-start.16) | collective-permute-done | bytes 262176 | tf_op jit(solution)/shard_map/ppermute | solution.py:17
  120.8 1.7 convolution_bitcast_fusion.1
  123.0 2.4 collective-permute-start.22
  127.1 3.9 %collective-permute-done.20 = f32[256,256]{1,0:T(8,128)S(1)} collective-permute-done((f32[256,256]{1,0:T(8,128)S(1)}, f32[256,256]{1,0:T(8,128)S(1)}, u32[]{:S(2)}, u32[]{:S(2)}) %collective-permute-start.20) | collective-permute-done | bytes 262176 | tf_op jit(solution)/shard_map/ppermute | solution.py:17
  131.0 6.5 %collective-permute-done.22 = f32[256,256]{1,0:T(8,128)S(1)} collective-permute-done((f32[256,256]{1,0:T(8,128)S(1)}, f32[256,256]{1,0:T(8,128)S(1)}, u32[]{:S(2)}, u32[]{:S(2)}) %collective-permute-start.22) | collective-permute-done | bytes 262176 | tf_op jit(solution)/shard_map/ppermute | solution.py:17
  139.0 1.8 collective-permute-start.23
  142.5 6.2 %collective-permute-done.21 = f32[256,256]{1,0:T(8,128)S(1)} collective-permute-done((f32[256,256]{1,0:T(8,128)S(1)}, f32[256,256]{1,0:T(8,128)S(1)}, u32[]{:S(2)}, u32[]{:S(2)}) %collective-permute-start.21) | collective-permute-done | bytes 262176 | tf_op jit(solution)/shard_map/ppermute | solution.py:17
  149.4 2.4 collective-permute-done.23
  152.5 1.8 fusion
  154.4 1.9 collective-permute-done.24
  159.4 5.4 %collective-permute-done.25 = f32[256,256]{0,1:T(8,128)S(1)} collective-permute-done((f32[256,256]{0,1:T(8,128)S(1)}, f32[256,256]{0,1:T(8,128)S(1)}, u32[]{:S(2)}, u32[]{:S(2)}) %collective-permute-start.25) | collective-permute-done | bytes 262176 | tf_op jit(solution)/shard_map/ppermute | solution.py:17
  168.3 5.1 %collective-permute-done.26 = f32[256,256]{0,1:T(8,128)S(1)} collective-permute-done((f32[256,256]{0,1:T(8,128)S(1)}, f32[256,256]{0,1:T(8,128)S(1)}, u32[]{:S(2)}, u32[]{:S(2)}) %collective-permute-start.26) | collective-permute-done | bytes 262176 | tf_op jit(solution)/shard_map/ppermute | solution.py:17
  175.8 1.9 collective-permute-done.29
  179.1 1.8 convolution_bitcast_fusion
  181.4 2.4 collective-permute-start.32
  184.7 4.7 %collective-permute-done.30 = f32[256,256]{1,0:T(8,128)S(1)} collective-permute-done((f32[256,256]{1,0:T(8,128)S(1)}, f32[256,256]{1,0:T(8,128)S(1)}, u32[]{:S(2)}, u32[]{:S(2)}) %collective-permute-start.30) | collective-permute-done | bytes 262176 | tf_op jit(solution)/shard_map/ppermute | solution.py:17
  189.4 6.4 %collective-permute-done.32 = f32[256,256]{1,0:T(8,128)S(1)} collective-permute-done((f32[256,256]{1,0:T(8,128)S(1)}, f32[256,256]{1,0:T(8,128)S(1)}, u32[]{:S(2)}, u32[]{:S(2)}) %collective-permute-start.32) | collective-permute-done | bytes 262176 | tf_op jit(solution)/shard_map/ppermute | solution.py:17
  197.4 1.8 collective-permute-start.33
  199.1 17.0 %early_below.1.a_ref = f32[8192,256]{1,0:T(8,128)} custom-call(s32[4,64]{1,0:T(4,128)} %mask.9, bf16[4,8192,512]{2,1,0:T(8,128)(2,1)} %f_ref.9, bf16[3,512,256]{2,1,0:T(8,128)(2,1)} %maximum_maximum_fusion.x_ref), custom_call_target="tpu_custom_call" | custom-call | flops 6442450944 | bytes 33554432 | tf_op jit(solution)/shard_map/early_below/pallas_call | solution.py:76
  218.3 5.5 %last_below.5 = f32[2048,256]{1,0:T(8,128)} custom-call(s32[4,64]{1,0:T(4,128)} %mask.9, s32[1]{0:T(128)S(6)} %sub.36.sel, bf16[4,8192,512]{2,1,0:T(8,128)(2,1)} %f_ref.9, bf16[512,256]{1,0:T(8,128)(2,1)} %fusion.35.x_ref, f32[8192,256]{1,0:T(8,128)} %early_below.1.a_ref), custom_call_target="tpu_custom_call" | custom-call | flops 536870912 | bytes 6291456 | tf_op jit(solution)/shard_map/last_below/pallas_call | solution.py:115
  223.8 5.5 %last_below.7 = f32[2048,256]{1,0:T(8,128)} custom-call(s32[4,64]{1,0:T(4,128)} %mask.9, s32[1]{0:T(128)S(6)} %sub.36.sel, bf16[4,8192,512]{2,1,0:T(8,128)(2,1)} %f_ref.9, bf16[512,256]{1,0:T(8,128)(2,1)} %fusion.35.x_ref, f32[8192,256]{1,0:T(8,128)} %early_below.1.a_ref), custom_call_target="tpu_custom_call" | custom-call | flops 536870912 | bytes 6291456 | tf_op jit(solution)/shard_map/last_below/pallas_call | solution.py:115
  229.8 5.5 %last_below.4 = f32[2048,256]{1,0:T(8,128)} custom-call(s32[4,64]{1,0:T(4,128)} %mask.9, s32[1]{0:T(128)} %bitcast.45.sel, bf16[4,8192,512]{2,1,0:T(8,128)(2,1)} %f_ref.9, bf16[512,256]{1,0:T(8,128)(2,1)} %fusion.35.x_ref, f32[8192,256]{1,0:T(8,128)} %early_below.1.a_ref), custom_call_target="tpu_custom_call" | custom-call | flops 536870912 | bytes 6291456 | tf_op jit(solution)/shard_map/last_below/pallas_call | solution.py:115
  235.3 2.5 add.190
  239.4 5.5 %last_below.6 = f32[2048,256]{1,0:T(8,128)} custom-call(s32[4,64]{1,0:T(4,128)} %mask.9, s32[1]{0:T(128)} %bitcast.45.sel, bf16[4,8192,512]{2,1,0:T(8,128)(2,1)} %f_ref.9, bf16[512,256]{1,0:T(8,128)(2,1)} %fusion.35.x_ref, f32[8192,256]{1,0:T(8,128)} %early_below.1.a_ref), custom_call_target="tpu_custom_call" | custom-call | flops 536870912 | bytes 6291456 | tf_op jit(solution)/shard_map/last_below/pallas_call | solution.py:115
  244.9 2.5 add.197
  251.3 12.9 %collective-permute-done.35 = f32[2,512,256]{2,1,0:T(8,128)} collective-permute-done((f32[2,512,256]{2,1,0:T(8,128)}, f32[2,512,256]{2,1,0:T(8,128)}, u32[]{:S(2)}, u32[]{:S(2)}) %collective-permute-start.35) | collective-permute-done | bytes 1048608 | tf_op jit(solution)/shard_map/ppermute | solution.py:17
  266.2 9.9 %collective-permute-done.38 = f32[2,512,256]{2,1,0:T(8,128)} collective-permute-done((f32[2,512,256]{2,1,0:T(8,128)}, f32[2,512,256]{2,1,0:T(8,128)}, u32[]{:S(2)}, u32[]{:S(2)}) %collective-permute-start.38) | collective-permute-done | bytes 1048608 | tf_op jit(solution)/shard_map/ppermute | solution.py:17
  280.5 5.4 %collective-permute-done.36 = f32[512,256]{1,0:T(8,128)S(1)} collective-permute-done((f32[512,256]{1,0:T(8,128)S(1)}, f32[512,256]{1,0:T(8,128)S(1)}, u32[]{:S(2)}, u32[]{:S(2)}) %collective-permute-start.36) | collective-permute-done | bytes 524320 | tf_op jit(solution)/shard_map/ppermute | solution.py:17
  286.0 2.9 %collective-permute-done.39 = f32[512,256]{1,0:T(8,128)S(1)} collective-permute-done((f32[512,256]{1,0:T(8,128)S(1)}, f32[512,256]{1,0:T(8,128)S(1)}, u32[]{:S(2)}, u32[]{:S(2)}) %collective-permute-start.39) | collective-permute-done | bytes 524320 | tf_op jit(solution)/shard_map/ppermute | solution.py:17
  (152 shorter events, 69.4 us)
Async XLA Ops:
  0.6 7.6 %copy-start.17 = (s32[6,8]{1,0:T(8,128)S(1)}, s32[6,8]{1,0:T(8,128)}, u32[]{:S(2)}) copy-start(s32[6,8]{1,0:T(8,128)} %param.11) | copy-start | bytes 580
  2.7 9.8 %collective-permute-start = (f32[256,256]{1,0:T(8,128)S(1)}, f32[256,256]{1,0:T(8,128)S(1)}, u32[]{:S(2)}, u32[]{:S(2)}) collective-permute-start(f32[256,256]{1,0:T(8,128)S(1)} %get-tuple-element.49), channel_id=1, source_target_pairs={{0,8},{8,0},{16,24},{24,16},{1,9},{9,1},{17,25},{25,17},{2,10},{10... | collective-permute-start | bytes 786440 | tf_op jit(solution)/shard_map/ppermute | solution.py:17
  5.8 14.2 %collective-permute-start.2 = (f32[256,256]{1,0:T(8,128)S(1)}, f32[256,256]{1,0:T(8,128)S(1)}, u32[]{:S(2)}, u32[]{:S(2)}) collective-permute-start(f32[256,256]{1,0:T(8,128)S(1)} %get-tuple-element.50), channel_id=1, source_target_pairs={{0,24},{8,16},{16,8},{24,0},{1,25},{9,17},{17,9},{25,1},{2,26},{10... | collective-permute-start | bytes 786440 | tf_op jit(solution)/shard_map/ppermute | solution.py:17
  20.1 11.2 %collective-permute-start.1 = (f32[256,256]{1,0:T(8,128)S(1)}, f32[256,256]{1,0:T(8,128)S(1)}, u32[]{:S(2)}, u32[]{:S(2)}) collective-permute-start(f32[256,256]{1,0:T(8,128)S(1)} %get-tuple-element.47), channel_id=1, source_target_pairs={{0,24},{8,16},{16,8},{24,0},{1,25},{9,17},{17,9},{25,1},{2,26},{10... | collective-permute-start | bytes 786440 | tf_op jit(solution)/shard_map/ppermute | solution.py:17
  21.6 12.3 %collective-permute-start.3 = (f32[256,256]{1,0:T(8,128)S(1)}, f32[256,256]{1,0:T(8,128)S(1)}, u32[]{:S(2)}, u32[]{:S(2)}) collective-permute-start(f32[256,256]{1,0:T(8,128)S(1)} %get-tuple-element.48), channel_id=1, source_target_pairs={{0,8},{8,0},{16,24},{24,16},{1,9},{9,1},{17,25},{25,17},{2,10},{10... | collective-permute-start | bytes 786440 | tf_op jit(solution)/shard_map/ppermute | solution.py:17
  36.4 2.0 collective-permute-start.4
  38.5 8.4 %collective-permute-start.5 = (f32[256,256]{0,1:T(8,128)S(1)}, f32[256,256]{0,1:T(8,128)S(1)}, u32[]{:S(2)}, u32[]{:S(2)}) collective-permute-start(f32[256,256]{0,1:T(8,128)S(1)} %get-tuple-element.45), channel_id=1, source_target_pairs={{0,2},{1,3},{2,0},{3,1},{4,6},{5,7},{6,4},{7,5},{8,10},{9,11},{10,... | collective-permute-start | bytes 786440 | tf_op jit(solution)/shard_map/ppermute | solution.py:17
  40.0 8.1 %collective-permute-start.7 = (f32[256,256]{0,1:T(8,128)S(1)}, f32[256,256]{0,1:T(8,128)S(1)}, u32[]{:S(2)}, u32[]{:S(2)}) collective-permute-start(f32[256,256]{0,1:T(8,128)S(1)} %get-tuple-element.46), channel_id=1, source_target_pairs={{0,4},{1,5},{2,6},{3,7},{4,0},{5,1},{6,2},{7,3},{8,12},{9,13},{10,... | collective-permute-start | bytes 786440 | tf_op jit(solution)/shard_map/ppermute | solution.py:17
  48.2 7.3 %collective-permute-start.6 = (f32[256,256]{0,1:T(8,128)S(1)}, f32[256,256]{0,1:T(8,128)S(1)}, u32[]{:S(2)}, u32[]{:S(2)}) collective-permute-start(f32[256,256]{0,1:T(8,128)S(1)} %get-tuple-element.43), channel_id=1, source_target_pairs={{0,4},{1,5},{2,6},{3,7},{4,0},{5,1},{6,2},{7,3},{8,12},{9,13},{10,... | collective-permute-start | bytes 786440 | tf_op jit(solution)/shard_map/ppermute | solution.py:17
  49.8 6.9 %collective-permute-start.8 = (f32[256,256]{0,1:T(8,128)S(1)}, f32[256,256]{0,1:T(8,128)S(1)}, u32[]{:S(2)}, u32[]{:S(2)}) collective-permute-start(f32[256,256]{0,1:T(8,128)S(1)} %get-tuple-element.44), channel_id=1, source_target_pairs={{0,2},{1,3},{2,0},{3,1},{4,6},{5,7},{6,4},{7,5},{8,10},{9,11},{10,... | collective-permute-start | bytes 786440 | tf_op jit(solution)/shard_map/ppermute | solution.py:17
  57.6 4.9 %collective-permute-start.9 = (f32[512,256]{0,1:T(8,128)}, f32[512,256]{0,1:T(8,128)}, u32[]{:S(2)}, u32[]{:S(2)}) collective-permute-start(f32[512,256]{0,1:T(8,128)} %pad_maximum_fusion.2), channel_id=1, source_target_pairs={{0,1},{1,0},{2,3},{3,2},{4,5},{5,4},{6,7},{7,6},{8,9},{9,8},{10,11... | collective-permute-start | bytes 1572872 | tf_op jit(solution)/shard_map/ppermute | solution.py:17
  65.5 8.8 %collective-permute-start.10 = (f32[256,256]{1,0:T(8,128)S(1)}, f32[256,256]{1,0:T(8,128)S(1)}, u32[]{:S(2)}, u32[]{:S(2)}) collective-permute-start(f32[256,256]{1,0:T(8,128)S(1)} %get-tuple-element.41), channel_id=1, source_target_pairs={{0,8},{8,0},{16,24},{24,16},{1,9},{9,1},{17,25},{25,17},{2,10},{10... | collective-permute-start | bytes 786440 | tf_op jit(solution)/shard_map/ppermute | solution.py:17
  65.9 14.9 %collective-permute-start.12 = (f32[256,256]{1,0:T(8,128)S(1)}, f32[256,256]{1,0:T(8,128)S(1)}, u32[]{:S(2)}, u32[]{:S(2)}) collective-permute-start(f32[256,256]{1,0:T(8,128)S(1)} %get-tuple-element.42), channel_id=1, source_target_pairs={{0,24},{8,16},{16,8},{24,0},{1,25},{9,17},{17,9},{25,1},{2,26},{10... | collective-permute-start | bytes 786440 | tf_op jit(solution)/shard_map/ppermute | solution.py:17
  80.9 11.1 %collective-permute-start.11 = (f32[256,256]{1,0:T(8,128)S(1)}, f32[256,256]{1,0:T(8,128)S(1)}, u32[]{:S(2)}, u32[]{:S(2)}) collective-permute-start(f32[256,256]{1,0:T(8,128)S(1)} %get-tuple-element.39), channel_id=1, source_target_pairs={{0,24},{8,16},{16,8},{24,0},{1,25},{9,17},{17,9},{25,1},{2,26},{10... | collective-permute-start | bytes 786440 | tf_op jit(solution)/shard_map/ppermute | solution.py:17
  82.3 13.2 %collective-permute-start.13 = (f32[256,256]{1,0:T(8,128)S(1)}, f32[256,256]{1,0:T(8,128)S(1)}, u32[]{:S(2)}, u32[]{:S(2)}) collective-permute-start(f32[256,256]{1,0:T(8,128)S(1)} %get-tuple-element.40), channel_id=1, source_target_pairs={{0,8},{8,0},{16,24},{24,16},{1,9},{9,1},{17,25},{25,17},{2,10},{10... | collective-permute-start | bytes 786440 | tf_op jit(solution)/shard_map/ppermute | solution.py:17
  98.0 2.0 collective-permute-start.14
  100.1 8.4 %collective-permute-start.15 = (f32[256,256]{0,1:T(8,128)S(1)}, f32[256,256]{0,1:T(8,128)S(1)}, u32[]{:S(2)}, u32[]{:S(2)}) collective-permute-start(f32[256,256]{0,1:T(8,128)S(1)} %get-tuple-element.37), channel_id=1, source_target_pairs={{0,2},{1,3},{2,0},{3,1},{4,6},{5,7},{6,4},{7,5},{8,10},{9,11},{10,... | collective-permute-start | bytes 786440 | tf_op jit(solution)/shard_map/ppermute | solution.py:17
  100.7 8.1 %collective-permute-start.17 = (f32[256,256]{0,1:T(8,128)S(1)}, f32[256,256]{0,1:T(8,128)S(1)}, u32[]{:S(2)}, u32[]{:S(2)}) collective-permute-start(f32[256,256]{0,1:T(8,128)S(1)} %get-tuple-element.38), channel_id=1, source_target_pairs={{0,4},{1,5},{2,6},{3,7},{4,0},{5,1},{6,2},{7,3},{8,12},{9,13},{10,... | collective-permute-start | bytes 786440 | tf_op jit(solution)/shard_map/ppermute | solution.py:17
  108.9 7.3 %collective-permute-start.16 = (f32[256,256]{0,1:T(8,128)S(1)}, f32[256,256]{0,1:T(8,128)S(1)}, u32[]{:S(2)}, u32[]{:S(2)}) collective-permute-start(f32[256,256]{0,1:T(8,128)S(1)} %get-tuple-element.35), channel_id=1, source_target_pairs={{0,4},{1,5},{2,6},{3,7},{4,0},{5,1},{6,2},{7,3},{8,12},{9,13},{10,... | collective-permute-start | bytes 786440 | tf_op jit(solution)/shard_map/ppermute | solution.py:17
  109.5 6.9 %collective-permute-start.18 = (f32[256,256]{0,1:T(8,128)S(1)}, f32[256,256]{0,1:T(8,128)S(1)}, u32[]{:S(2)}, u32[]{:S(2)}) collective-permute-start(f32[256,256]{0,1:T(8,128)S(1)} %get-tuple-element.36), channel_id=1, source_target_pairs={{0,2},{1,3},{2,0},{3,1},{4,6},{5,7},{6,4},{7,5},{8,10},{9,11},{10,... | collective-permute-start | bytes 786440 | tf_op jit(solution)/shard_map/ppermute | solution.py:17
  117.3 2.3 collective-permute-start.19
  122.5 8.4 %collective-permute-start.20 = (f32[256,256]{1,0:T(8,128)S(1)}, f32[256,256]{1,0:T(8,128)S(1)}, u32[]{:S(2)}, u32[]{:S(2)}) collective-permute-start(f32[256,256]{1,0:T(8,128)S(1)} %get-tuple-element.33), channel_id=1, source_target_pairs={{0,8},{8,0},{16,24},{24,16},{1,9},{9,1},{17,25},{25,17},{2,10},{10... | collective-permute-start | bytes 786440 | tf_op jit(solution)/shard_map/ppermute | solution.py:17
  123.0 14.5 %collective-permute-start.22 = (f32[256,256]{1,0:T(8,128)S(1)}, f32[256,256]{1,0:T(8,128)S(1)}, u32[]{:S(2)}, u32[]{:S(2)}) collective-permute-start(f32[256,256]{1,0:T(8,128)S(1)} %get-tuple-element.34), channel_id=1, source_target_pairs={{0,24},{8,16},{16,8},{24,0},{1,25},{9,17},{17,9},{25,1},{2,26},{10... | collective-permute-start | bytes 786440 | tf_op jit(solution)/shard_map/ppermute | solution.py:17
  137.5 11.2 %collective-permute-start.21 = (f32[256,256]{1,0:T(8,128)S(1)}, f32[256,256]{1,0:T(8,128)S(1)}, u32[]{:S(2)}, u32[]{:S(2)}) collective-permute-start(f32[256,256]{1,0:T(8,128)S(1)} %get-tuple-element.31), channel_id=1, source_target_pairs={{0,24},{8,16},{16,8},{24,0},{1,25},{9,17},{17,9},{25,1},{2,26},{10... | collective-permute-start | bytes 786440 | tf_op jit(solution)/shard_map/ppermute | solution.py:17
  139.0 12.8 %collective-permute-start.23 = (f32[256,256]{1,0:T(8,128)S(1)}, f32[256,256]{1,0:T(8,128)S(1)}, u32[]{:S(2)}, u32[]{:S(2)}) collective-permute-start(f32[256,256]{1,0:T(8,128)S(1)} %get-tuple-element.32), channel_id=1, source_target_pairs={{0,8},{8,0},{16,24},{24,16},{1,9},{9,1},{17,25},{25,17},{2,10},{10... | collective-permute-start | bytes 786440 | tf_op jit(solution)/shard_map/ppermute | solution.py:17
  154.3 2.0 collective-permute-start.24
  156.4 8.4 %collective-permute-start.25 = (f32[256,256]{0,1:T(8,128)S(1)}, f32[256,256]{0,1:T(8,128)S(1)}, u32[]{:S(2)}, u32[]{:S(2)}) collective-permute-start(f32[256,256]{0,1:T(8,128)S(1)} %get-tuple-element.29), channel_id=1, source_target_pairs={{0,2},{1,3},{2,0},{3,1},{4,6},{5,7},{6,4},{7,5},{8,10},{9,11},{10,... | collective-permute-start | bytes 786440 | tf_op jit(solution)/shard_map/ppermute | solution.py:17
  157.9 8.1 %collective-permute-start.27 = (f32[256,256]{0,1:T(8,128)S(1)}, f32[256,256]{0,1:T(8,128)S(1)}, u32[]{:S(2)}, u32[]{:S(2)}) collective-permute-start(f32[256,256]{0,1:T(8,128)S(1)} %get-tuple-element.30), channel_id=1, source_target_pairs={{0,4},{1,5},{2,6},{3,7},{4,0},{5,1},{6,2},{7,3},{8,12},{9,13},{10,... | collective-permute-start | bytes 786440 | tf_op jit(solution)/shard_map/ppermute | solution.py:17
  166.1 7.3 %collective-permute-start.26 = (f32[256,256]{0,1:T(8,128)S(1)}, f32[256,256]{0,1:T(8,128)S(1)}, u32[]{:S(2)}, u32[]{:S(2)}) collective-permute-start(f32[256,256]{0,1:T(8,128)S(1)} %get-tuple-element.27), channel_id=1, source_target_pairs={{0,4},{1,5},{2,6},{3,7},{4,0},{5,1},{6,2},{7,3},{8,12},{9,13},{10,... | collective-permute-start | bytes 786440 | tf_op jit(solution)/shard_map/ppermute | solution.py:17
  167.6 6.9 %collective-permute-start.28 = (f32[256,256]{0,1:T(8,128)S(1)}, f32[256,256]{0,1:T(8,128)S(1)}, u32[]{:S(2)}, u32[]{:S(2)}) collective-permute-start(f32[256,256]{0,1:T(8,128)S(1)} %get-tuple-element.28), channel_id=1, source_target_pairs={{0,2},{1,3},{2,0},{3,1},{4,6},{5,7},{6,4},{7,5},{8,10},{9,11},{10,... | collective-permute-start | bytes 786440 | tf_op jit(solution)/shard_map/ppermute | solution.py:17
  175.5 2.3 collective-permute-start.29
  179.0 4.7 %copy-start.12 = (bf16[1,256,256]{2,1,0:T(8,128)(2,1)S(1)}, bf16[1,256,256]{2,1,0:T(8,128)(2,1)}, u32[]{:S(2)}) copy-start(bf16[1,256,256]{2,1,0:T(8,128)(2,1)} %get-tuple-element.4) | copy-start | bytes 393220
  179.0 4.7 %copy-start.13 = (bf16[1,256,256]{2,1,0:T(8,128)(2,1)S(1)}, bf16[1,256,256]{2,1,0:T(8,128)(2,1)}, u32[]{:S(2)}) copy-start(bf16[1,256,256]{2,1,0:T(8,128)(2,1)} %get-tuple-element.6) | copy-start | bytes 393220
  179.0 4.7 %copy-start.14 = (bf16[1,256,256]{2,1,0:T(8,128)(2,1)S(1)}, bf16[1,256,256]{2,1,0:T(8,128)(2,1)}, u32[]{:S(2)}) copy-start(bf16[1,256,256]{2,1,0:T(8,128)(2,1)} %get-tuple-element.8) | copy-start | bytes 393220
  180.9 8.5 %collective-permute-start.30 = (f32[256,256]{1,0:T(8,128)S(1)}, f32[256,256]{1,0:T(8,128)S(1)}, u32[]{:S(2)}, u32[]{:S(2)}) collective-permute-start(f32[256,256]{1,0:T(8,128)S(1)} %get-tuple-element.25), channel_id=1, source_target_pairs={{0,8},{8,0},{16,24},{24,16},{1,9},{9,1},{17,25},{25,17},{2,10},{10... | collective-permute-start | bytes 786440 | tf_op jit(solution)/shard_map/ppermute | solution.py:17
  181.4 14.4 %collective-permute-start.32 = (f32[256,256]{1,0:T(8,128)S(1)}, f32[256,256]{1,0:T(8,128)S(1)}, u32[]{:S(2)}, u32[]{:S(2)}) collective-permute-start(f32[256,256]{1,0:T(8,128)S(1)} %get-tuple-element.26), channel_id=1, source_target_pairs={{0,24},{8,16},{16,8},{24,0},{1,25},{9,17},{17,9},{25,1},{2,26},{10... | collective-permute-start | bytes 786440 | tf_op jit(solution)/shard_map/ppermute | solution.py:17
  195.9 20.3 %collective-permute-start.31 = (f32[256,256]{1,0:T(8,128)S(1)}, f32[256,256]{1,0:T(8,128)S(1)}, u32[]{:S(2)}, u32[]{:S(2)}) collective-permute-start(f32[256,256]{1,0:T(8,128)S(1)} %get-tuple-element.23), channel_id=1, source_target_pairs={{0,24},{8,16},{16,8},{24,0},{1,25},{9,17},{17,9},{25,1},{2,26},{10... | collective-permute-start | bytes 786440 | tf_op jit(solution)/shard_map/ppermute | solution.py:17
  197.4 18.9 %collective-permute-start.33 = (f32[256,256]{1,0:T(8,128)S(1)}, f32[256,256]{1,0:T(8,128)S(1)}, u32[]{:S(2)}, u32[]{:S(2)}) collective-permute-start(f32[256,256]{1,0:T(8,128)S(1)} %get-tuple-element.24), channel_id=1, source_target_pairs={{0,8},{8,0},{16,24},{24,16},{1,9},{9,1},{17,25},{25,17},{2,10},{10... | collective-permute-start | bytes 786440 | tf_op jit(solution)/shard_map/ppermute | solution.py:17
  223.8 11.4 %collective-permute-start.34 = (f32[2048,256]{1,0:T(8,128)}, f32[2048,256]{1,0:T(8,128)}, u32[]{:S(2)}, u32[]{:S(2)}) collective-permute-start(f32[2048,256]{1,0:T(8,128)} %last_below.5), channel_id=1, source_target_pairs={{0,1},{1,0},{2,3},{3,2},{4,5},{5,4},{6,7},{7,6},{8,9},{9,8},{10,11... | collective-permute-start | bytes 6291464 | tf_op jit(solution)/shard_map/ppermute | solution.py:17
  229.3 15.6 %collective-permute-start.37 = (f32[2048,256]{1,0:T(8,128)}, f32[2048,256]{1,0:T(8,128)}, u32[]{:S(2)}, u32[]{:S(2)}) collective-permute-start(f32[2048,256]{1,0:T(8,128)} %last_below.7), channel_id=1, source_target_pairs={{0,1},{1,0},{2,3},{3,2},{4,5},{5,4},{6,7},{7,6},{8,9},{9,8},{10,11... | collective-permute-start | bytes 6291464 | tf_op jit(solution)/shard_map/ppermute | solution.py:17
  238.8 25.4 %collective-permute-start.35 = (f32[2,512,256]{2,1,0:T(8,128)}, f32[2,512,256]{2,1,0:T(8,128)}, u32[]{:S(2)}, u32[]{:S(2)}) collective-permute-start(f32[2,512,256]{2,1,0:T(8,128)} %dynamic-slice_bitcast_fusion.1), channel_id=1, source_target_pairs={{0,2},{1,3},{2,0},{3,1},{4,6},{5,7},{6,4},{7,5},{8,10},{9,11},{10,... | collective-permute-start | bytes 3145736 | tf_op jit(solution)/shard_map/ppermute | solution.py:17
  249.7 26.4 %collective-permute-start.38 = (f32[2,512,256]{2,1,0:T(8,128)}, f32[2,512,256]{2,1,0:T(8,128)}, u32[]{:S(2)}, u32[]{:S(2)}) collective-permute-start(f32[2,512,256]{2,1,0:T(8,128)} %dynamic-slice_bitcast_fusion), channel_id=1, source_target_pairs={{0,4},{1,5},{2,6},{3,7},{4,0},{5,1},{6,2},{7,3},{8,12},{9,13},{10,... | collective-permute-start | bytes 3145736 | tf_op jit(solution)/shard_map/ppermute | solution.py:17
  251.3 24.9 %copy-start.1 = (f32[2048,256]{1,0:T(8,128)S(1)}, f32[2048,256]{1,0:T(8,128)}, u32[]{:S(2)}) copy-start(f32[2048,256]{1,0:T(8,128)} %copy-done) | copy-start | bytes 6291460
  265.6 13.4 %copy-start.5 = (f32[256,256]{1,0:T(8,128)S(1)}, f32[256,256]{1,0:T(8,128)}, u32[]{:S(2)}) copy-start(f32[256,256]{1,0:T(8,128)} %copy-done.4) | copy-start | bytes 786436
  265.6 13.4 %copy-start.7 = (f32[256,256]{1,0:T(8,128)S(1)}, f32[256,256]{1,0:T(8,128)}, u32[]{:S(2)}) copy-start(f32[256,256]{1,0:T(8,128)} %copy-done.6) | copy-start | bytes 786436
  265.6 20.3 %collective-permute-start.36 = (f32[512,256]{1,0:T(8,128)S(1)}, f32[512,256]{1,0:T(8,128)S(1)}, u32[]{:S(2)}, u32[]{:S(2)}) collective-permute-start(f32[512,256]{1,0:T(8,128)S(1)} %dynamic-slice_bitcast_fusion.3), channel_id=1, source_target_pairs={{0,4},{1,5},{2,6},{3,7},{4,0},{5,1},{6,2},{7,3},{8,12},{9,13},{10,... | collective-permute-start | bytes 1572872 | tf_op jit(solution)/shard_map/ppermute | solution.py:17
  277.5 11.4 %collective-permute-start.39 = (f32[512,256]{1,0:T(8,128)S(1)}, f32[512,256]{1,0:T(8,128)S(1)}, u32[]{:S(2)}, u32[]{:S(2)}) collective-permute-start(f32[512,256]{1,0:T(8,128)S(1)} %dynamic-slice_bitcast_fusion.2), channel_id=1, source_target_pairs={{0,2},{1,3},{2,0},{3,1},{4,6},{5,7},{6,4},{7,5},{8,10},{9,11},{10,... | collective-permute-start | bytes 1572872 | tf_op jit(solution)/shard_map/ppermute | solution.py:17
  280.5 8.5 %copy-start.11 = (f32[1024,256]{1,0:T(8,128)S(1)}, f32[1024,256]{1,0:T(8,128)}, u32[]{:S(2)}) copy-start(f32[1024,256]{1,0:T(8,128)} %param.8) | copy-start | bytes 3145732
  (10 other events, 18.8 us)

commit v2 on v0

v2 whole, which is shorter than its diff:
```python
import functools

import jax
import jax.numpy as jnp
from jax import lax
from jax.experimental import pallas as pl
from jax.experimental.pallas import tpu as pltpu
from jax.sharding import PartitionSpec as P

BLK = 128
PANELS = 4
F32 = jnp.float32
BF16 = jnp.bfloat16
VMEM = pl.BlockSpec(memory_space=pltpu.VMEM)
SMEM = pl.BlockSpec(memory_space=pltpu.SMEM)
HBM = pl.BlockSpec(memory_space=pltpu.HBM)


def swap(x, axis, mask):
    n = lax.axis_size(axis)
    return lax.ppermute(x, axis, [(i, i ^ mask) for i in range(n)])


def after(x, *others):
    return lax.optimization_barrier((x, *others))[0]


def half(x, bit, dim):
    size = x.shape[dim] // 2
    return lax.dynamic_slice_in_dim(x, bit * size, size, dim)


def halves(x):
    rows = x.shape[0] // 2
    return [x[:rows], x[rows:]]


def sum_parts(parts, axis, masks, queue):
    for step in range(len(masks)):
        got = [swap(p, axis, masks[(step + j) % len(masks)]) for j, p in enumerate(parts)]
        new = [p + g for p, g in zip(parts, got)]
        if queue:
            new = lax.optimization_barrier((*new, queue.pop(0)(parts[-1])))[: len(new)]
        parts = list(new)
    return parts


def sum_row(parts, queue):
    if lax.axis_size("row") == 4:
        return sum_parts(parts, "row", (1, 3), queue)
    bit = lax.axis_index("row") & 1
    x = jnp.concatenate(parts, axis=0)
    mine = half(x, bit, 0) + swap(half(x, 1 - bit, 0), "row", 1)
    mine = jnp.concatenate(sum_parts(halves(mine), "row", (2, 6), queue), axis=0)
    back = swap(mine, "row", 1)
    return [jnp.where(bit == 0, mine, back), jnp.where(bit == 0, back, mine)]


def col_masks():
    n = lax.axis_size("col")
    return tuple(2 << b for b in range(n.bit_length() - 2))


def stage_kernel(sel, c_ref, d_ref, *refs):
    outs, sem = refs[:4], refs[4]
    copies = []
    for side in range(2):
        half_of = sel[0] if side else 1 - sel[0]
        rows, depth = outs[side].shape[1], outs[2 + side].shape[2]
        sources = (c_ref.at[:, pl.ds(half_of * rows, rows), :], d_ref.at[:, :, pl.ds(half_of * depth, depth)])
        for k, source in enumerate(sources):
            copies.append(pltpu.make_async_copy(source, outs[2 * k + side], sem.at[2 * k + side]))
    for copy in copies:
        copy.start()
    for copy in copies:
        copy.wait()


def stage(bit, couple, dinv):
    pairs, rows, depth = couple.shape
    panels, height, width = dinv.shape
    shapes = [(pairs, rows // 2, depth)] * 2 + [(panels, height, width // 2)] * 2
    out = pl.pallas_call(
        stage_kernel,
        out_shape=[jax.ShapeDtypeStruct(shape, BF16) for shape in shapes],
        in_specs=[SMEM, HBM, HBM],
        out_specs=[VMEM] * 4,
        scratch_shapes=[pltpu.SemaphoreType.DMA((4,))],
        compiler_params=pltpu.CompilerParams(vmem_limit_bytes=44 << 20),
        name="stage",
    )(bit, couple, dinv)
    return out[:2], out[2:]


def last_kernel(base, *refs):
    f_ref, outs, sem = refs[0], refs[1:-1], refs[-1]
    own = outs[0].shape[0]
    copies = []
    for q, out in enumerate(outs):
        source = f_ref.at[PANELS - 1, pl.ds(base[q] * own, own), :]
        copies.append(pltpu.make_async_copy(source, out, sem.at[q]))
    for copy in copies:
        copy.start()
    for copy in copies:
        copy.wait()


def last_rows(blocks, factor, own):
    _, rows, depth = factor.shape
    n = rows // own
    return pl.pallas_call(
        last_kernel,
        out_shape=[jax.ShapeDtypeStruct((own, depth), BF16)] * n,
        in_specs=[SMEM, HBM],
        out_specs=[VMEM] * n,
        scratch_shapes=[pltpu.SemaphoreType.DMA((n,))],
        compiler_params=pltpu.CompilerParams(vmem_limit_bytes=33 << 20),
        name="last_rows",
    )(blocks, factor)


def scatter(sums, part, bits):
    order = list(range(1, bits))
    order = order[-part:] + order[:-part] if part else order
    for bit in order:
        mask = 1 << bit
        got = {q: swap(x, "col", mask) for q, x in sorted(sums.items(), reverse=True) if q & mask}
        sums = {q: x + got[q | mask] for q, x in sums.items() if not q & mask}
    return sums[0]


def local(rhs_window, rhs_below, dinv, couple, window_mask, below_factor, below_mask):
    n = lax.axis_size("col")
    bits = n.bit_length() - 1
    me = lax.axis_index("col")
    bit = me & 1
    sel = bit.astype(jnp.int32)[None]
    sides = (1 - bit, bit)
    blocks = me ^ jnp.arange(n, dtype=jnp.int32)
    gain = jnp.repeat(window_mask.astype(F32), BLK, axis=1)
    gains = [half(gain, s, 1) for s in sides]
    rhs = [[halves(half(r, s, 0)) for s in sides] for r in rhs_window]
    own = rhs_below.shape[0]
    rows = below_factor.shape[1] // 2
    below_gain = jnp.repeat(below_mask.astype(F32), BLK, axis=1)
    early = [None, None]
    store = {}

    def early_step(panel, top, solved, dep):
        factor = below_factor[panel, top * rows : (top + 1) * rows]
        term = jnp.dot(factor, after(solved, dep), preferred_element_type=F32)
        term = below_gain[panel, top * rows : (top + 1) * rows, None] * term
        early[top] = early[top] + term if panel else term
        return early[top]

    def stage_step(dep):
        store["couple"], store["dinv"] = stage(after(sel, dep), couple, dinv)
        return store["couple"][0]

    def last_step(dep):
        store["last"] = last_rows(after(blocks, dep), below_factor, own)
        return store["last"][0]

    def tail(q, solved):
        term = jnp.dot(store["last"][q], solved, preferred_element_type=F32)
        scale = lax.dynamic_slice_in_dim(below_gain[-1], (me ^ q) * own, own, 0)
        at = ((me ^ q) % (n // 2)) * own
        parts = [lax.dynamic_slice_in_dim(e, at, own, 0) for e in early]
        base = jnp.where((me ^ q) < n // 2, parts[0], parts[1])
        return base + scale[:, None] * term

    def update(target, side, solved):
        total = None
        for source in range(target):
            pair = target * (target - 1) // 2 + source
            product = jnp.dot(store["couple"][side][pair], solved[source], preferred_element_type=F32)
            product = gains[side][pair][:, None] * product
            total = product if total is None else total + product
        return total

    solutions, solved = [], []
    queue = [stage_step, last_step]
    for target in range(PANELS):
        right = rhs[target]
        if target > 0:
            away = swap(update(target, 0, solved), "col", 1)
            home = sum_parts(halves(update(target, 1, solved) + away), "col", col_masks(), [])
            back = [swap(h, "col", 1) for h in home]
            right = [[r - b for r, b in zip(rhs[target][0], back)], [r - h for r, h in zip(rhs[target][1], home)]]
        parts = []
        for piece in range(2):
            total = None
            for side in (1, 0):
                if target == 0:
                    inverse = half(dinv[0], sides[side], 1)
                else:
                    inverse = store["dinv"][side][target]
                height, width = inverse.shape[0] // 2, inverse.shape[1] // 2
                for k in range(2):
                    block = inverse[piece * height : (piece + 1) * height, k * width : (k + 1) * width]
                    product = jnp.dot(block, right[side][k].astype(BF16), preferred_element_type=F32)
                    total = product if total is None else total + product
            parts.append(total)
        parts = sum_row(parts, queue)
        while queue:
            queue.pop(0)(parts[0])
        solutions.append(jnp.concatenate(parts, axis=0))
        solved.append(jnp.concatenate([p.astype(BF16) for p in parts], axis=0))
        if target < PANELS - 1:
            queue = [functools.partial(early_step, target, top, solved[-1]) for top in range(2)]
    sent = {q: swap(tail(q, solved[-1]), "col", 1) for q in range(n - 1, 0, -2)}
    sums = {q: halves(tail(q, solved[-1]) + sent[q + 1]) for q in range(n - 2, -1, -2)}
    done = [scatter({q: x[j] for q, x in sums.items()}, j, bits) for j in range(2)]
    return (jnp.stack(solutions), rhs_below - jnp.concatenate(done, axis=0))


def solution(mesh):
    return jax.shard_map(
        local,
        mesh=mesh,
        in_specs=(
            P(None, "row", None),
            P(("row", "col"), None),
            P(None, "col", "row"),
            P(None, "row", "col"),
            P(None, "row"),
            P(None, "row", "col"),
            P(None, "row"),
        ),
        out_specs=(P(None, "col", None), P(("row", "col"), None)),
        check_vma=False,
    )
```

time: 448 us -> 250 us (0.56)
  waiting for transfers between devices: 355 us -> 121 us
  starting transfers between devices: 0.51 us -> 45.5 us
  matrix products: 68.9 us -> 40 us
  local copies, waits for them, and re-layouts: 3.61 us -> 16.7 us
  between operations: 14.2 us -> 2 us
  Pallas kernels: 0 us -> 10.1 us
  other arithmetic: 5.28 us -> 13.7 us
    psum x7 -> x0, waiting for transfers between devices: 286 us -> none  [the longest x3 158 us: local(): partial_value = lax.psum(partial_value, 'col')]
    ppermute x0 -> x47, waiting for transfers between devices: none -> 121 us  [swap(): return lax.ppermute(x, axis, [(i, i ^ mask) for i in range(n)])]
    reduce_scatter x1 -> x0, waiting for transfers between devices: 68.3 us -> none  [local(): below_sum = lax.psum_scatter(term, 'col', scatter_dimension=0, tiled=True)]
    ppermute x0 -> x47, starting transfers between devices: none -> 45.5 us  [swap(): return lax.ppermute(x, axis, [(i, i ^ mask) for i in range(n)])]
    dot_general x14 -> x58, matrix products: 68.9 us -> 40 us  [the longest x6 25.5 us: early_step(): term = jnp.dot(factor, after(solved, dep), preferred_element_type=F32)]
    pallas_call x0 -> x2, Pallas kernels: none -> 10.1 us  [the longest x1 5.77 us: stage(): pl.pallas_call(stage_kernel, out_shape=[jax.ShapeDtypeStruct(shape, BF16)...]
    add x0 -> x21, other arithmetic: none -> 7.7 us  [the longest x19 7.22 us: sum_parts(): new = [p + g for p, g in zip(parts, got)]]
  transfers between devices with their start and end apart: 8 -> 47, of which waited for: 8 -> 38; matrix products, arithmetic and copies ran while one was open for 9% -> 20% of each run, Pallas kernels for 0% -> 4%
where the time goes in v2:
time: 250 us; the launch traced here: 249 us
  waiting for transfers between devices  121 us (48%)
  starting transfers between devices  45.5 us (18%)
  matrix products  40 us (16%)
  local copies, waits for them, and re-layouts  16.7 us (7%)
  other arithmetic  13.7 us (5%)
  Pallas kernels  10.1 us (4%)
    ppermute x47, waiting for transfers between devices, swap(): return lax.ppermute(x, axis, [(i, i ^ mask) for i in range(n)])  121 us
    ppermute x47, starting transfers between devices, swap(): return lax.ppermute(x, axis, [(i, i ^ mask) for i in range(n)])  45.5 us
    dot_general x6, matrix products, early_step(): term = jnp.dot(factor, after(solved, dep), preferred_element_type=F32)  25.5 us
    add x19, other arithmetic, sum_parts(): new = [p + g for p, g in zip(parts, got)]  7.22 us
    dot_general x32, matrix products, local(): jnp.dot(block, right[side][k].astype(BF16), preferred_element_type=F32)  6.83 us
    unnamed x100, local copies, waits for them, and re-layouts  6.81 us
    pallas_call x1, Pallas kernels, stage(): pl.pallas_call(stage_kernel, out_shape=[jax.ShapeDtypeStruct(shape, BF16)...  5.77 us
  transfers between devices with their start and end apart: 47, of which 38 were waited for; matrix products, arithmetic and copies ran while one was open for 20% of the time, Pallas kernels for 4%

profile of v2, /device:TPU:0, one launch (start us, length us, event | category | flops | bytes accessed | tf_op | source)
XLA Modules:
  0.0 249.1 jit_solution(17749217832759954451)
XLA Ops:
  4.2 3.1 %collective-permute-start = (f32[256,256]{1,0:T(8,128)S(1)}, f32[256,256]{1,0:T(8,128)S(1)}, u32[]{:S(2)}, u32[]{:S(2)}) collective-permute-start(f32[256,256]{1,0:T(8,128)S(1)} %convolution_add_fusion.9), channel_id=1, source_target_pairs={{0,8},{8,0},{16,24},{24,16},{1,9},{9,1},{17,25},{25,17},{2,10},{10... | collective-permute-start | bytes 786440 | tf_op jit(solution)/shard_map/ppermute | solution.py:21
  8.0 2.5 %collective-permute-start.1 = (f32[256,256]{1,0:T(8,128)S(1)}, f32[256,256]{1,0:T(8,128)S(1)}, u32[]{:S(2)}, u32[]{:S(2)}) collective-permute-start(f32[256,256]{1,0:T(8,128)S(1)} %convolution_add_fusion.6), channel_id=1, source_target_pairs={{0,24},{8,16},{16,8},{24,0},{1,25},{9,17},{17,9},{25,1},{2,26},{10... | collective-permute-start | bytes 786440 | tf_op jit(solution)/shard_map/ppermute | solution.py:21
  12.0 5.8 %stage.1 = (bf16[6,512,512]{2,1,0:T(8,128)(2,1)S(1)}, bf16[6,512,512]{2,1,0:T(8,128)(2,1)}, bf16[4,512,512]{2,1,0:T(8,128)(2,1)S(1)}, bf16[4,512,512]{2,1,0:T(8,128)(2,1)S(1)}) custom-call(s32[1]{0:T(128)} %bitcast.6.sel, bf16[6,1024,512]{2,1,0:T(8,128)(2,1)} %c_ref.1, bf16[4,512,1024]{2,1,0:T(8,128)(2,1)} %d_ref.1), custom_call_target="tpu_custom_call" | custom-call | tf_op jit(solution)/shard_map/stage/pallas_call | solution.py:83
  19.1 1.6 copy-done.16
  23.6 2.6 %collective-permute-start.2 = (f32[256,256]{1,0:T(8,128)}, f32[256,256]{1,0:T(8,128)}, u32[]{:S(2)}, u32[]{:S(2)}) collective-permute-start(f32[256,256]{1,0:T(8,128)} %add.353), channel_id=1, source_target_pairs={{0,24},{8,16},{16,8},{24,0},{1,25},{9,17},{17,9},{25,1},{2,26},{10... | collective-permute-start | bytes 786440 | tf_op jit(solution)/shard_map/ppermute | solution.py:21
  26.5 4.3 %last_rows.1 = (bf16[1024,512]{1,0:T(8,128)(2,1)S(1)}, bf16[1024,512]{1,0:T(8,128)(2,1)S(1)}, bf16[1024,512]{1,0:T(8,128)(2,1)S(1)}, bf16[1024,512]{1,0:T(8,128)...) custom-call(s32[8]{0:T(128)S(1)} %iota_xor_fusion.base, ...), custom_call_target="tpu_custom_call" | custom-call | tf_op jit(solution)/shard_map/last_rows/pallas_call | solution.py:111
  31.1 2.3 add.359
  33.4 3.7 %collective-permute-done.2 = f32[256,256]{1,0:T(8,128)} collective-permute-done((f32[256,256]{1,0:T(8,128)}, f32[256,256]{1,0:T(8,128)}, u32[]{:S(2)}, u32[]{:S(2)}) %collective-permute-start.2) | collective-permute-done | bytes 262176 | tf_op jit(solution)/shard_map/ppermute | solution.py:21
  41.1 1.6 collective-permute-start.5
  42.7 1.5 collective-permute-start.7
  45.1 4.8 %collective-permute-done.5 = f32[256,256]{1,0:T(8,128)S(1)} collective-permute-done((f32[256,256]{1,0:T(8,128)S(1)}, f32[256,256]{1,0:T(8,128)S(1)}, u32[]{:S(2)}, u32[]{:S(2)}) %collective-permute-start.5) | collective-permute-done | bytes 262176 | tf_op jit(solution)/shard_map/ppermute | solution.py:21
  51.1 1.6 collective-permute-start.6
  53.6 5.2 %collective-permute-done.6 = f32[256,256]{1,0:T(8,128)S(1)} collective-permute-done((f32[256,256]{1,0:T(8,128)S(1)}, f32[256,256]{1,0:T(8,128)S(1)}, u32[]{:S(2)}, u32[]{:S(2)}) %collective-permute-start.6) | collective-permute-done | bytes 262176 | tf_op jit(solution)/shard_map/ppermute | solution.py:21
  64.8 3.5 %fusion.9 = f32[4096,256]{0,1:T(8,128)S(1)} fusion(bf16[512,256]{1,0:T(8,128)(2,1)S(1)} %pad_maximum_fusion.1, bf16[4,8192,512]{2,1,0:T(8,128)(2,1)} %refs_0_.1, f32[4096]{0:T(1024)S(1)} %bitcast.263), kind=kOutput, calls=%fused_computation.15 | convolution fusion | flops 1074790400 | bytes 8667136 | tf_op jit(solution)/shard_map/dot_general | solution.py:151
  68.3 6.0 %collective-permute-done.12 = f32[256,256]{1,0:T(8,128)S(1)} collective-permute-done((f32[256,256]{1,0:T(8,128)S(1)}, f32[256,256]{1,0:T(8,128)S(1)}, u32[]{:S(2)}, u32[]{:S(2)}) %collective-permute-start.12) | collective-permute-done | bytes 262176 | tf_op jit(solution)/shard_map/ppermute | solution.py:21
  74.3 4.2 %collective-permute-done.11 = f32[256,256]{1,0:T(8,128)S(1)} collective-permute-done((f32[256,256]{1,0:T(8,128)S(1)}, f32[256,256]{1,0:T(8,128)S(1)}, u32[]{:S(2)}, u32[]{:S(2)}) %collective-permute-start.11) | collective-permute-done | bytes 262176 | tf_op jit(solution)/shard_map/ppermute | solution.py:21
  78.6 2.5 %collective-permute-start.13 = (f32[256,256]{1,0:T(8,128)S(1)}, f32[256,256]{1,0:T(8,128)S(1)}, u32[]{:S(2)}, u32[]{:S(2)}) collective-permute-start(f32[256,256]{1,0:T(8,128)S(1)} %add.368), channel_id=1, source_target_pairs={{0,24},{8,16},{16,8},{24,0},{1,25},{9,17},{17,9},{25,1},{2,26},{10... | collective-permute-start | bytes 786440 | tf_op jit(solution)/shard_map/ppermute | solution.py:21
  81.2 3.5 %fusion.8 = f32[4096,256]{0,1:T(8,128)S(1)} fusion(bf16[512,256]{1,0:T(8,128)(2,1)S(1)} %pad_maximum_fusion.1, bf16[4,8192,512]{2,1,0:T(8,128)(2,1)} %refs_0_.1, f32[4096]{0:T(1024)S(1)} %bitcast.262), kind=kOutput, calls=%fused_computation.13 | convolution fusion | flops 1074790400 | bytes 8667136 | tf_op jit(solution)/shard_map/dot_general | solution.py:151
  84.7 2.1 collective-permute-done.14
  86.8 5.8 %collective-permute-done.13 = f32[256,256]{1,0:T(8,128)S(1)} collective-permute-done((f32[256,256]{1,0:T(8,128)S(1)}, f32[256,256]{1,0:T(8,128)S(1)}, u32[]{:S(2)}, u32[]{:S(2)}) %collective-permute-start.13) | collective-permute-done | bytes 262176 | tf_op jit(solution)/shard_map/ppermute | solution.py:21
  93.5 1.6 collective-permute-done.15
  96.9 6.9 %collective-permute-done.16 = f32[256,256]{1,0:T(8,128)S(1)} collective-permute-done((f32[256,256]{1,0:T(8,128)S(1)}, f32[256,256]{1,0:T(8,128)S(1)}, u32[]{:S(2)}, u32[]{:S(2)}) %collective-permute-start.16) | collective-permute-done | bytes 262176 | tf_op jit(solution)/shard_map/ppermute | solution.py:21
  106.5 5.0 %collective-permute-done.17 = f32[256,256]{1,0:T(8,128)S(1)} collective-permute-done((f32[256,256]{1,0:T(8,128)S(1)}, f32[256,256]{1,0:T(8,128)S(1)}, u32[]{:S(2)}, u32[]{:S(2)}) %collective-permute-start.17) | collective-permute-done | bytes 262176 | tf_op jit(solution)/shard_map/ppermute | solution.py:21
  114.9 1.8 collective-permute-start.23
  117.7 5.5 %fusion.7 = f32[4096,256]{0,1:T(8,128)} fusion(f32[4096,256]{0,1:T(8,128)S(1)} %fusion.9, bf16[512,256]{1,0:T(8,128)(2,1)S(1)} %pad_maximum_fusion.2, bf16[4,8192,512]{2,1,0:T(8,128)(2,1)} %refs_0_.1, f32[4096]{0:T(1024)S(1)} %bitcast.261), kind=kOutput, calls=%fused_computation.11 | convolution fusion | flops 1075838976 | bytes 12861440 | tf_op jit(solution)/shard_map/dot_general | solution.py:151
  123.2 2.7 %collective-permute-done.23 = f32[256,256]{1,0:T(8,128)S(1)} collective-permute-done((f32[256,256]{1,0:T(8,128)S(1)}, f32[256,256]{1,0:T(8,128)S(1)}, u32[]{:S(2)}, u32[]{:S(2)}) %collective-permute-start.23) | collective-permute-done | bytes 262176 | tf_op jit(solution)/shard_map/ppermute | solution.py:21
  126.0 4.6 %collective-permute-done.22 = f32[256,256]{1,0:T(8,128)S(1)} collective-permute-done((f32[256,256]{1,0:T(8,128)S(1)}, f32[256,256]{1,0:T(8,128)S(1)}, u32[]{:S(2)}, u32[]{:S(2)}) %collective-permute-start.22) | collective-permute-done | bytes 262176 | tf_op jit(solution)/shard_map/ppermute | solution.py:21
  130.8 2.1 collective-permute-start.24
  132.9 5.5 %fusion.5 = f32[4096,256]{0,1:T(8,128)} fusion(f32[4096,256]{0,1:T(8,128)S(1)} %fusion.8, bf16[512,256]{1,0:T(8,128)(2,1)S(1)} %pad_maximum_fusion.2, bf16[4,8192,512]{2,1,0:T(8,128)(2,1)} %refs_0_.1, f32[4096]{0:T(1024)S(1)} %bitcast.260), kind=kOutput, calls=%fused_computation.8 | convolution fusion | flops 1075838976 | bytes 12861440 | tf_op jit(solution)/shard_map/dot_general | solution.py:151
  139.4 5.4 %collective-permute-done.24 = f32[256,256]{1,0:T(8,128)S(1)} collective-permute-done((f32[256,256]{1,0:T(8,128)S(1)}, f32[256,256]{1,0:T(8,128)S(1)}, u32[]{:S(2)}, u32[]{:S(2)}) %collective-permute-start.24) | collective-permute-done | bytes 262176 | tf_op jit(solution)/shard_map/ppermute | solution.py:21
  149.7 1.5 collective-permute-start.29
  153.1 3.7 %collective-permute-done.27 = f32[256,256]{1,0:T(8,128)S(1)} collective-permute-done((f32[256,256]{1,0:T(8,128)}, f32[256,256]{1,0:T(8,128)S(1)}, u32[]{:S(2)}, u32[]{:S(2)}) %collective-permute-start.27) | collective-permute-done | bytes 262176 | tf_op jit(solution)/shard_map/ppermute | solution.py:21
  157.9 1.8 slice_add_fusion.5
  159.7 1.5 collective-permute-start.28
  162.4 1.6 copy.17
  172.9 1.8 collective-permute-start.34
  175.8 3.7 %fusion.3 = f32[4096,256]{0,1:T(8,128)S(1)} fusion(f32[4096,256]{0,1:T(8,128)S(1)} %copy-done.19, bf16[512,256]{1,0:T(8,128)(2,1)S(1)} %pad_maximum_fusion.3, bf16[4,8192,512]{2,1,0:T(8,128)(2,1)} %refs_0_.1, f32[4096]{0:T(1024)S(1)} %bitcast.259), kind=kOutput, calls=%fused_computation.5 | convolution fusion | flops 1075838976 | bytes 12861440 | tf_op jit(solution)/shard_map/dot_general | solution.py:151
  179.5 4.5 %collective-permute-done.34 = f32[256,256]{1,0:T(8,128)S(1)} collective-permute-done((f32[256,256]{1,0:T(8,128)S(1)}, f32[256,256]{1,0:T(8,128)S(1)}, u32[]{:S(2)}, u32[]{:S(2)}) %collective-permute-start.34) | collective-permute-done | bytes 262176 | tf_op jit(solution)/shard_map/ppermute | solution.py:21
  184.0 4.7 %collective-permute-done.33 = f32[256,256]{1,0:T(8,128)S(1)} collective-permute-done((f32[256,256]{1,0:T(8,128)S(1)}, f32[256,256]{1,0:T(8,128)S(1)}, u32[]{:S(2)}, u32[]{:S(2)}) %collective-permute-start.33) | collective-permute-done | bytes 262176 | tf_op jit(solution)/shard_map/ppermute | solution.py:21
  188.9 2.0 collective-permute-start.35
  191.0 3.7 %fusion.1 = f32[4096,256]{0,1:T(8,128)S(1)} fusion(f32[4096,256]{0,1:T(8,128)S(1)} %copy-done.18, bf16[512,256]{1,0:T(8,128)(2,1)S(1)} %pad_maximum_fusion.3, bf16[4,8192,512]{2,1,0:T(8,128)(2,1)} %refs_0_.1, f32[4096]{0:T(1024)S(1)} %bitcast.258), kind=kOutput, calls=%fused_computation.2 | convolution fusion | flops 1075838976 | bytes 12861440 | tf_op jit(solution)/shard_map/dot_general | solution.py:151
  194.7 2.9 %collective-permute-done.36 = f32[256,256]{1,0:T(8,128)S(1)} collective-permute-done((f32[256,256]{1,0:T(8,128)S(1)}, f32[256,256]{1,0:T(8,128)S(1)}, u32[]{:S(2)}, u32[]{:S(2)}) %collective-permute-start.36) | collective-permute-done | bytes 262176 | tf_op jit(solution)/shard_map/ppermute | solution.py:21
  197.6 5.3 %collective-permute-done.35 = f32[256,256]{1,0:T(8,128)S(1)} collective-permute-done((f32[256,256]{1,0:T(8,128)S(1)}, f32[256,256]{1,0:T(8,128)S(1)}, u32[]{:S(2)}, u32[]{:S(2)}) %collective-permute-start.35) | collective-permute-done | bytes 262176 | tf_op jit(solution)/shard_map/ppermute | solution.py:21
  209.8 11.3 %collective-permute-done.45 = f32[512,256]{0,1:T(8,128)S(1)} collective-permute-done((f32[512,256]{0,1:T(8,128)S(1)}, f32[512,256]{0,1:T(8,128)S(1)}, u32[]{:S(2)}, u32[]{:S(2)}) %collective-permute-start.45) | collective-permute-done | bytes 524320 | tf_op jit(solution)/shard_map/ppermute | solution.py:21
  224.1 1.6 collective-permute-start.44
  227.7 8.6 %collective-permute-done.39 = f32[512,256]{0,1:T(8,128)S(1)} collective-permute-done((f32[512,256]{0,1:T(8,128)S(1)}, f32[512,256]{0,1:T(8,128)S(1)}, u32[]{:S(2)}, u32[]{:S(2)}) %collective-permute-start.39) | collective-permute-done | bytes 524320 | tf_op jit(solution)/shard_map/ppermute | solution.py:21
  236.2 9.4 %collective-permute-done.46 = f32[512,256]{0,1:T(8,128)S(1)} collective-permute-done((f32[512,256]{0,1:T(8,128)S(1)}, f32[512,256]{0,1:T(8,128)S(1)}, u32[]{:S(2)}, u32[]{:S(2)}) %collective-permute-start.46) | collective-permute-done | bytes 524320 | tf_op jit(solution)/shard_map/ppermute | solution.py:21
  245.6 1.7 collective-permute-done.44
  (270 shorter events, 66.5 us)
Async XLA Ops:
  4.2 16.6 %collective-permute-start = (f32[256,256]{1,0:T(8,128)S(1)}, f32[256,256]{1,0:T(8,128)S(1)}, u32[]{:S(2)}, u32[]{:S(2)}) collective-permute-start(f32[256,256]{1,0:T(8,128)S(1)} %convolution_add_fusion.9), channel_id=1, source_target_pairs={{0,8},{8,0},{16,24},{24,16},{1,9},{9,1},{17,25},{25,17},{2,10},{10... | collective-permute-start | bytes 786440 | tf_op jit(solution)/shard_map/ppermute | solution.py:21
  8.0 13.5 %collective-permute-start.1 = (f32[256,256]{1,0:T(8,128)S(1)}, f32[256,256]{1,0:T(8,128)S(1)}, u32[]{:S(2)}, u32[]{:S(2)}) collective-permute-start(f32[256,256]{1,0:T(8,128)S(1)} %convolution_add_fusion.6), channel_id=1, source_target_pairs={{0,24},{8,16},{16,8},{24,0},{1,25},{9,17},{17,9},{25,1},{2,26},{10... | collective-permute-start | bytes 786440 | tf_op jit(solution)/shard_map/ppermute | solution.py:21
  22.3 8.8 %collective-permute-start.3 = (f32[256,256]{1,0:T(8,128)}, f32[256,256]{1,0:T(8,128)}, u32[]{:S(2)}, u32[]{:S(2)}) collective-permute-start(f32[256,256]{1,0:T(8,128)} %add.357), channel_id=1, source_target_pairs={{0,8},{8,0},{16,24},{24,16},{1,9},{9,1},{17,25},{25,17},{2,10},{10... | collective-permute-start | bytes 786440 | tf_op jit(solution)/shard_map/ppermute | solution.py:21
  23.6 13.4 %collective-permute-start.2 = (f32[256,256]{1,0:T(8,128)}, f32[256,256]{1,0:T(8,128)}, u32[]{:S(2)}, u32[]{:S(2)}) collective-permute-start(f32[256,256]{1,0:T(8,128)} %add.353), channel_id=1, source_target_pairs={{0,24},{8,16},{16,8},{24,0},{1,25},{9,17},{17,9},{25,1},{2,26},{10... | collective-permute-start | bytes 786440 | tf_op jit(solution)/shard_map/ppermute | solution.py:21
  38.5 2.2 collective-permute-start.4
  41.1 8.8 %collective-permute-start.5 = (f32[256,256]{1,0:T(8,128)S(1)}, f32[256,256]{1,0:T(8,128)S(1)}, u32[]{:S(2)}, u32[]{:S(2)}) collective-permute-start(f32[256,256]{1,0:T(8,128)S(1)} %get-tuple-element.129), channel_id=1, source_target_pairs={{0,2},{1,3},{2,0},{3,1},{4,6},{5,7},{6,4},{7,5},{8,10},{9,11},{10,... | collective-permute-start | bytes 786440 | tf_op jit(solution)/shard_map/ppermute | solution.py:21
  42.7 8.4 %collective-permute-start.7 = (f32[256,256]{1,0:T(8,128)S(1)}, f32[256,256]{1,0:T(8,128)S(1)}, u32[]{:S(2)}, u32[]{:S(2)}) collective-permute-start(f32[256,256]{1,0:T(8,128)S(1)} %get-tuple-element.130), channel_id=1, source_target_pairs={{0,4},{1,5},{2,6},{3,7},{4,0},{5,1},{6,2},{7,3},{8,12},{9,13},{10,... | collective-permute-start | bytes 786440 | tf_op jit(solution)/shard_map/ppermute | solution.py:21
  51.1 7.7 %collective-permute-start.6 = (f32[256,256]{1,0:T(8,128)S(1)}, f32[256,256]{1,0:T(8,128)S(1)}, u32[]{:S(2)}, u32[]{:S(2)}) collective-permute-start(f32[256,256]{1,0:T(8,128)S(1)} %get-tuple-element.127), channel_id=1, source_target_pairs={{0,4},{1,5},{2,6},{3,7},{4,0},{5,1},{6,2},{7,3},{8,12},{9,13},{10,... | collective-permute-start | bytes 786440 | tf_op jit(solution)/shard_map/ppermute | solution.py:21
  52.7 7.3 %collective-permute-start.8 = (f32[256,256]{1,0:T(8,128)S(1)}, f32[256,256]{1,0:T(8,128)S(1)}, u32[]{:S(2)}, u32[]{:S(2)}) collective-permute-start(f32[256,256]{1,0:T(8,128)S(1)} %get-tuple-element.128), channel_id=1, source_target_pairs={{0,2},{1,3},{2,0},{3,1},{4,6},{5,7},{6,4},{7,5},{8,10},{9,11},{10,... | collective-permute-start | bytes 786440 | tf_op jit(solution)/shard_map/ppermute | solution.py:21
  60.2 1.6 collective-permute-start.10
  60.2 1.9 collective-permute-start.9
  63.2 11.1 %collective-permute-start.12 = (f32[256,256]{1,0:T(8,128)S(1)}, f32[256,256]{1,0:T(8,128)S(1)}, u32[]{:S(2)}, u32[]{:S(2)}) collective-permute-start(f32[256,256]{1,0:T(8,128)S(1)} %fusion.52), channel_id=1, source_target_pairs={{0,24},{8,16},{16,8},{24,0},{1,25},{9,17},{17,9},{25,1},{2,26},{10... | collective-permute-start | bytes 786440 | tf_op jit(solution)/shard_map/ppermute | solution.py:21
  64.7 13.7 %collective-permute-start.11 = (f32[256,256]{1,0:T(8,128)S(1)}, f32[256,256]{1,0:T(8,128)S(1)}, u32[]{:S(2)}, u32[]{:S(2)}) collective-permute-start(f32[256,256]{1,0:T(8,128)S(1)} %fusion.54), channel_id=1, source_target_pairs={{0,8},{8,0},{16,24},{24,16},{1,9},{9,1},{17,25},{25,17},{2,10},{10... | collective-permute-start | bytes 786440 | tf_op jit(solution)/shard_map/ppermute | solution.py:21
  78.5 8.3 %collective-permute-start.14 = (f32[256,256]{1,0:T(8,128)S(1)}, f32[256,256]{1,0:T(8,128)S(1)}, u32[]{:S(2)}, u32[]{:S(2)}) collective-permute-start(f32[256,256]{1,0:T(8,128)S(1)} %add.372), channel_id=1, source_target_pairs={{0,8},{8,0},{16,24},{24,16},{1,9},{9,1},{17,25},{25,17},{2,10},{10... | collective-permute-start | bytes 786440 | tf_op jit(solution)/shard_map/ppermute | solution.py:21
  78.6 14.0 %collective-permute-start.13 = (f32[256,256]{1,0:T(8,128)S(1)}, f32[256,256]{1,0:T(8,128)S(1)}, u32[]{:S(2)}, u32[]{:S(2)}) collective-permute-start(f32[256,256]{1,0:T(8,128)S(1)} %add.368), channel_id=1, source_target_pairs={{0,24},{8,16},{16,8},{24,0},{1,25},{9,17},{17,9},{25,1},{2,26},{10... | collective-permute-start | bytes 786440 | tf_op jit(solution)/shard_map/ppermute | solution.py:21
  93.1 2.0 collective-permute-start.15
  95.4 8.4 %collective-permute-start.16 = (f32[256,256]{1,0:T(8,128)S(1)}, f32[256,256]{1,0:T(8,128)S(1)}, u32[]{:S(2)}, u32[]{:S(2)}) collective-permute-start(f32[256,256]{1,0:T(8,128)S(1)} %get-tuple-element.125), channel_id=1, source_target_pairs={{0,2},{1,3},{2,0},{3,1},{4,6},{5,7},{6,4},{7,5},{8,10},{9,11},{10,... | collective-permute-start | bytes 786440 | tf_op jit(solution)/shard_map/ppermute | solution.py:21
  96.1 8.1 %collective-permute-start.18 = (f32[256,256]{1,0:T(8,128)S(1)}, f32[256,256]{1,0:T(8,128)S(1)}, u32[]{:S(2)}, u32[]{:S(2)}) collective-permute-start(f32[256,256]{1,0:T(8,128)S(1)} %get-tuple-element.126), channel_id=1, source_target_pairs={{0,4},{1,5},{2,6},{3,7},{4,0},{5,1},{6,2},{7,3},{8,12},{9,13},{10,... | collective-permute-start | bytes 786440 | tf_op jit(solution)/shard_map/ppermute | solution.py:21
  104.2 7.3 %collective-permute-start.17 = (f32[256,256]{1,0:T(8,128)S(1)}, f32[256,256]{1,0:T(8,128)S(1)}, u32[]{:S(2)}, u32[]{:S(2)}) collective-permute-start(f32[256,256]{1,0:T(8,128)S(1)} %get-tuple-element.123), channel_id=1, source_target_pairs={{0,4},{1,5},{2,6},{3,7},{4,0},{5,1},{6,2},{7,3},{8,12},{9,13},{10,... | collective-permute-start | bytes 786440 | tf_op jit(solution)/shard_map/ppermute | solution.py:21
  104.8 6.9 %collective-permute-start.19 = (f32[256,256]{1,0:T(8,128)S(1)}, f32[256,256]{1,0:T(8,128)S(1)}, u32[]{:S(2)}, u32[]{:S(2)}) collective-permute-start(f32[256,256]{1,0:T(8,128)S(1)} %get-tuple-element.124), channel_id=1, source_target_pairs={{0,2},{1,3},{2,0},{3,1},{4,6},{5,7},{6,4},{7,5},{8,10},{9,11},{10,... | collective-permute-start | bytes 786440 | tf_op jit(solution)/shard_map/ppermute | solution.py:21
  111.8 1.6 collective-permute-start.20
  111.9 1.9 collective-permute-start.21
  114.9 11.1 %collective-permute-start.23 = (f32[256,256]{1,0:T(8,128)S(1)}, f32[256,256]{1,0:T(8,128)S(1)}, u32[]{:S(2)}, u32[]{:S(2)}) collective-permute-start(f32[256,256]{1,0:T(8,128)S(1)} %fusion.48), channel_id=1, source_target_pairs={{0,24},{8,16},{16,8},{24,0},{1,25},{9,17},{17,9},{25,1},{2,26},{10... | collective-permute-start | bytes 786440 | tf_op jit(solution)/shard_map/ppermute | solution.py:21
  116.8 13.8 %collective-permute-start.22 = (f32[256,256]{1,0:T(8,128)S(1)}, f32[256,256]{1,0:T(8,128)S(1)}, u32[]{:S(2)}, u32[]{:S(2)}) collective-permute-start(f32[256,256]{1,0:T(8,128)S(1)} %fusion.50), channel_id=1, source_target_pairs={{0,8},{8,0},{16,24},{24,16},{1,9},{9,1},{17,25},{25,17},{2,10},{10... | collective-permute-start | bytes 786440 | tf_op jit(solution)/shard_map/ppermute | solution.py:21
  130.6 8.7 %collective-permute-start.25 = (f32[256,256]{1,0:T(8,128)S(1)}, f32[256,256]{1,0:T(8,128)S(1)}, u32[]{:S(2)}, u32[]{:S(2)}) collective-permute-start(f32[256,256]{1,0:T(8,128)S(1)} %add.389), channel_id=1, source_target_pairs={{0,8},{8,0},{16,24},{24,16},{1,9},{9,1},{17,25},{25,17},{2,10},{10... | collective-permute-start | bytes 786440 | tf_op jit(solution)/shard_map/ppermute | solution.py:21
  130.8 14.0 %collective-permute-start.24 = (f32[256,256]{1,0:T(8,128)S(1)}, f32[256,256]{1,0:T(8,128)S(1)}, u32[]{:S(2)}, u32[]{:S(2)}) collective-permute-start(f32[256,256]{1,0:T(8,128)S(1)} %add.385), channel_id=1, source_target_pairs={{0,24},{8,16},{16,8},{24,0},{1,25},{9,17},{17,9},{25,1},{2,26},{10... | collective-permute-start | bytes 786440 | tf_op jit(solution)/shard_map/ppermute | solution.py:21
  145.2 2.0 collective-permute-start.26
  147.2 21.3 %copy-start.20 = (f32[1,1024,256]{2,1,0:T(8,128)S(1)}, f32[1,1024,256]{2,1,0:T(8,128)}, u32[]{:S(2)}) copy-start(f32[1,1024,256]{2,1,0:T(8,128)} %get-tuple-element.90) | copy-start | bytes 3145732
  148.3 8.6 %collective-permute-start.27 = (f32[256,256]{1,0:T(8,128)}, f32[256,256]{1,0:T(8,128)S(1)}, u32[]{:S(2)}, u32[]{:S(2)}) collective-permute-start(f32[256,256]{1,0:T(8,128)} %get-tuple-element.121), channel_id=1, source_target_pairs={{0,2},{1,3},{2,0},{3,1},{4,6},{5,7},{6,4},{7,5},{8,10},{9,11},{10,... | collective-permute-start | bytes 786440 | tf_op jit(solution)/shard_map/ppermute | solution.py:21
  149.7 8.2 %collective-permute-start.29 = (f32[256,256]{1,0:T(8,128)S(1)}, f32[256,256]{1,0:T(8,128)}, u32[]{:S(2)}, u32[]{:S(2)}) collective-permute-start(f32[256,256]{1,0:T(8,128)S(1)} %get-tuple-element.122), channel_id=1, source_target_pairs={{0,4},{1,5},{2,6},{3,7},{4,0},{5,1},{6,2},{7,3},{8,12},{9,13},{10,... | collective-permute-start | bytes 786440 | tf_op jit(solution)/shard_map/ppermute | solution.py:21
  159.7 7.5 %collective-permute-start.28 = (f32[256,256]{1,0:T(8,128)}, f32[256,256]{1,0:T(8,128)}, u32[]{:S(2)}, u32[]{:S(2)}) collective-permute-start(f32[256,256]{1,0:T(8,128)} %get-tuple-element.119), channel_id=1, source_target_pairs={{0,4},{1,5},{2,6},{3,7},{4,0},{5,1},{6,2},{7,3},{8,12},{9,13},{10,... | collective-permute-start | bytes 786440 | tf_op jit(solution)/shard_map/ppermute | solution.py:21
  161.2 7.2 %collective-permute-start.30 = (f32[256,256]{1,0:T(8,128)}, f32[256,256]{1,0:T(8,128)}, u32[]{:S(2)}, u32[]{:S(2)}) collective-permute-start(f32[256,256]{1,0:T(8,128)} %get-tuple-element.120), channel_id=1, source_target_pairs={{0,2},{1,3},{2,0},{3,1},{4,6},{5,7},{6,4},{7,5},{8,10},{9,11},{10,... | collective-permute-start | bytes 786440 | tf_op jit(solution)/shard_map/ppermute | solution.py:21
  169.9 1.9 collective-permute-start.31
  170.0 1.9 collective-permute-start.32
  172.9 11.1 %collective-permute-start.34 = (f32[256,256]{1,0:T(8,128)S(1)}, f32[256,256]{1,0:T(8,128)S(1)}, u32[]{:S(2)}, u32[]{:S(2)}) collective-permute-start(f32[256,256]{1,0:T(8,128)S(1)} %fusion.44), channel_id=1, source_target_pairs={{0,24},{8,16},{16,8},{24,0},{1,25},{9,17},{17,9},{25,1},{2,26},{10... | collective-permute-start | bytes 786440 | tf_op jit(solution)/shard_map/ppermute | solution.py:21
  175.0 13.8 %collective-permute-start.33 = (f32[256,256]{1,0:T(8,128)S(1)}, f32[256,256]{1,0:T(8,128)S(1)}, u32[]{:S(2)}, u32[]{:S(2)}) collective-permute-start(f32[256,256]{1,0:T(8,128)S(1)} %fusion.46), channel_id=1, source_target_pairs={{0,8},{8,0},{16,24},{24,16},{1,9},{9,1},{17,25},{25,17},{2,10},{10... | collective-permute-start | bytes 786440 | tf_op jit(solution)/shard_map/ppermute | solution.py:21
  188.8 8.8 %collective-permute-start.36 = (f32[256,256]{1,0:T(8,128)S(1)}, f32[256,256]{1,0:T(8,128)S(1)}, u32[]{:S(2)}, u32[]{:S(2)}) collective-permute-start(f32[256,256]{1,0:T(8,128)S(1)} %add.410), channel_id=1, source_target_pairs={{0,8},{8,0},{16,24},{24,16},{1,9},{9,1},{17,25},{25,17},{2,10},{10... | collective-permute-start | bytes 786440 | tf_op jit(solution)/shard_map/ppermute | solution.py:21
  188.9 14.0 %collective-permute-start.35 = (f32[256,256]{1,0:T(8,128)S(1)}, f32[256,256]{1,0:T(8,128)S(1)}, u32[]{:S(2)}, u32[]{:S(2)}) collective-permute-start(f32[256,256]{1,0:T(8,128)S(1)} %add.406), channel_id=1, source_target_pairs={{0,24},{8,16},{16,8},{24,0},{1,25},{9,17},{17,9},{25,1},{2,26},{10... | collective-permute-start | bytes 786440 | tf_op jit(solution)/shard_map/ppermute | solution.py:21
  203.6 3.0 %collective-permute-start.41 = (f32[1024,256]{0,1:T(8,128)S(1)}, f32[1024,256]{0,1:T(8,128)S(1)}, u32[]{:S(2)}, u32[]{:S(2)}) collective-permute-start(f32[1024,256]{0,1:T(8,128)S(1)} %fusion.22), channel_id=1, source_target_pairs={{0,1},{1,0},{2,3},{3,2},{4,5},{5,4},{6,7},{7,6},{8,9},{9,8},{10,11... | collective-permute-start | bytes 3145736 | tf_op jit(solution)/shard_map/ppermute | solution.py:21
  204.3 4.2 %collective-permute-start.38 = (f32[1024,256]{0,1:T(8,128)S(1)}, f32[1024,256]{0,1:T(8,128)S(1)}, u32[]{:S(2)}, u32[]{:S(2)}) collective-permute-start(f32[1024,256]{0,1:T(8,128)S(1)} %fusion.28), channel_id=1, source_target_pairs={{0,1},{1,0},{2,3},{3,2},{4,5},{5,4},{6,7},{7,6},{8,9},{9,8},{10,11... | collective-permute-start | bytes 3145736 | tf_op jit(solution)/shard_map/ppermute | solution.py:21
  205.4 3.9 %collective-permute-start.40 = (f32[1024,256]{0,1:T(8,128)S(1)}, f32[1024,256]{0,1:T(8,128)S(1)}, u32[]{:S(2)}, u32[]{:S(2)}) collective-permute-start(f32[1024,256]{0,1:T(8,128)S(1)} %fusion.25), channel_id=1, source_target_pairs={{0,1},{1,0},{2,3},{3,2},{4,5},{5,4},{6,7},{7,6},{8,9},{9,8},{10,11... | collective-permute-start | bytes 3145736 | tf_op jit(solution)/shard_map/ppermute | solution.py:21
  206.0 21.1 %collective-permute-start.37 = (f32[1024,256]{0,1:T(8,128)S(1)}, f32[1024,256]{0,1:T(8,128)S(1)}, u32[]{:S(2)}, u32[]{:S(2)}) collective-permute-start(f32[1024,256]{0,1:T(8,128)S(1)} %fusion.31), channel_id=1, source_target_pairs={{0,1},{1,0},{2,3},{3,2},{4,5},{5,4},{6,7},{7,6},{8,9},{9,8},{10,11... | collective-permute-start | bytes 3145736 | tf_op jit(solution)/shard_map/ppermute | solution.py:21
  207.2 13.9 %collective-permute-start.45 = (f32[512,256]{0,1:T(8,128)S(1)}, f32[512,256]{0,1:T(8,128)S(1)}, u32[]{:S(2)}, u32[]{:S(2)}) collective-permute-start(f32[512,256]{0,1:T(8,128)S(1)} %get-tuple-element.104), channel_id=1, source_target_pairs={{0,4},{1,5},{2,6},{3,7},{4,0},{5,1},{6,2},{7,3},{8,12},{9,13},{10,... | collective-permute-start | bytes 1572872 | tf_op jit(solution)/shard_map/ppermute | solution.py:21
  207.7 15.6 %collective-permute-start.42 = (f32[512,256]{0,1:T(8,128)S(1)}, f32[512,256]{0,1:T(8,128)S(1)}, u32[]{:S(2)}, u32[]{:S(2)}) collective-permute-start(f32[512,256]{0,1:T(8,128)S(1)} %get-tuple-element.103), channel_id=1, source_target_pairs={{0,2},{1,3},{2,0},{3,1},{4,6},{5,7},{6,4},{7,5},{8,10},{9,11},{10,... | collective-permute-start | bytes 1572872 | tf_op jit(solution)/shard_map/ppermute | solution.py:21
  221.3 14.9 %collective-permute-start.39 = (f32[512,256]{0,1:T(8,128)S(1)}, f32[512,256]{0,1:T(8,128)S(1)}, u32[]{:S(2)}, u32[]{:S(2)}) collective-permute-start(f32[512,256]{0,1:T(8,128)S(1)} %get-tuple-element.99), channel_id=1, source_target_pairs={{0,2},{1,3},{2,0},{3,1},{4,6},{5,7},{6,4},{7,5},{8,10},{9,11},{10,... | collective-permute-start | bytes 1572872 | tf_op jit(solution)/shard_map/ppermute | solution.py:21
  222.2 23.5 %collective-permute-start.46 = (f32[512,256]{0,1:T(8,128)S(1)}, f32[512,256]{0,1:T(8,128)S(1)}, u32[]{:S(2)}, u32[]{:S(2)}) collective-permute-start(f32[512,256]{0,1:T(8,128)S(1)} %get-tuple-element.100), channel_id=1, source_target_pairs={{0,2},{1,3},{2,0},{3,1},{4,6},{5,7},{6,4},{7,5},{8,10},{9,11},{10,... | collective-permute-start | bytes 1572872 | tf_op jit(solution)/shard_map/ppermute | solution.py:21
  223.5 22.1 %collective-permute-start.43 = (f32[512,256]{0,1:T(8,128)S(1)}, f32[512,256]{0,1:T(8,128)S(1)}, u32[]{:S(2)}, u32[]{:S(2)}) collective-permute-start(f32[512,256]{0,1:T(8,128)S(1)} %get-tuple-element.101), channel_id=1, source_target_pairs={{0,4},{1,5},{2,6},{3,7},{4,0},{5,1},{6,2},{7,3},{8,12},{9,13},{10,... | collective-permute-start | bytes 1572872 | tf_op jit(solution)/shard_map/ppermute | solution.py:21
  224.1 23.2 %collective-permute-start.44 = (f32[512,256]{0,1:T(8,128)S(1)}, f32[512,256]{0,1:T(8,128)S(1)}, u32[]{:S(2)}, u32[]{:S(2)}) collective-permute-start(f32[512,256]{0,1:T(8,128)S(1)} %get-tuple-element.102), channel_id=1, source_target_pairs={{0,4},{1,5},{2,6},{3,7},{4,0},{5,1},{6,2},{7,3},{8,12},{9,13},{10,... | collective-permute-start | bytes 1572872 | tf_op jit(solution)/shard_map/ppermute | solution.py:21
  (46 other events, 290.8 us)

commit v3 on v2

--- a/solution.py
+++ b/solution.py
@@ -4,6 +4,7 @@
 import jax.numpy as jnp
 from jax import lax
 from jax.experimental import pallas as pl
+from jax.experimental.layout import Layout, with_layout_constraint
 from jax.experimental.pallas import tpu as pltpu
 from jax.sharding import PartitionSpec as P
 
@@ -47,7 +48,7 @@
 
 def sum_row(parts, queue):
     if lax.axis_size("row") == 4:
-        return sum_parts(parts, "row", (1, 3), queue)
+        return sum_parts(parts, "row", (1, 2), queue)
     bit = lax.axis_index("row") & 1
     x = jnp.concatenate(parts, axis=0)
     mine = half(x, bit, 0) + swap(half(x, 1 - bit, 0), "row", 1)
@@ -92,6 +93,10 @@
     return out[:2], out[2:]
 
 
+def row_major(x):
+    return with_layout_constraint(x, Layout(major_to_minor=tuple(range(x.ndim))))
+
+
 def last_kernel(base, *refs):
     f_ref, outs, sem = refs[0], refs[1:-1], refs[-1]
     own = outs[0].shape[0]
@@ -139,7 +144,7 @@
     blocks = me ^ jnp.arange(n, dtype=jnp.int32)
     gain = jnp.repeat(window_mask.astype(F32), BLK, axis=1)
     gains = [half(gain, s, 1) for s in sides]
-    rhs = [[halves(half(r, s, 0)) for s in sides] for r in rhs_window]
+    rhs = [None] + [[halves(half(rhs_window[t], s, 0)) for s in sides] for t in range(1, PANELS)]
     own = rhs_below.shape[0]
     rows = below_factor.shape[1] // 2
     below_gain = jnp.repeat(below_mask.astype(F32), BLK, axis=1)
@@ -150,7 +155,7 @@
         factor = below_factor[panel, top * rows : (top + 1) * rows]
         term = jnp.dot(factor, after(solved, dep), preferred_element_type=F32)
         term = below_gain[panel, top * rows : (top + 1) * rows, None] * term
-        early[top] = early[top] + term if panel else term
+        early[top] = row_major(early[top] + term if panel else term)
         return early[top]
 
     def stage_step(dep):
@@ -159,15 +164,18 @@
 
     def last_step(dep):
         store["last"] = last_rows(after(blocks, dep), below_factor, own)
-        return store["last"][0]
+        gain_of = after(below_gain[-1], dep)
+        scales = [lax.dynamic_slice_in_dim(gain_of, (me ^ q) * own, own, 0) for q in range(n)]
+        store["scale"] = lax.optimization_barrier(tuple(scales))
+        return store["scale"][0]
 
     def tail(q, solved):
         term = jnp.dot(store["last"][q], solved, preferred_element_type=F32)
-        scale = lax.dynamic_slice_in_dim(below_gain[-1], (me ^ q) * own, own, 0)
+        scale = store["scale"][q]
         at = ((me ^ q) % (n // 2)) * own
         parts = [lax.dynamic_slice_in_dim(e, at, own, 0) for e in early]
         base = jnp.where((me ^ q) < n // 2, parts[0], parts[1])
-        return base + scale[:, None] * term
+        return row_major(base + scale[:, None] * term)
 
     def update(target, side, solved):
         total = None
@@ -188,13 +196,13 @@
             back = [swap(h, "col", 1) for h in home]
             right = [[r - b for r, b in zip(rhs[target][0], back)], [r - h for r, h in zip(rhs[target][1], home)]]
         parts = []
-        for piece in range(2):
+        if target == 0:
+            reduced = rhs_window[0].astype(BF16)
+            parts = [jnp.dot(d, reduced, preferred_element_type=F32) for d in halves(dinv[0])]
+        for piece in range(2 if target else 0):
             total = None
             for side in (1, 0):
-                if target == 0:
-                    inverse = half(dinv[0], sides[side], 1)
-                else:
-                    inverse = store["dinv"][side][target]
+                inverse = store["dinv"][side][target]
                 height, width = inverse.shape[0] // 2, inverse.shape[1] // 2
                 for k in range(2):
                     block = inverse[piece * height : (piece + 1) * height, k * width : (k + 1) * width]
@@ -210,8 +218,10 @@
             queue = [functools.partial(early_step, target, top, solved[-1]) for top in range(2)]
     sent = {q: swap(tail(q, solved[-1]), "col", 1) for q in range(n - 1, 0, -2)}
     sums = {q: halves(tail(q, solved[-1]) + sent[q + 1]) for q in range(n - 2, -1, -2)}
+    sums = {q: lax.optimization_barrier(tuple(x)) for q, x in sums.items()}
     done = [scatter({q: x[j] for q, x in sums.items()}, j, bits) for j in range(2)]
-    return (jnp.stack(solutions), rhs_below - jnp.concatenate(done, axis=0))
+    below = [r - d for r, d in zip(halves(rhs_below), done)]
+    return (jnp.stack(solutions), jnp.concatenate(below, axis=0))
 
 
 def solution(mesh):

time: 250 us -> 243 us (0.972)
  local copies, waits for them, and re-layouts: 16.7 us -> 7.6 us
  waiting for transfers between devices: 121 us -> 130 us
  other arithmetic: 13.7 us -> 6.46 us
    ppermute x47, waiting for transfers between devices: 121 us -> 130 us  [swap(): return lax.ppermute(x, axis, [(i, i ^ mask) for i in range(n)])]
    add x19, other arithmetic: 7.22 us -> 1.8 us  [sum_parts(): new = [p + g for p, g in zip(parts, got)]]
    dot_general x0 -> x2, matrix products: none -> 3.39 us  [local(): jnp.dot(d, reduced, preferred_element_type=F32)]
    unnamed x100 -> x40, local copies, waits for them, and re-layouts: 6.81 us -> 3.52 us
    another operation x3 -> x0, local copies, waits for them, and re-layouts: 2.51 us -> none  [the longest x2 2.46 us: local(): rhs = [[halves(half(r, s, 0)) for s in sides] for r in rhs_window]]
    dot_general x32 -> x24, matrix products: 6.83 us -> 4.44 us  [local(): jnp.dot(block, right[side][k].astype(BF16), preferred_element_type=F32)]
  transfers between devices with their start and end apart: 47 -> 47, of which waited for: 38 -> 40; matrix products, arithmetic and copies ran while one was open for 20% -> 16% of each run, Pallas kernels for 4% -> 4%
where the time goes in v3:
time: 243 us
  waiting for transfers between devices  130 us (53%)
  starting transfers between devices  47.4 us (20%)
  matrix products  39.9 us (16%)
  Pallas kernels  9.76 us (4%)
  local copies, waits for them, and re-layouts  7.6 us (3%)
  other arithmetic  6.46 us (3%)
    ppermute x47, waiting for transfers between devices, swap(): return lax.ppermute(x, axis, [(i, i ^ mask) for i in range(n)])  130 us
    ppermute x47, starting transfers between devices, swap(): return lax.ppermute(x, axis, [(i, i ^ mask) for i in range(n)])  47.4 us
    dot_general x6, matrix products, early_step(): term = jnp.dot(factor, after(solved, dep), preferred_element_type=F32)  23.5 us
    pallas_call x1, Pallas kernels, stage(): pl.pallas_call(stage_kernel, out_shape=[jax.ShapeDtypeStruct(shape, BF16)...  5.74 us
  transfers between devices with their start and end apart: 47, of which 40 were waited for; matrix products, arithmetic and copies ran while one was open for 16% of the time, Pallas kernels for 4%

profile of v3, /device:TPU:0, one launch (start us, length us, event | category | flops | bytes accessed | tf_op | source)
XLA Modules:
  0.0 243.0 jit_solution(2106351629726551394)
XLA Ops:
  0.6 1.7 fusion.68
  2.3 4.1 %collective-permute-start.1 = (f32[256,256]{1,0:T(8,128)S(1)}, f32[256,256]{1,0:T(8,128)S(1)}, u32[]{:S(2)}, u32[]{:S(2)}) collective-permute-start(f32[256,256]{1,0:T(8,128)S(1)} %fusion.68), channel_id=1, source_target_pairs={{0,16},{8,24},{16,0},{24,8},{1,17},{9,25},{17,1},{25,9},{2,18},{10... | collective-permute-start | bytes 786440 | tf_op jit(solution)/shard_map/ppermute | solution.py:22
  6.4 1.7 fusion.70
  8.1 1.6 collective-permute-start
  10.8 5.7 %stage.1 = (bf16[6,512,512]{2,1,0:T(8,128)(2,1)S(1)}, bf16[6,512,512]{2,1,0:T(8,128)(2,1)}, bf16[4,512,512]{2,1,0:T(8,128)(2,1)S(1)}, bf16[4,512,512]{2,1,0:T(8,128)(2,1)S(1)}) custom-call(s32[1]{0:T(128)} %bitcast.3.sel, bf16[6,1024,512]{2,1,0:T(8,128)(2,1)} %c_ref.1, bf16[4,512,1024]{2,1,0:T(8,128)(2,1)} %d_ref.1), custom_call_target="tpu_custom_call" | custom-call | tf_op jit(solution)/shard_map/stage/pallas_call | solution.py:84
  17.9 1.7 copy-done.2
  20.5 3.0 %collective-permute-start.2 = (f32[256,256]{1,0:T(8,128)S(1)}, f32[256,256]{1,0:T(8,128)S(1)}, u32[]{:S(2)}, u32[]{:S(2)}) collective-permute-start(f32[256,256]{1,0:T(8,128)S(1)} %add.324), channel_id=1, source_target_pairs={{0,16},{8,24},{16,0},{24,8},{1,17},{9,25},{17,1},{25,9},{2,18},{10... | collective-permute-start | bytes 786440 | tf_op jit(solution)/shard_map/ppermute | solution.py:22
  24.4 8.3 %collective-permute-done.3 = f32[256,256]{1,0:T(8,128)S(1)} collective-permute-done((f32[256,256]{1,0:T(8,128)S(1)}, f32[256,256]{1,0:T(8,128)S(1)}, u32[]{:S(2)}, u32[]{:S(2)}) %collective-permute-start.3) | collective-permute-done | bytes 262176 | tf_op jit(solution)/shard_map/ppermute | solution.py:22
  32.8 1.7 collective-permute-done.2
  38.6 1.6 collective-permute-start.5
  40.1 1.5 collective-permute-start.7
  42.5 4.8 %collective-permute-done.5 = f32[256,256]{1,0:T(8,128)S(1)} collective-permute-done((f32[256,256]{1,0:T(8,128)S(1)}, f32[256,256]{1,0:T(8,128)S(1)}, u32[]{:S(2)}, u32[]{:S(2)}) %collective-permute-start.5) | collective-permute-done | bytes 262176 | tf_op jit(solution)/shard_map/ppermute | solution.py:22
  48.6 1.6 collective-permute-start.6
  51.1 5.2 %collective-permute-done.6 = f32[256,256]{1,0:T(8,128)S(1)} collective-permute-done((f32[256,256]{1,0:T(8,128)S(1)}, f32[256,256]{1,0:T(8,128)S(1)}, u32[]{:S(2)}, u32[]{:S(2)}) %collective-permute-start.6) | collective-permute-done | bytes 262176 | tf_op jit(solution)/shard_map/ppermute | solution.py:22
  61.0 3.1 %collective-permute-start.11 = (f32[256,256]{1,0:T(8,128)S(1)}, f32[256,256]{1,0:T(8,128)S(1)}, u32[]{:S(2)}, u32[]{:S(2)}) collective-permute-start(f32[256,256]{1,0:T(8,128)S(1)} %fusion.54), channel_id=1, source_target_pairs={{0,8},{8,0},{16,24},{24,16},{1,9},{9,1},{17,25},{25,17},{2,10},{10... | collective-permute-start | bytes 786440 | tf_op jit(solution)/shard_map/ppermute | solution.py:22
  64.0 3.0 %fusion.9 = f32[4096,256]{1,0:T(8,128)S(1)} fusion(bf16[512,256]{1,0:T(8,128)(2,1)S(1)} %pad_maximum_fusion.2, bf16[4,8192,512]{2,1,0:T(8,128)(2,1)} %refs_0_.1, f32[4096]{0:T(1024)S(1)} %bitcast.254), kind=kOutput, calls=%fused_computation.15 | convolution fusion | flops 1074790400 | bytes 8667136 | tf_op jit(solution)/shard_map/dot_general | solution.py:156
  67.1 8.4 %collective-permute-done.12 = f32[256,256]{1,0:T(8,128)S(1)} collective-permute-done((f32[256,256]{1,0:T(8,128)S(1)}, f32[256,256]{1,0:T(8,128)S(1)}, u32[]{:S(2)}, u32[]{:S(2)}) %collective-permute-start.12) | collective-permute-done | bytes 262176 | tf_op jit(solution)/shard_map/ppermute | solution.py:22
  76.1 2.1 collective-permute-start.13
  78.1 3.0 %fusion.8 = f32[4096,256]{1,0:T(8,128)S(1)} fusion(bf16[512,256]{1,0:T(8,128)(2,1)S(1)} %pad_maximum_fusion.2, bf16[4,8192,512]{2,1,0:T(8,128)(2,1)} %refs_0_.1, f32[4096]{0:T(1024)S(1)} %bitcast.253), kind=kOutput, calls=%fused_computation.13 | convolution fusion | flops 1074790400 | bytes 8667136 | tf_op jit(solution)/shard_map/dot_general | solution.py:156
  81.2 7.0 %collective-permute-done.14 = f32[256,256]{1,0:T(8,128)S(1)} collective-permute-done((f32[256,256]{1,0:T(8,128)S(1)}, f32[256,256]{1,0:T(8,128)S(1)}, u32[]{:S(2)}, u32[]{:S(2)}) %collective-permute-start.14) | collective-permute-done | bytes 262176 | tf_op jit(solution)/shard_map/ppermute | solution.py:22
  88.2 2.3 collective-permute-done.13
  91.3 1.6 collective-permute-done.15
  94.8 6.9 %collective-permute-done.16 = f32[256,256]{1,0:T(8,128)S(1)} collective-permute-done((f32[256,256]{1,0:T(8,128)S(1)}, f32[256,256]{1,0:T(8,128)S(1)}, u32[]{:S(2)}, u32[]{:S(2)}) %collective-permute-start.16) | collective-permute-done | bytes 262176 | tf_op jit(solution)/shard_map/ppermute | solution.py:22
  104.4 5.0 %collective-permute-done.17 = f32[256,256]{1,0:T(8,128)S(1)} collective-permute-done((f32[256,256]{1,0:T(8,128)S(1)}, f32[256,256]{1,0:T(8,128)S(1)}, u32[]{:S(2)}, u32[]{:S(2)}) %collective-permute-start.17) | collective-permute-done | bytes 262176 | tf_op jit(solution)/shard_map/ppermute | solution.py:22
  113.3 1.7 collective-permute-start.22
  115.0 5.6 %fusion.7 = f32[4096,256]{1,0:T(8,128)} fusion(f32[4096,256]{1,0:T(8,128)S(1)} %fusion.9, bf16[512,256]{1,0:T(8,128)(2,1)S(1)} %pad_maximum_fusion.3, bf16[4,8192,512]{2,1,0:T(8,128)(2,1)} %refs_0_.1, f32[4096]{0:T(1024)S(1)} %bitcast.251), kind=kOutput, calls=%fused_computation.11 | convolution fusion | flops 1075838976 | bytes 12861440 | tf_op jit(solution)/shard_map/dot_general | solution.py:156
  120.6 5.9 %collective-permute-done.23 = f32[256,256]{1,0:T(8,128)S(1)} collective-permute-done((f32[256,256]{1,0:T(8,128)S(1)}, f32[256,256]{1,0:T(8,128)S(1)}, u32[]{:S(2)}, u32[]{:S(2)}) %collective-permute-start.23) | collective-permute-done | bytes 262176 | tf_op jit(solution)/shard_map/ppermute | solution.py:22
  127.2 2.8 %collective-permute-start.24 = (f32[256,256]{1,0:T(8,128)S(1)}, f32[256,256]{1,0:T(8,128)S(1)}, u32[]{:S(2)}, u32[]{:S(2)}) collective-permute-start(f32[256,256]{1,0:T(8,128)S(1)} %add.363), channel_id=1, source_target_pairs={{0,16},{8,24},{16,0},{24,8},{1,17},{9,25},{17,1},{25,9},{2,18},{10... | collective-permute-start | bytes 786440 | tf_op jit(solution)/shard_map/ppermute | solution.py:22
  130.0 5.6 %fusion.5 = f32[4096,256]{1,0:T(8,128)} fusion(f32[4096,256]{1,0:T(8,128)S(1)} %fusion.8, bf16[512,256]{1,0:T(8,128)(2,1)S(1)} %pad_maximum_fusion.3, bf16[4,8192,512]{2,1,0:T(8,128)(2,1)} %refs_0_.1, f32[4096]{0:T(1024)S(1)} %bitcast.250), kind=kOutput, calls=%fused_computation.8 | convolution fusion | flops 1075838976 | bytes 12861440 | tf_op jit(solution)/shard_map/dot_general | solution.py:156
  135.6 4.6 %collective-permute-done.25 = f32[256,256]{1,0:T(8,128)S(1)} collective-permute-done((f32[256,256]{1,0:T(8,128)S(1)}, f32[256,256]{1,0:T(8,128)S(1)}, u32[]{:S(2)}, u32[]{:S(2)}) %collective-permute-start.25) | collective-permute-done | bytes 262176 | tf_op jit(solution)/shard_map/ppermute | solution.py:22
  146.4 1.5 collective-permute-start.29
  148.0 4.0 %last_rows.1 = (bf16[1024,512]{1,0:T(8,128)(2,1)S(1)}, bf16[1024,512]{1,0:T(8,128)(2,1)S(1)}, bf16[1024,512]{1,0:T(8,128)(2,1)S(1)}, bf16[1024,512]{1,0:T(8,128)...) custom-call(s32[8]{0:T(128)S(1)} %iota_xor_fusion.base, ...), custom_call_target="tpu_custom_call" | custom-call | tf_op jit(solution)/shard_map/last_rows/pallas_call | solution.py:116
  152.1 1.6 collective-permute-done.27
  155.9 1.6 collective-permute-start.28
  158.2 5.0 %collective-permute-done.28 = f32[256,256]{1,0:T(8,128)S(1)} collective-permute-done((f32[256,256]{1,0:T(8,128)S(1)}, f32[256,256]{1,0:T(8,128)S(1)}, u32[]{:S(2)}, u32[]{:S(2)}) %collective-permute-start.28) | collective-permute-done | bytes 262176 | tf_op jit(solution)/shard_map/ppermute | solution.py:22
  168.1 2.8 %collective-permute-start.33 = (f32[256,256]{1,0:T(8,128)S(1)}, f32[256,256]{1,0:T(8,128)S(1)}, u32[]{:S(2)}, u32[]{:S(2)}) collective-permute-start(f32[256,256]{1,0:T(8,128)S(1)} %fusion.46), channel_id=1, source_target_pairs={{0,8},{8,0},{16,24},{24,16},{1,9},{9,1},{17,25},{25,17},{2,10},{10... | collective-permute-start | bytes 786440 | tf_op jit(solution)/shard_map/ppermute | solution.py:22
  170.9 3.2 %fusion.3 = f32[4096,256]{1,0:T(8,128)S(1)} fusion(f32[4096,256]{1,0:T(8,128)S(1)} %copy-done.5, bf16[512,256]{1,0:T(8,128)(2,1)S(1)} %pad_maximum_fusion.4, bf16[4,8192,512]{2,1,0:T(8,128)(2,1)} %refs_0_.1, f32[4096]{0:T(1024)S(1)} %bitcast.249), kind=kOutput, calls=%fused_computation.5 | convolution fusion | flops 1075838976 | bytes 12861440 | tf_op jit(solution)/shard_map/dot_general | solution.py:156
  174.1 8.3 %collective-permute-done.34 = f32[256,256]{1,0:T(8,128)S(1)} collective-permute-done((f32[256,256]{1,0:T(8,128)S(1)}, f32[256,256]{1,0:T(8,128)S(1)}, u32[]{:S(2)}, u32[]{:S(2)}) %collective-permute-start.34) | collective-permute-done | bytes 262176 | tf_op jit(solution)/shard_map/ppermute | solution.py:22
  182.9 2.1 collective-permute-start.35
  185.0 3.1 %fusion.1 = f32[4096,256]{1,0:T(8,128)S(1)} fusion(f32[4096,256]{1,0:T(8,128)S(1)} %copy-done.4, bf16[512,256]{1,0:T(8,128)(2,1)S(1)} %pad_maximum_fusion.4, bf16[4,8192,512]{2,1,0:T(8,128)(2,1)} %refs_0_.1, f32[4096]{0:T(1024)S(1)} %bitcast.248), kind=kOutput, calls=%fused_computation.2 | convolution fusion | flops 1075838976 | bytes 12861440 | tf_op jit(solution)/shard_map/dot_general | solution.py:156
  188.0 7.0 %collective-permute-done.36 = f32[256,256]{1,0:T(8,128)S(1)} collective-permute-done((f32[256,256]{1,0:T(8,128)S(1)}, f32[256,256]{1,0:T(8,128)S(1)}, u32[]{:S(2)}, u32[]{:S(2)}) %collective-permute-start.36) | collective-permute-done | bytes 262176 | tf_op jit(solution)/shard_map/ppermute | solution.py:22
  195.1 2.3 collective-permute-done.35
  206.6 1.6 collective-permute-start.44
  208.2 10.1 %collective-permute-done.45 = f32[512,256]{1,0:T(8,128)S(1)} collective-permute-done((f32[512,256]{1,0:T(8,128)S(1)}, f32[512,256]{1,0:T(8,128)S(1)}, u32[]{:S(2)}, u32[]{:S(2)}) %collective-permute-start.45) | collective-permute-done | bytes 524320 | tf_op jit(solution)/shard_map/ppermute | solution.py:22
  219.0 11.0 %collective-permute-done.42 = f32[512,256]{1,0:T(8,128)S(1)} collective-permute-done((f32[512,256]{1,0:T(8,128)S(1)}, f32[512,256]{1,0:T(8,128)S(1)}, u32[]{:S(2)}, u32[]{:S(2)}) %collective-permute-start.42) | collective-permute-done | bytes 524320 | tf_op jit(solution)/shard_map/ppermute | solution.py:22
  230.1 1.6 collective-permute-start.43
  232.3 7.7 %collective-permute-done.46 = f32[512,256]{1,0:T(8,128)S(1)} collective-permute-done((f32[512,256]{1,0:T(8,128)S(1)}, f32[512,256]{1,0:T(8,128)S(1)}, u32[]{:S(2)}, u32[]{:S(2)}) %collective-permute-start.46) | collective-permute-done | bytes 524320 | tf_op jit(solution)/shard_map/ppermute | solution.py:22
  240.0 1.6 collective-permute-done.43
  (203 shorter events, 52.4 us)
Async XLA Ops:
  2.3 17.3 %collective-permute-start.1 = (f32[256,256]{1,0:T(8,128)S(1)}, f32[256,256]{1,0:T(8,128)S(1)}, u32[]{:S(2)}, u32[]{:S(2)}) collective-permute-start(f32[256,256]{1,0:T(8,128)S(1)} %fusion.68), channel_id=1, source_target_pairs={{0,16},{8,24},{16,0},{24,8},{1,17},{9,25},{17,1},{25,9},{2,18},{10... | collective-permute-start | bytes 786440 | tf_op jit(solution)/shard_map/ppermute | solution.py:22
  8.1 12.3 %collective-permute-start = (f32[256,256]{1,0:T(8,128)S(1)}, f32[256,256]{1,0:T(8,128)S(1)}, u32[]{:S(2)}, u32[]{:S(2)}) collective-permute-start(f32[256,256]{1,0:T(8,128)S(1)} %fusion.70), channel_id=1, source_target_pairs={{0,8},{8,0},{16,24},{24,16},{1,9},{9,1},{17,25},{25,17},{2,10},{10... | collective-permute-start | bytes 786440 | tf_op jit(solution)/shard_map/ppermute | solution.py:22
  20.5 12.3 %collective-permute-start.3 = (f32[256,256]{1,0:T(8,128)S(1)}, f32[256,256]{1,0:T(8,128)S(1)}, u32[]{:S(2)}, u32[]{:S(2)}) collective-permute-start(f32[256,256]{1,0:T(8,128)S(1)} %add.325), channel_id=1, source_target_pairs={{0,8},{8,0},{16,24},{24,16},{1,9},{9,1},{17,25},{25,17},{2,10},{10... | collective-permute-start | bytes 786440 | tf_op jit(solution)/shard_map/ppermute | solution.py:22
  20.5 14.0 %collective-permute-start.2 = (f32[256,256]{1,0:T(8,128)S(1)}, f32[256,256]{1,0:T(8,128)S(1)}, u32[]{:S(2)}, u32[]{:S(2)}) collective-permute-start(f32[256,256]{1,0:T(8,128)S(1)} %add.324), channel_id=1, source_target_pairs={{0,16},{8,24},{16,0},{24,8},{1,17},{9,25},{17,1},{25,9},{2,18},{10... | collective-permute-start | bytes 786440 | tf_op jit(solution)/shard_map/ppermute | solution.py:22
  36.0 2.0 collective-permute-start.4
  38.6 8.8 %collective-permute-start.5 = (f32[256,256]{1,0:T(8,128)S(1)}, f32[256,256]{1,0:T(8,128)S(1)}, u32[]{:S(2)}, u32[]{:S(2)}) collective-permute-start(f32[256,256]{1,0:T(8,128)S(1)} %get-tuple-element.161), channel_id=1, source_target_pairs={{0,2},{1,3},{2,0},{3,1},{4,6},{5,7},{6,4},{7,5},{8,10},{9,11},{10,... | collective-permute-start | bytes 786440 | tf_op jit(solution)/shard_map/ppermute | solution.py:22
  40.1 8.4 %collective-permute-start.7 = (f32[256,256]{1,0:T(8,128)S(1)}, f32[256,256]{1,0:T(8,128)S(1)}, u32[]{:S(2)}, u32[]{:S(2)}) collective-permute-start(f32[256,256]{1,0:T(8,128)S(1)} %get-tuple-element.162), channel_id=1, source_target_pairs={{0,4},{1,5},{2,6},{3,7},{4,0},{5,1},{6,2},{7,3},{8,12},{9,13},{10,... | collective-permute-start | bytes 786440 | tf_op jit(solution)/shard_map/ppermute | solution.py:22
  48.6 7.7 %collective-permute-start.6 = (f32[256,256]{1,0:T(8,128)S(1)}, f32[256,256]{1,0:T(8,128)S(1)}, u32[]{:S(2)}, u32[]{:S(2)}) collective-permute-start(f32[256,256]{1,0:T(8,128)S(1)} %get-tuple-element.159), channel_id=1, source_target_pairs={{0,4},{1,5},{2,6},{3,7},{4,0},{5,1},{6,2},{7,3},{8,12},{9,13},{10,... | collective-permute-start | bytes 786440 | tf_op jit(solution)/shard_map/ppermute | solution.py:22
  50.2 7.3 %collective-permute-start.8 = (f32[256,256]{1,0:T(8,128)S(1)}, f32[256,256]{1,0:T(8,128)S(1)}, u32[]{:S(2)}, u32[]{:S(2)}) collective-permute-start(f32[256,256]{1,0:T(8,128)S(1)} %get-tuple-element.160), channel_id=1, source_target_pairs={{0,2},{1,3},{2,0},{3,1},{4,6},{5,7},{6,4},{7,5},{8,10},{9,11},{10,... | collective-permute-start | bytes 786440 | tf_op jit(solution)/shard_map/ppermute | solution.py:22
  57.6 1.6 collective-permute-start.10
  57.7 1.9 collective-permute-start.9
  60.7 14.8 %collective-permute-start.12 = (f32[256,256]{1,0:T(8,128)S(1)}, f32[256,256]{1,0:T(8,128)S(1)}, u32[]{:S(2)}, u32[]{:S(2)}) collective-permute-start(f32[256,256]{1,0:T(8,128)S(1)} %fusion.52), channel_id=1, source_target_pairs={{0,16},{8,24},{16,0},{24,8},{1,17},{9,25},{17,1},{25,9},{2,18},{10... | collective-permute-start | bytes 786440 | tf_op jit(solution)/shard_map/ppermute | solution.py:22
  61.0 15.0 %collective-permute-start.11 = (f32[256,256]{1,0:T(8,128)S(1)}, f32[256,256]{1,0:T(8,128)S(1)}, u32[]{:S(2)}, u32[]{:S(2)}) collective-permute-start(f32[256,256]{1,0:T(8,128)S(1)} %fusion.54), channel_id=1, source_target_pairs={{0,8},{8,0},{16,24},{24,16},{1,9},{9,1},{17,25},{25,17},{2,10},{10... | collective-permute-start | bytes 786440 | tf_op jit(solution)/shard_map/ppermute | solution.py:22
  76.0 12.2 %collective-permute-start.14 = (f32[256,256]{1,0:T(8,128)S(1)}, f32[256,256]{1,0:T(8,128)S(1)}, u32[]{:S(2)}, u32[]{:S(2)}) collective-permute-start(f32[256,256]{1,0:T(8,128)S(1)} %add.350), channel_id=1, source_target_pairs={{0,8},{8,0},{16,24},{24,16},{1,9},{9,1},{17,25},{25,17},{2,10},{10... | collective-permute-start | bytes 786440 | tf_op jit(solution)/shard_map/ppermute | solution.py:22
  76.1 14.5 %collective-permute-start.13 = (f32[256,256]{1,0:T(8,128)S(1)}, f32[256,256]{1,0:T(8,128)S(1)}, u32[]{:S(2)}, u32[]{:S(2)}) collective-permute-start(f32[256,256]{1,0:T(8,128)S(1)} %add.346), channel_id=1, source_target_pairs={{0,16},{8,24},{16,0},{24,8},{1,17},{9,25},{17,1},{25,9},{2,18},{10... | collective-permute-start | bytes 786440 | tf_op jit(solution)/shard_map/ppermute | solution.py:22
  90.9 2.0 collective-permute-start.15
  93.2 8.4 %collective-permute-start.16 = (f32[256,256]{1,0:T(8,128)S(1)}, f32[256,256]{1,0:T(8,128)S(1)}, u32[]{:S(2)}, u32[]{:S(2)}) collective-permute-start(f32[256,256]{1,0:T(8,128)S(1)} %get-tuple-element.157), channel_id=1, source_target_pairs={{0,2},{1,3},{2,0},{3,1},{4,6},{5,7},{6,4},{7,5},{8,10},{9,11},{10,... | collective-permute-start | bytes 786440 | tf_op jit(solution)/shard_map/ppermute | solution.py:22
  93.9 8.1 %collective-permute-start.18 = (f32[256,256]{1,0:T(8,128)S(1)}, f32[256,256]{1,0:T(8,128)S(1)}, u32[]{:S(2)}, u32[]{:S(2)}) collective-permute-start(f32[256,256]{1,0:T(8,128)S(1)} %get-tuple-element.158), channel_id=1, source_target_pairs={{0,4},{1,5},{2,6},{3,7},{4,0},{5,1},{6,2},{7,3},{8,12},{9,13},{10,... | collective-permute-start | bytes 786440 | tf_op jit(solution)/shard_map/ppermute | solution.py:22
  102.1 7.3 %collective-permute-start.17 = (f32[256,256]{1,0:T(8,128)S(1)}, f32[256,256]{1,0:T(8,128)S(1)}, u32[]{:S(2)}, u32[]{:S(2)}) collective-permute-start(f32[256,256]{1,0:T(8,128)S(1)} %get-tuple-element.155), channel_id=1, source_target_pairs={{0,4},{1,5},{2,6},{3,7},{4,0},{5,1},{6,2},{7,3},{8,12},{9,13},{10,... | collective-permute-start | bytes 786440 | tf_op jit(solution)/shard_map/ppermute | solution.py:22
  102.6 6.9 %collective-permute-start.19 = (f32[256,256]{1,0:T(8,128)S(1)}, f32[256,256]{1,0:T(8,128)S(1)}, u32[]{:S(2)}, u32[]{:S(2)}) collective-permute-start(f32[256,256]{1,0:T(8,128)S(1)} %get-tuple-element.156), channel_id=1, source_target_pairs={{0,2},{1,3},{2,0},{3,1},{4,6},{5,7},{6,4},{7,5},{8,10},{9,11},{10,... | collective-permute-start | bytes 786440 | tf_op jit(solution)/shard_map/ppermute | solution.py:22
  109.7 1.6 collective-permute-start.20
  109.8 1.9 collective-permute-start.21
  112.7 13.8 %collective-permute-start.23 = (f32[256,256]{1,0:T(8,128)S(1)}, f32[256,256]{1,0:T(8,128)S(1)}, u32[]{:S(2)}, u32[]{:S(2)}) collective-permute-start(f32[256,256]{1,0:T(8,128)S(1)} %fusion.48), channel_id=1, source_target_pairs={{0,16},{8,24},{16,0},{24,8},{1,17},{9,25},{17,1},{25,9},{2,18},{10... | collective-permute-start | bytes 786440 | tf_op jit(solution)/shard_map/ppermute | solution.py:22
  113.3 13.8 %collective-permute-start.22 = (f32[256,256]{1,0:T(8,128)S(1)}, f32[256,256]{1,0:T(8,128)S(1)}, u32[]{:S(2)}, u32[]{:S(2)}) collective-permute-start(f32[256,256]{1,0:T(8,128)S(1)} %fusion.50), channel_id=1, source_target_pairs={{0,8},{8,0},{16,24},{24,16},{1,9},{9,1},{17,25},{25,17},{2,10},{10... | collective-permute-start | bytes 786440 | tf_op jit(solution)/shard_map/ppermute | solution.py:22
  127.1 13.2 %collective-permute-start.25 = (f32[256,256]{1,0:T(8,128)S(1)}, f32[256,256]{1,0:T(8,128)S(1)}, u32[]{:S(2)}, u32[]{:S(2)}) collective-permute-start(f32[256,256]{1,0:T(8,128)S(1)} %add.367), channel_id=1, source_target_pairs={{0,8},{8,0},{16,24},{24,16},{1,9},{9,1},{17,25},{25,17},{2,10},{10... | collective-permute-start | bytes 786440 | tf_op jit(solution)/shard_map/ppermute | solution.py:22
  127.2 14.3 %collective-permute-start.24 = (f32[256,256]{1,0:T(8,128)S(1)}, f32[256,256]{1,0:T(8,128)S(1)}, u32[]{:S(2)}, u32[]{:S(2)}) collective-permute-start(f32[256,256]{1,0:T(8,128)S(1)} %add.363), channel_id=1, source_target_pairs={{0,16},{8,24},{16,0},{24,8},{1,17},{9,25},{17,1},{25,9},{2,18},{10... | collective-permute-start | bytes 786440 | tf_op jit(solution)/shard_map/ppermute | solution.py:22
  141.9 2.0 collective-permute-start.26
  145.0 8.7 %collective-permute-start.27 = (f32[256,256]{1,0:T(8,128)}, f32[256,256]{1,0:T(8,128)}, u32[]{:S(2)}, u32[]{:S(2)}) collective-permute-start(f32[256,256]{1,0:T(8,128)} %get-tuple-element.153), channel_id=1, source_target_pairs={{0,2},{1,3},{2,0},{3,1},{4,6},{5,7},{6,4},{7,5},{8,10},{9,11},{10,... | collective-permute-start | bytes 786440 | tf_op jit(solution)/shard_map/ppermute | solution.py:22
  146.4 8.4 %collective-permute-start.29 = (f32[256,256]{1,0:T(8,128)}, f32[256,256]{1,0:T(8,128)}, u32[]{:S(2)}, u32[]{:S(2)}) collective-permute-start(f32[256,256]{1,0:T(8,128)} %get-tuple-element.154), channel_id=1, source_target_pairs={{0,4},{1,5},{2,6},{3,7},{4,0},{5,1},{6,2},{7,3},{8,12},{9,13},{10,... | collective-permute-start | bytes 786440 | tf_op jit(solution)/shard_map/ppermute | solution.py:22
  152.1 14.6 %copy-start.10 = (bf16[512,512]{1,0:T(8,128)(2,1)S(1)}, bf16[512,512]{1,0:T(8,128)(2,1)}, u32[]{:S(2)}) copy-start(bf16[512,512]{1,0:T(8,128)(2,1)} %get-tuple-element.126) | copy-start | bytes 1572868
  155.9 7.3 %collective-permute-start.28 = (f32[256,256]{1,0:T(8,128)S(1)}, f32[256,256]{1,0:T(8,128)S(1)}, u32[]{:S(2)}, u32[]{:S(2)}) collective-permute-start(f32[256,256]{1,0:T(8,128)S(1)} %get-tuple-element.151), channel_id=1, source_target_pairs={{0,4},{1,5},{2,6},{3,7},{4,0},{5,1},{6,2},{7,3},{8,12},{9,13},{10,... | collective-permute-start | bytes 786440 | tf_op jit(solution)/shard_map/ppermute | solution.py:22
  157.5 6.9 %collective-permute-start.30 = (f32[256,256]{1,0:T(8,128)S(1)}, f32[256,256]{1,0:T(8,128)S(1)}, u32[]{:S(2)}, u32[]{:S(2)}) collective-permute-start(f32[256,256]{1,0:T(8,128)S(1)} %get-tuple-element.152), channel_id=1, source_target_pairs={{0,2},{1,3},{2,0},{3,1},{4,6},{5,7},{6,4},{7,5},{8,10},{9,11},{10,... | collective-permute-start | bytes 786440 | tf_op jit(solution)/shard_map/ppermute | solution.py:22
  164.5 1.6 collective-permute-start.31
  164.6 1.9 collective-permute-start.32
  167.6 14.8 %collective-permute-start.34 = (f32[256,256]{1,0:T(8,128)S(1)}, f32[256,256]{1,0:T(8,128)S(1)}, u32[]{:S(2)}, u32[]{:S(2)}) collective-permute-start(f32[256,256]{1,0:T(8,128)S(1)} %fusion.44), channel_id=1, source_target_pairs={{0,16},{8,24},{16,0},{24,8},{1,17},{9,25},{17,1},{25,9},{2,18},{10... | collective-permute-start | bytes 786440 | tf_op jit(solution)/shard_map/ppermute | solution.py:22
  168.1 14.7 %collective-permute-start.33 = (f32[256,256]{1,0:T(8,128)S(1)}, f32[256,256]{1,0:T(8,128)S(1)}, u32[]{:S(2)}, u32[]{:S(2)}) collective-permute-start(f32[256,256]{1,0:T(8,128)S(1)} %fusion.46), channel_id=1, source_target_pairs={{0,8},{8,0},{16,24},{24,16},{1,9},{9,1},{17,25},{25,17},{2,10},{10... | collective-permute-start | bytes 786440 | tf_op jit(solution)/shard_map/ppermute | solution.py:22
  182.8 12.2 %collective-permute-start.36 = (f32[256,256]{1,0:T(8,128)S(1)}, f32[256,256]{1,0:T(8,128)S(1)}, u32[]{:S(2)}, u32[]{:S(2)}) collective-permute-start(f32[256,256]{1,0:T(8,128)S(1)} %add.388), channel_id=1, source_target_pairs={{0,8},{8,0},{16,24},{24,16},{1,9},{9,1},{17,25},{25,17},{2,10},{10... | collective-permute-start | bytes 786440 | tf_op jit(solution)/shard_map/ppermute | solution.py:22
  182.9 14.5 %collective-permute-start.35 = (f32[256,256]{1,0:T(8,128)S(1)}, f32[256,256]{1,0:T(8,128)S(1)}, u32[]{:S(2)}, u32[]{:S(2)}) collective-permute-start(f32[256,256]{1,0:T(8,128)S(1)} %add.384), channel_id=1, source_target_pairs={{0,16},{8,24},{16,0},{24,8},{1,17},{9,25},{17,1},{25,9},{2,18},{10... | collective-permute-start | bytes 786440 | tf_op jit(solution)/shard_map/ppermute | solution.py:22
  197.9 4.2 %collective-permute-start.38 = (f32[1024,256]{1,0:T(8,128)S(1)}, f32[1024,256]{1,0:T(8,128)S(1)}, u32[]{:S(2)}, u32[]{:S(2)}) collective-permute-start(f32[1024,256]{1,0:T(8,128)S(1)} %fusion.28), channel_id=1, source_target_pairs={{0,1},{1,0},{2,3},{3,2},{4,5},{5,4},{6,7},{7,6},{8,9},{9,8},{10,11... | collective-permute-start | bytes 3145736 | tf_op jit(solution)/shard_map/ppermute | solution.py:22
  198.5 4.3 %collective-permute-start.41 = (f32[1024,256]{1,0:T(8,128)S(1)}, f32[1024,256]{1,0:T(8,128)S(1)}, u32[]{:S(2)}, u32[]{:S(2)}) collective-permute-start(f32[1024,256]{1,0:T(8,128)S(1)} %fusion.22), channel_id=1, source_target_pairs={{0,1},{1,0},{2,3},{3,2},{4,5},{5,4},{6,7},{7,6},{8,9},{9,8},{10,11... | collective-permute-start | bytes 3145736 | tf_op jit(solution)/shard_map/ppermute | solution.py:22
  199.5 32.2 %collective-permute-start.37 = (f32[1024,256]{1,0:T(8,128)S(1)}, f32[1024,256]{1,0:T(8,128)S(1)}, u32[]{:S(2)}, u32[]{:S(2)}) collective-permute-start(f32[1024,256]{1,0:T(8,128)S(1)} %fusion.31), channel_id=1, source_target_pairs={{0,1},{1,0},{2,3},{3,2},{4,5},{5,4},{6,7},{7,6},{8,9},{9,8},{10,11... | collective-permute-start | bytes 3145736 | tf_op jit(solution)/shard_map/ppermute | solution.py:22
  200.1 5.9 %collective-permute-start.40 = (f32[1024,256]{1,0:T(8,128)S(1)}, f32[1024,256]{1,0:T(8,128)S(1)}, u32[]{:S(2)}, u32[]{:S(2)}) collective-permute-start(f32[1024,256]{1,0:T(8,128)S(1)} %fusion.25), channel_id=1, source_target_pairs={{0,1},{1,0},{2,3},{3,2},{4,5},{5,4},{6,7},{7,6},{8,9},{9,8},{10,11... | collective-permute-start | bytes 3145736 | tf_op jit(solution)/shard_map/ppermute | solution.py:22
  203.4 14.9 %collective-permute-start.45 = (f32[512,256]{1,0:T(8,128)S(1)}, f32[512,256]{1,0:T(8,128)S(1)}, u32[]{:S(2)}, u32[]{:S(2)}) collective-permute-start(f32[512,256]{1,0:T(8,128)S(1)} %get-tuple-element.107), channel_id=1, source_target_pairs={{0,4},{1,5},{2,6},{3,7},{4,0},{5,1},{6,2},{7,3},{8,12},{9,13},{10,... | collective-permute-start | bytes 1572872 | tf_op jit(solution)/shard_map/ppermute | solution.py:22
  204.0 28.3 %collective-permute-start.39 = (f32[512,256]{1,0:T(8,128)S(1)}, f32[512,256]{1,0:T(8,128)S(1)}, u32[]{:S(2)}, u32[]{:S(2)}) collective-permute-start(f32[512,256]{1,0:T(8,128)S(1)} %get-tuple-element.93), channel_id=1, source_target_pairs={{0,2},{1,3},{2,0},{3,1},{4,6},{5,7},{6,4},{7,5},{8,10},{9,11},{10,... | collective-permute-start | bytes 1572872 | tf_op jit(solution)/shard_map/ppermute | solution.py:22
  204.6 25.5 %collective-permute-start.42 = (f32[512,256]{1,0:T(8,128)S(1)}, f32[512,256]{1,0:T(8,128)S(1)}, u32[]{:S(2)}, u32[]{:S(2)}) collective-permute-start(f32[512,256]{1,0:T(8,128)S(1)} %get-tuple-element.103), channel_id=1, source_target_pairs={{0,2},{1,3},{2,0},{3,1},{4,6},{5,7},{6,4},{7,5},{8,10},{9,11},{10,... | collective-permute-start | bytes 1572872 | tf_op jit(solution)/shard_map/ppermute | solution.py:22
  206.6 25.7 %collective-permute-start.44 = (f32[512,256]{1,0:T(8,128)S(1)}, f32[512,256]{1,0:T(8,128)S(1)}, u32[]{:S(2)}, u32[]{:S(2)}) collective-permute-start(f32[512,256]{1,0:T(8,128)S(1)} %get-tuple-element.105), channel_id=1, source_target_pairs={{0,4},{1,5},{2,6},{3,7},{4,0},{5,1},{6,2},{7,3},{8,12},{9,13},{10,... | collective-permute-start | bytes 1572872 | tf_op jit(solution)/shard_map/ppermute | solution.py:22
  218.3 21.7 %collective-permute-start.46 = (f32[512,256]{1,0:T(8,128)S(1)}, f32[512,256]{1,0:T(8,128)S(1)}, u32[]{:S(2)}, u32[]{:S(2)}) collective-permute-start(f32[512,256]{1,0:T(8,128)S(1)} %add.425), channel_id=1, source_target_pairs={{0,2},{1,3},{2,0},{3,1},{4,6},{5,7},{6,4},{7,5},{8,10},{9,11},{10,... | collective-permute-start | bytes 1572872 | tf_op jit(solution)/shard_map/ppermute | solution.py:22
  230.1 11.5 %collective-permute-start.43 = (f32[512,256]{1,0:T(8,128)S(1)}, f32[512,256]{1,0:T(8,128)S(1)}, u32[]{:S(2)}, u32[]{:S(2)}) collective-permute-start(f32[512,256]{1,0:T(8,128)S(1)} %add.422), channel_id=1, source_target_pairs={{0,4},{1,5},{2,6},{3,7},{4,0},{5,1},{6,2},{7,3},{8,12},{9,13},{10,... | collective-permute-start | bytes 1572872 | tf_op jit(solution)/shard_map/ppermute | solution.py:22
  (17 other events, 131.0 us)

commit v4 on v3

--- a/solution.py
+++ b/solution.py
@@ -44,6 +44,10 @@
             new = lax.optimization_barrier((*new, queue.pop(0)(parts[-1])))[: len(new)]
         parts = list(new)
     return parts
+
+
+def exchange(parts, axis, masks, step):
+    return [swap(p, axis, masks[(step + j) % len(masks)]) for j, p in enumerate(parts)]
 
 
 def sum_row(parts, queue):
@@ -169,13 +173,35 @@
         store["scale"] = lax.optimization_barrier(tuple(scales))
         return store["scale"][0]
 
-    def tail(q, solved):
+    def tail(q, piece, solved):
+        cols = solved.shape[1]
         term = jnp.dot(store["last"][q], solved, preferred_element_type=F32)
-        scale = store["scale"][q]
         at = ((me ^ q) % (n // 2)) * own
-        parts = [lax.dynamic_slice_in_dim(e, at, own, 0) for e in early]
+        parts = [lax.dynamic_slice(e, (at, piece * cols), (own, cols)) for e in early]
         base = jnp.where((me ^ q) < n // 2, parts[0], parts[1])
-        return row_major(base + scale[:, None] * term)
+        return row_major(base + store["scale"][q][:, None] * term)
+
+    def tail_pairs(piece, solved):
+        sent = {q: swap(tail(q, piece, solved), "col", 1) for q in range(n - 1, 0, -2)}
+        sums = {q: halves(tail(q, piece, solved) + sent[q + 1]) for q in range(n - 2, -1, -2)}
+        return {q: lax.optimization_barrier(tuple(x)) for q, x in sums.items()}
+
+    def tail_rest(sums):
+        return [scatter({q: x[j] for q, x in sums.items()}, j, bits) for j in range(2)]
+
+    def inverse_dots(target, right):
+        parts = []
+        for piece in range(2):
+            total = None
+            for side in (1, 0):
+                inverse = store["dinv"][side][target]
+                height, width = inverse.shape[0] // 2, inverse.shape[1] // 2
+                for k in range(2):
+                    block = inverse[piece * height : (piece + 1) * height, k * width : (k + 1) * width]
+                    product = jnp.dot(block, right[side][k].astype(BF16), preferred_element_type=F32)
+                    total = product if total is None else total + product
+            parts.append(total)
+        return parts
 
     def update(target, side, solved):
         total = None
@@ -195,32 +221,51 @@
             home = sum_parts(halves(update(target, 1, solved) + away), "col", col_masks(), [])
             back = [swap(h, "col", 1) for h in home]
             right = [[r - b for r, b in zip(rhs[target][0], back)], [r - h for r, h in zip(rhs[target][1], home)]]
-        parts = []
+        if target == PANELS - 1:
+            break
         if target == 0:
             reduced = rhs_window[0].astype(BF16)
             parts = [jnp.dot(d, reduced, preferred_element_type=F32) for d in halves(dinv[0])]
-        for piece in range(2 if target else 0):
-            total = None
-            for side in (1, 0):
-                inverse = store["dinv"][side][target]
-                height, width = inverse.shape[0] // 2, inverse.shape[1] // 2
-                for k in range(2):
-                    block = inverse[piece * height : (piece + 1) * height, k * width : (k + 1) * width]
-                    product = jnp.dot(block, right[side][k].astype(BF16), preferred_element_type=F32)
-                    total = product if total is None else total + product
-            parts.append(total)
+        else:
+            parts = inverse_dots(target, right)
         parts = sum_row(parts, queue)
         while queue:
             queue.pop(0)(parts[0])
         solutions.append(jnp.concatenate(parts, axis=0))
         solved.append(jnp.concatenate([p.astype(BF16) for p in parts], axis=0))
-        if target < PANELS - 1:
-            queue = [functools.partial(early_step, target, top, solved[-1]) for top in range(2)]
-    sent = {q: swap(tail(q, solved[-1]), "col", 1) for q in range(n - 1, 0, -2)}
-    sums = {q: halves(tail(q, solved[-1]) + sent[q + 1]) for q in range(n - 2, -1, -2)}
-    sums = {q: lax.optimization_barrier(tuple(x)) for q, x in sums.items()}
-    done = [scatter({q: x[j] for q, x in sums.items()}, j, bits) for j in range(2)]
-    below = [r - d for r, d in zip(halves(rhs_below), done)]
+        queue = [functools.partial(early_step, target, top, solved[-1]) for top in range(2)]
+    cols = rhs_window.shape[-1] // 2
+    first, second = [
+        inverse_dots(target, [[r[:, k * cols : (k + 1) * cols] for r in side] for side in right]) for k in range(2)
+    ]
+
+    def joined(parts):
+        return jnp.concatenate([p.astype(BF16) for p in parts], axis=0)
+
+    if lax.axis_size("row") == 4:
+        masks = (1, 2)
+        got = exchange(first, "row", masks, 0)
+        done = queue[0](first[-1])
+        first = lax.optimization_barrier((*[p + g for p, g in zip(first, got)], done))[:2]
+        got = exchange(first, "row", masks, 1)
+        second = lax.optimization_barrier((*second, *first))[:2]
+        other = exchange(second, "row", masks, 0)
+        done = queue[1](second[-1])
+        first = lax.optimization_barrier((*[p + g for p, g in zip(first, got)], done))[:2]
+        second = lax.optimization_barrier((*[p + g for p, g in zip(second, other)], *first))[:2]
+        got = exchange(second, "row", masks, 1)
+        sums = tail_pairs(0, after(joined(first), *second))
+        ready = [x for q in sums if q for x in sums[q]]
+        second = lax.optimization_barrier((*[p + g for p, g in zip(second, got)], *ready))[:2]
+    else:
+        first = sum_row(first, queue)
+        second = sum_row(second, queue)
+        sums = tail_pairs(0, joined(first))
+    later = tail_pairs(1, joined(second))
+    done = [tail_rest(sums), tail_rest(later)]
+    solutions = [after(x, later[n - 2][0]) for x in solutions]
+    solutions.append(jnp.concatenate([jnp.concatenate(p, axis=1) for p in zip(first, second)], axis=0))
+    below = [r - jnp.concatenate(d, axis=1) for r, d in zip(halves(rhs_below), zip(*done))]
     return (jnp.stack(solutions), jnp.concatenate(below, axis=0))
 
 

time: 243 us -> 243 us (level)
  waiting for transfers between devices: 130 us -> 114 us
  starting transfers between devices: 47.4 us -> 57.5 us
  matrix products: 39.9 us -> 44.6 us
    ppermute x47 -> x61, waiting for transfers between devices: 130 us -> 114 us  [swap(): return lax.ppermute(x, axis, [(i, i ^ mask) for i in range(n)])]
    ppermute x47 -> x61, starting transfers between devices: 47.4 us -> 57.5 us  [swap(): return lax.ppermute(x, axis, [(i, i ^ mask) for i in range(n)])]
    dot_general x8 -> x16, matrix products: 3.89 us -> 7.16 us  [tail(): term = jnp.dot(store['last'][q], solved, preferred_element_type=F32)]
    dot_general x24 -> x32, matrix products: 4.44 us -> 5.66 us  [inverse_dots(): jnp.dot(block, right[side][k].astype(BF16), preferred_element_type=F32)]
  transfers between devices with their start and end apart: 47 -> 61, of which waited for: 40 -> 43; matrix products, arithmetic and copies ran while one was open for 16% -> 18% of each run, Pallas kernels for 4% -> 4%
where the time goes in v4:
time: 243 us; the launch traced here: 242 us
  waiting for transfers between devices  114 us (47%)
  starting transfers between devices  57.5 us (24%)
  matrix products  44.6 us (18%)
  Pallas kernels  9.81 us (4%)
  local copies, waits for them, and re-layouts  7.83 us (3%)
  other arithmetic  6.42 us (3%)
    ppermute x61, waiting for transfers between devices, swap(): return lax.ppermute(x, axis, [(i, i ^ mask) for i in range(n)])  114 us
    ppermute x61, starting transfers between devices, swap(): return lax.ppermute(x, axis, [(i, i ^ mask) for i in range(n)])  57.5 us
    dot_general x6, matrix products, early_step(): term = jnp.dot(factor, after(solved, dep), preferred_element_type=F32)  23.7 us
    dot_general x16, matrix products, tail(): term = jnp.dot(store['last'][q], solved, preferred_element_type=F32)  7.16 us
    pallas_call x1, Pallas kernels, stage(): pl.pallas_call(stage_kernel, out_shape=[jax.ShapeDtypeStruct(shape, BF16)...  5.79 us
    dot_general x32, matrix products, inverse_dots(): jnp.dot(block, right[side][k].astype(BF16), preferred_element_type=F32)  5.66 us
  transfers between devices with their start and end apart: 61, of which 43 were waited for; matrix products, arithmetic and copies ran while one was open for 18% of the time, Pallas kernels for 4%

profile of v4, /device:TPU:0, one launch (start us, length us, event | category | flops | bytes accessed | tf_op | source)
XLA Modules:
  0.0 242.5 jit_solution(14829272233989940957)
XLA Ops:
  0.6 1.7 fusion.80
  2.3 4.1 %collective-permute-start.1 = (f32[256,256]{1,0:T(8,128)S(1)}, f32[256,256]{1,0:T(8,128)S(1)}, u32[]{:S(2)}, u32[]{:S(2)}) collective-permute-start(f32[256,256]{1,0:T(8,128)S(1)} %fusion.80), channel_id=1, source_target_pairs={{0,16},{8,24},{16,0},{24,8},{1,17},{9,25},{17,1},{25,9},{2,18},{10... | collective-permute-start | bytes 786440 | tf_op jit(solution)/shard_map/ppermute | solution.py:22
  6.4 1.7 fusion.82
  8.1 1.6 collective-permute-start
  11.4 5.8 %stage.1 = (bf16[6,512,512]{2,1,0:T(8,128)(2,1)S(1)}, bf16[6,512,512]{2,1,0:T(8,128)(2,1)}, bf16[4,512,512]{2,1,0:T(8,128)(2,1)S(1)}, bf16[4,512,512]{2,1,0:T(8,128)(2,1)S(1)}) custom-call(s32[1]{0:T(128)} %bitcast.3.sel, bf16[6,1024,512]{2,1,0:T(8,128)(2,1)} %c_ref.1, bf16[4,512,1024]{2,1,0:T(8,128)(2,1)} %d_ref.1), custom_call_target="tpu_custom_call" | custom-call | tf_op jit(solution)/shard_map/stage/pallas_call | solution.py:88
  18.5 1.6 copy-done.2
  20.8 2.7 %collective-permute-start.2 = (f32[256,256]{1,0:T(8,128)S(1)}, f32[256,256]{1,0:T(8,128)S(1)}, u32[]{:S(2)}, u32[]{:S(2)}) collective-permute-start(f32[256,256]{1,0:T(8,128)S(1)} %add.432), channel_id=1, source_target_pairs={{0,16},{8,24},{16,0},{24,8},{1,17},{9,25},{17,1},{25,9},{2,18},{10... | collective-permute-start | bytes 786440 | tf_op jit(solution)/shard_map/ppermute | solution.py:22
  24.5 8.7 %collective-permute-done.3 = f32[256,256]{1,0:T(8,128)S(1)} collective-permute-done((f32[256,256]{1,0:T(8,128)S(1)}, f32[256,256]{1,0:T(8,128)S(1)}, u32[]{:S(2)}, u32[]{:S(2)}) %collective-permute-start.3) | collective-permute-done | bytes 262176 | tf_op jit(solution)/shard_map/ppermute | solution.py:22
  38.8 1.5 collective-permute-start.5
  42.0 5.6 %collective-permute-done.5 = f32[256,256]{1,0:T(8,128)S(1)} collective-permute-done((f32[256,256]{1,0:T(8,128)S(1)}, f32[256,256]{1,0:T(8,128)S(1)}, u32[]{:S(2)}, u32[]{:S(2)}) %collective-permute-start.5) | collective-permute-done | bytes 262176 | tf_op jit(solution)/shard_map/ppermute | solution.py:22
  48.8 1.6 collective-permute-start.6
  51.3 5.2 %collective-permute-done.6 = f32[256,256]{1,0:T(8,128)S(1)} collective-permute-done((f32[256,256]{1,0:T(8,128)S(1)}, f32[256,256]{1,0:T(8,128)S(1)}, u32[]{:S(2)}, u32[]{:S(2)}) %collective-permute-start.6) | collective-permute-done | bytes 262176 | tf_op jit(solution)/shard_map/ppermute | solution.py:22
  61.5 2.7 %collective-permute-start.11 = (f32[256,256]{1,0:T(8,128)S(1)}, f32[256,256]{1,0:T(8,128)S(1)}, u32[]{:S(2)}, u32[]{:S(2)}) collective-permute-start(f32[256,256]{1,0:T(8,128)S(1)} %fusion.60), channel_id=1, source_target_pairs={{0,8},{8,0},{16,24},{24,16},{1,9},{9,1},{17,25},{25,17},{2,10},{10... | collective-permute-start | bytes 786440 | tf_op jit(solution)/shard_map/ppermute | solution.py:22
  64.2 3.1 %fusion.9 = f32[4096,256]{1,0:T(8,128)S(1)} fusion(bf16[512,256]{1,0:T(8,128)(2,1)S(1)} %pad_maximum_fusion.5, bf16[4,8192,512]{2,1,0:T(8,128)(2,1)} %refs_0_.1, f32[4096]{0:T(1024)S(1)} %bitcast.262), kind=kOutput, calls=%fused_computation.15 | convolution fusion | flops 1074790400 | bytes 8667136 | tf_op jit(solution)/shard_map/dot_general | solution.py:160
  67.3 8.4 %collective-permute-done.12 = f32[256,256]{1,0:T(8,128)S(1)} collective-permute-done((f32[256,256]{1,0:T(8,128)S(1)}, f32[256,256]{1,0:T(8,128)S(1)}, u32[]{:S(2)}, u32[]{:S(2)}) %collective-permute-start.12) | collective-permute-done | bytes 262176 | tf_op jit(solution)/shard_map/ppermute | solution.py:22
  76.2 2.1 collective-permute-start.13
  78.3 3.0 %fusion.8 = f32[4096,256]{1,0:T(8,128)S(1)} fusion(bf16[512,256]{1,0:T(8,128)(2,1)S(1)} %pad_maximum_fusion.5, bf16[4,8192,512]{2,1,0:T(8,128)(2,1)} %refs_0_.1, f32[4096]{0:T(1024)S(1)} %bitcast.261), kind=kOutput, calls=%fused_computation.13 | convolution fusion | flops 1074790400 | bytes 8667136 | tf_op jit(solution)/shard_map/dot_general | solution.py:160
  81.4 7.1 %collective-permute-done.14 = f32[256,256]{1,0:T(8,128)S(1)} collective-permute-done((f32[256,256]{1,0:T(8,128)S(1)}, f32[256,256]{1,0:T(8,128)S(1)}, u32[]{:S(2)}, u32[]{:S(2)}) %collective-permute-start.14) | collective-permute-done | bytes 262176 | tf_op jit(solution)/shard_map/ppermute | solution.py:22
  88.5 2.2 collective-permute-done.13
  91.5 1.6 collective-permute-done.15
  95.0 6.9 %collective-permute-done.16 = f32[256,256]{1,0:T(8,128)S(1)} collective-permute-done((f32[256,256]{1,0:T(8,128)S(1)}, f32[256,256]{1,0:T(8,128)S(1)}, u32[]{:S(2)}, u32[]{:S(2)}) %collective-permute-start.16) | collective-permute-done | bytes 262176 | tf_op jit(solution)/shard_map/ppermute | solution.py:22
  104.6 5.0 %collective-permute-done.17 = f32[256,256]{1,0:T(8,128)S(1)} collective-permute-done((f32[256,256]{1,0:T(8,128)S(1)}, f32[256,256]{1,0:T(8,128)S(1)}, u32[]{:S(2)}, u32[]{:S(2)}) %collective-permute-start.17) | collective-permute-done | bytes 262176 | tf_op jit(solution)/shard_map/ppermute | solution.py:22
  113.4 1.8 collective-permute-start.22
  115.3 5.5 %fusion.7 = f32[4096,256]{1,0:T(8,128)} fusion(f32[4096,256]{1,0:T(8,128)S(1)} %fusion.9, bf16[512,256]{1,0:T(8,128)(2,1)S(1)} %pad_maximum_fusion.6, bf16[4,8192,512]{2,1,0:T(8,128)(2,1)} %refs_0_.1, f32[4096]{0:T(1024)S(1)} %bitcast.259), kind=kOutput, calls=%fused_computation.11 | convolution fusion | flops 1075838976 | bytes 12861440 | tf_op jit(solution)/shard_map/dot_general | solution.py:160
  120.8 6.0 %collective-permute-done.23 = f32[256,256]{1,0:T(8,128)S(1)} collective-permute-done((f32[256,256]{1,0:T(8,128)S(1)}, f32[256,256]{1,0:T(8,128)S(1)}, u32[]{:S(2)}, u32[]{:S(2)}) %collective-permute-start.23) | collective-permute-done | bytes 262176 | tf_op jit(solution)/shard_map/ppermute | solution.py:22
  127.4 2.8 %collective-permute-start.24 = (f32[256,256]{1,0:T(8,128)S(1)}, f32[256,256]{1,0:T(8,128)S(1)}, u32[]{:S(2)}, u32[]{:S(2)}) collective-permute-start(f32[256,256]{1,0:T(8,128)S(1)} %add.475), channel_id=1, source_target_pairs={{0,16},{8,24},{16,0},{24,8},{1,17},{9,25},{17,1},{25,9},{2,18},{10... | collective-permute-start | bytes 786440 | tf_op jit(solution)/shard_map/ppermute | solution.py:22
  130.2 5.5 %fusion.5 = f32[4096,256]{1,0:T(8,128)} fusion(f32[4096,256]{1,0:T(8,128)S(1)} %fusion.8, bf16[512,256]{1,0:T(8,128)(2,1)S(1)} %pad_maximum_fusion.6, bf16[4,8192,512]{2,1,0:T(8,128)(2,1)} %refs_0_.1, f32[4096]{0:T(1024)S(1)} %bitcast.258), kind=kOutput, calls=%fused_computation.8 | convolution fusion | flops 1075838976 | bytes 12861440 | tf_op jit(solution)/shard_map/dot_general | solution.py:160
  135.8 4.7 %collective-permute-done.25 = f32[256,256]{1,0:T(8,128)S(1)} collective-permute-done((f32[256,256]{1,0:T(8,128)S(1)}, f32[256,256]{1,0:T(8,128)S(1)}, u32[]{:S(2)}, u32[]{:S(2)}) %collective-permute-start.25) | collective-permute-done | bytes 262176 | tf_op jit(solution)/shard_map/ppermute | solution.py:22
  148.3 4.0 %last_rows.1 = (bf16[1024,512]{1,0:T(8,128)(2,1)S(1)}, bf16[1024,512]{1,0:T(8,128)(2,1)S(1)}, bf16[1024,512]{1,0:T(8,128)(2,1)S(1)}, bf16[1024,512]{1,0:T(8,128)...) custom-call(s32[8]{0:T(128)S(1)} %iota_xor_fusion.base, ...), custom_call_target="tpu_custom_call" | custom-call | tf_op jit(solution)/shard_map/last_rows/pallas_call | solution.py:120
  152.4 1.6 collective-permute-done.27
  156.2 1.6 collective-permute-start.28
  158.6 4.9 %collective-permute-done.28 = f32[256,256]{1,0:T(8,128)S(1)} collective-permute-done((f32[256,256]{1,0:T(8,128)S(1)}, f32[256,256]{1,0:T(8,128)S(1)}, u32[]{:S(2)}, u32[]{:S(2)}) %collective-permute-start.28) | collective-permute-done | bytes 262176 | tf_op jit(solution)/shard_map/ppermute | solution.py:22
  168.8 2.7 %collective-permute-start.33 = (f32[256,128]{1,0:T(8,128)S(1)}, f32[256,128]{1,0:T(8,128)S(1)}, u32[]{:S(2)}, u32[]{:S(2)}) collective-permute-start(f32[256,128]{1,0:T(8,128)S(1)} %fusion.66), channel_id=1, source_target_pairs={{0,8},{8,0},{16,24},{24,16},{1,9},{9,1},{17,25},{25,17},{2,10},{10... | collective-permute-start | bytes 393224 | tf_op jit(solution)/shard_map/ppermute | solution.py:22
  171.6 3.4 %fusion.3 = f32[4096,256]{1,0:T(8,128)S(1)} fusion(f32[4096,256]{1,0:T(8,128)S(1)} %copy-done.5, bf16[512,256]{1,0:T(8,128)(2,1)S(1)} %pad_maximum_fusion.7, bf16[4,8192,512]{2,1,0:T(8,128)(2,1)} %refs_0_.1, f32[4096]{0:T(1024)S(1)} %bitcast.257), kind=kOutput, calls=%fused_computation.5 | convolution fusion | flops 1075838976 | bytes 12861440 | tf_op jit(solution)/shard_map/dot_general | solution.py:160
  175.4 2.1 collective-permute-done.34
  178.0 2.0 collective-permute-start.37
  180.9 1.9 collective-permute-start.35
  182.9 3.1 %fusion.1 = f32[4096,256]{1,0:T(8,128)S(1)} fusion(f32[4096,256]{1,0:T(8,128)S(1)} %copy-done.4, bf16[512,256]{1,0:T(8,128)(2,1)S(1)} %pad_maximum_fusion.7, bf16[4,8192,512]{2,1,0:T(8,128)(2,1)} %refs_0_.1, f32[4096]{0:T(1024)S(1)} %bitcast.256), kind=kOutput, calls=%fused_computation.2 | convolution fusion | flops 1075838976 | bytes 12861440 | tf_op jit(solution)/shard_map/dot_general | solution.py:160
  186.0 4.8 %collective-permute-done.37 = f32[256,128]{1,0:T(8,128)S(1)} collective-permute-done((f32[256,128]{1,0:T(8,128)S(1)}, f32[256,128]{1,0:T(8,128)S(1)}, u32[]{:S(2)}, u32[]{:S(2)}) %collective-permute-start.37) | collective-permute-done | bytes 131104 | tf_op jit(solution)/shard_map/ppermute | solution.py:22
  192.5 2.0 collective-permute-start.39
  197.2 1.6 collective-permute-done.40
  198.7 2.0 collective-permute-done.39
  202.9 1.6 collective-permute-start.55
  208.1 3.0 %collective-permute-done.56 = f32[512,128]{1,0:T(8,128)S(1)} collective-permute-done((f32[512,128]{1,0:T(8,128)S(1)}, f32[512,128]{1,0:T(8,128)S(1)}, u32[]{:S(2)}, u32[]{:S(2)}) %collective-permute-start.56) | collective-permute-done | bytes 262176 | tf_op jit(solution)/shard_map/ppermute | solution.py:22
  216.0 1.6 collective-permute-start.59
  217.6 5.5 %collective-permute-done.57 = f32[512,128]{1,0:T(8,128)S(1)} collective-permute-done((f32[512,128]{1,0:T(8,128)S(1)}, f32[512,128]{1,0:T(8,128)S(1)}, u32[]{:S(2)}, u32[]{:S(2)}) %collective-permute-start.57) | collective-permute-done | bytes 262176 | tf_op jit(solution)/shard_map/ppermute | solution.py:22
  224.9 4.9 %collective-permute-done.59 = f32[512,128]{1,0:T(8,128)S(1)} collective-permute-done((f32[512,128]{1,0:T(8,128)S(1)}, f32[512,128]{1,0:T(8,128)S(1)}, u32[]{:S(2)}, u32[]{:S(2)}) %collective-permute-start.59) | collective-permute-done | bytes 262176 | tf_op jit(solution)/shard_map/ppermute | solution.py:22
  235.4 5.8 %collective-permute-done.60 = f32[512,128]{1,0:T(8,128)S(1)} collective-permute-done((f32[512,128]{1,0:T(8,128)S(1)}, f32[512,128]{1,0:T(8,128)S(1)}, u32[]{:S(2)}, u32[]{:S(2)}) %collective-permute-start.60) | collective-permute-done | bytes 262176 | tf_op jit(solution)/shard_map/ppermute | solution.py:22
  (292 shorter events, 69.8 us)
Async XLA Ops:
  2.3 17.8 %collective-permute-start.1 = (f32[256,256]{1,0:T(8,128)S(1)}, f32[256,256]{1,0:T(8,128)S(1)}, u32[]{:S(2)}, u32[]{:S(2)}) collective-permute-start(f32[256,256]{1,0:T(8,128)S(1)} %fusion.80), channel_id=1, source_target_pairs={{0,16},{8,24},{16,0},{24,8},{1,17},{9,25},{17,1},{25,9},{2,18},{10... | collective-permute-start | bytes 786440 | tf_op jit(solution)/shard_map/ppermute | solution.py:22
  8.1 12.3 %collective-permute-start = (f32[256,256]{1,0:T(8,128)S(1)}, f32[256,256]{1,0:T(8,128)S(1)}, u32[]{:S(2)}, u32[]{:S(2)}) collective-permute-start(f32[256,256]{1,0:T(8,128)S(1)} %fusion.82), channel_id=1, source_target_pairs={{0,8},{8,0},{16,24},{24,16},{1,9},{9,1},{17,25},{25,17},{2,10},{10... | collective-permute-start | bytes 786440 | tf_op jit(solution)/shard_map/ppermute | solution.py:22
  20.5 12.7 %collective-permute-start.3 = (f32[256,256]{1,0:T(8,128)S(1)}, f32[256,256]{1,0:T(8,128)S(1)}, u32[]{:S(2)}, u32[]{:S(2)}) collective-permute-start(f32[256,256]{1,0:T(8,128)S(1)} %add.433), channel_id=1, source_target_pairs={{0,8},{8,0},{16,24},{24,16},{1,9},{9,1},{17,25},{25,17},{2,10},{10... | collective-permute-start | bytes 786440 | tf_op jit(solution)/shard_map/ppermute | solution.py:22
  20.8 13.8 %collective-permute-start.2 = (f32[256,256]{1,0:T(8,128)S(1)}, f32[256,256]{1,0:T(8,128)S(1)}, u32[]{:S(2)}, u32[]{:S(2)}) collective-permute-start(f32[256,256]{1,0:T(8,128)S(1)} %add.432), channel_id=1, source_target_pairs={{0,16},{8,24},{16,0},{24,8},{1,17},{9,25},{17,1},{25,9},{2,18},{10... | collective-permute-start | bytes 786440 | tf_op jit(solution)/shard_map/ppermute | solution.py:22
  38.8 8.8 %collective-permute-start.5 = (f32[256,256]{1,0:T(8,128)S(1)}, f32[256,256]{1,0:T(8,128)S(1)}, u32[]{:S(2)}, u32[]{:S(2)}) collective-permute-start(f32[256,256]{1,0:T(8,128)S(1)} %get-tuple-element.205), channel_id=1, source_target_pairs={{0,2},{1,3},{2,0},{3,1},{4,6},{5,7},{6,4},{7,5},{8,10},{9,11},{10,... | collective-permute-start | bytes 786440 | tf_op jit(solution)/shard_map/ppermute | solution.py:22
  40.3 8.4 %collective-permute-start.7 = (f32[256,256]{1,0:T(8,128)S(1)}, f32[256,256]{1,0:T(8,128)S(1)}, u32[]{:S(2)}, u32[]{:S(2)}) collective-permute-start(f32[256,256]{1,0:T(8,128)S(1)} %get-tuple-element.206), channel_id=1, source_target_pairs={{0,4},{1,5},{2,6},{3,7},{4,0},{5,1},{6,2},{7,3},{8,12},{9,13},{10,... | collective-permute-start | bytes 786440 | tf_op jit(solution)/shard_map/ppermute | solution.py:22
  48.8 7.7 %collective-permute-start.6 = (f32[256,256]{1,0:T(8,128)S(1)}, f32[256,256]{1,0:T(8,128)S(1)}, u32[]{:S(2)}, u32[]{:S(2)}) collective-permute-start(f32[256,256]{1,0:T(8,128)S(1)} %get-tuple-element.203), channel_id=1, source_target_pairs={{0,4},{1,5},{2,6},{3,7},{4,0},{5,1},{6,2},{7,3},{8,12},{9,13},{10,... | collective-permute-start | bytes 786440 | tf_op jit(solution)/shard_map/ppermute | solution.py:22
  50.4 7.3 %collective-permute-start.8 = (f32[256,256]{1,0:T(8,128)S(1)}, f32[256,256]{1,0:T(8,128)S(1)}, u32[]{:S(2)}, u32[]{:S(2)}) collective-permute-start(f32[256,256]{1,0:T(8,128)S(1)} %get-tuple-element.204), channel_id=1, source_target_pairs={{0,2},{1,3},{2,0},{3,1},{4,6},{5,7},{6,4},{7,5},{8,10},{9,11},{10,... | collective-permute-start | bytes 786440 | tf_op jit(solution)/shard_map/ppermute | solution.py:22
  60.9 14.8 %collective-permute-start.12 = (f32[256,256]{1,0:T(8,128)S(1)}, f32[256,256]{1,0:T(8,128)S(1)}, u32[]{:S(2)}, u32[]{:S(2)}) collective-permute-start(f32[256,256]{1,0:T(8,128)S(1)} %fusion.62), channel_id=1, source_target_pairs={{0,16},{8,24},{16,0},{24,8},{1,17},{9,25},{17,1},{25,9},{2,18},{10... | collective-permute-start | bytes 786440 | tf_op jit(solution)/shard_map/ppermute | solution.py:22
  61.5 14.6 %collective-permute-start.11 = (f32[256,256]{1,0:T(8,128)S(1)}, f32[256,256]{1,0:T(8,128)S(1)}, u32[]{:S(2)}, u32[]{:S(2)}) collective-permute-start(f32[256,256]{1,0:T(8,128)S(1)} %fusion.60), channel_id=1, source_target_pairs={{0,8},{8,0},{16,24},{24,16},{1,9},{9,1},{17,25},{25,17},{2,10},{10... | collective-permute-start | bytes 786440 | tf_op jit(solution)/shard_map/ppermute | solution.py:22
  76.2 12.3 %collective-permute-start.14 = (f32[256,256]{1,0:T(8,128)S(1)}, f32[256,256]{1,0:T(8,128)S(1)}, u32[]{:S(2)}, u32[]{:S(2)}) collective-permute-start(f32[256,256]{1,0:T(8,128)S(1)} %add.458), channel_id=1, source_target_pairs={{0,8},{8,0},{16,24},{24,16},{1,9},{9,1},{17,25},{25,17},{2,10},{10... | collective-permute-start | bytes 786440 | tf_op jit(solution)/shard_map/ppermute | solution.py:22
  76.2 14.4 %collective-permute-start.13 = (f32[256,256]{1,0:T(8,128)S(1)}, f32[256,256]{1,0:T(8,128)S(1)}, u32[]{:S(2)}, u32[]{:S(2)}) collective-permute-start(f32[256,256]{1,0:T(8,128)S(1)} %add.457), channel_id=1, source_target_pairs={{0,16},{8,24},{16,0},{24,8},{1,17},{9,25},{17,1},{25,9},{2,18},{10... | collective-permute-start | bytes 786440 | tf_op jit(solution)/shard_map/ppermute | solution.py:22
  93.4 8.4 %collective-permute-start.16 = (f32[256,256]{1,0:T(8,128)S(1)}, f32[256,256]{1,0:T(8,128)S(1)}, u32[]{:S(2)}, u32[]{:S(2)}) collective-permute-start(f32[256,256]{1,0:T(8,128)S(1)} %get-tuple-element.201), channel_id=1, source_target_pairs={{0,2},{1,3},{2,0},{3,1},{4,6},{5,7},{6,4},{7,5},{8,10},{9,11},{10,... | collective-permute-start | bytes 786440 | tf_op jit(solution)/shard_map/ppermute | solution.py:22
  94.1 8.1 %collective-permute-start.18 = (f32[256,256]{1,0:T(8,128)S(1)}, f32[256,256]{1,0:T(8,128)S(1)}, u32[]{:S(2)}, u32[]{:S(2)}) collective-permute-start(f32[256,256]{1,0:T(8,128)S(1)} %get-tuple-element.202), channel_id=1, source_target_pairs={{0,4},{1,5},{2,6},{3,7},{4,0},{5,1},{6,2},{7,3},{8,12},{9,13},{10,... | collective-permute-start | bytes 786440 | tf_op jit(solution)/shard_map/ppermute | solution.py:22
  102.3 7.3 %collective-permute-start.17 = (f32[256,256]{1,0:T(8,128)S(1)}, f32[256,256]{1,0:T(8,128)S(1)}, u32[]{:S(2)}, u32[]{:S(2)}) collective-permute-start(f32[256,256]{1,0:T(8,128)S(1)} %get-tuple-element.199), channel_id=1, source_target_pairs={{0,4},{1,5},{2,6},{3,7},{4,0},{5,1},{6,2},{7,3},{8,12},{9,13},{10,... | collective-permute-start | bytes 786440 | tf_op jit(solution)/shard_map/ppermute | solution.py:22
  102.8 6.9 %collective-permute-start.19 = (f32[256,256]{1,0:T(8,128)S(1)}, f32[256,256]{1,0:T(8,128)S(1)}, u32[]{:S(2)}, u32[]{:S(2)}) collective-permute-start(f32[256,256]{1,0:T(8,128)S(1)} %get-tuple-element.200), channel_id=1, source_target_pairs={{0,2},{1,3},{2,0},{3,1},{4,6},{5,7},{6,4},{7,5},{8,10},{9,11},{10,... | collective-permute-start | bytes 786440 | tf_op jit(solution)/shard_map/ppermute | solution.py:22
  112.9 13.9 %collective-permute-start.23 = (f32[256,256]{1,0:T(8,128)S(1)}, f32[256,256]{1,0:T(8,128)S(1)}, u32[]{:S(2)}, u32[]{:S(2)}) collective-permute-start(f32[256,256]{1,0:T(8,128)S(1)} %fusion.58), channel_id=1, source_target_pairs={{0,16},{8,24},{16,0},{24,8},{1,17},{9,25},{17,1},{25,9},{2,18},{10... | collective-permute-start | bytes 786440 | tf_op jit(solution)/shard_map/ppermute | solution.py:22
  113.4 13.8 %collective-permute-start.22 = (f32[256,256]{1,0:T(8,128)S(1)}, f32[256,256]{1,0:T(8,128)S(1)}, u32[]{:S(2)}, u32[]{:S(2)}) collective-permute-start(f32[256,256]{1,0:T(8,128)S(1)} %fusion.56), channel_id=1, source_target_pairs={{0,8},{8,0},{16,24},{24,16},{1,9},{9,1},{17,25},{25,17},{2,10},{10... | collective-permute-start | bytes 786440 | tf_op jit(solution)/shard_map/ppermute | solution.py:22
  127.3 13.2 %collective-permute-start.25 = (f32[256,256]{1,0:T(8,128)S(1)}, f32[256,256]{1,0:T(8,128)S(1)}, u32[]{:S(2)}, u32[]{:S(2)}) collective-permute-start(f32[256,256]{1,0:T(8,128)S(1)} %add.476), channel_id=1, source_target_pairs={{0,8},{8,0},{16,24},{24,16},{1,9},{9,1},{17,25},{25,17},{2,10},{10... | collective-permute-start | bytes 786440 | tf_op jit(solution)/shard_map/ppermute | solution.py:22
  127.4 14.4 %collective-permute-start.24 = (f32[256,256]{1,0:T(8,128)S(1)}, f32[256,256]{1,0:T(8,128)S(1)}, u32[]{:S(2)}, u32[]{:S(2)}) collective-permute-start(f32[256,256]{1,0:T(8,128)S(1)} %add.475), channel_id=1, source_target_pairs={{0,16},{8,24},{16,0},{24,8},{1,17},{9,25},{17,1},{25,9},{2,18},{10... | collective-permute-start | bytes 786440 | tf_op jit(solution)/shard_map/ppermute | solution.py:22
  145.3 8.7 %collective-permute-start.27 = (f32[256,256]{1,0:T(8,128)}, f32[256,256]{1,0:T(8,128)}, u32[]{:S(2)}, u32[]{:S(2)}) collective-permute-start(f32[256,256]{1,0:T(8,128)} %get-tuple-element.197), channel_id=1, source_target_pairs={{0,2},{1,3},{2,0},{3,1},{4,6},{5,7},{6,4},{7,5},{8,10},{9,11},{10,... | collective-permute-start | bytes 786440 | tf_op jit(solution)/shard_map/ppermute | solution.py:22
  146.8 8.4 %collective-permute-start.29 = (f32[256,256]{1,0:T(8,128)}, f32[256,256]{1,0:T(8,128)}, u32[]{:S(2)}, u32[]{:S(2)}) collective-permute-start(f32[256,256]{1,0:T(8,128)} %get-tuple-element.198), channel_id=1, source_target_pairs={{0,4},{1,5},{2,6},{3,7},{4,0},{5,1},{6,2},{7,3},{8,12},{9,13},{10,... | collective-permute-start | bytes 786440 | tf_op jit(solution)/shard_map/ppermute | solution.py:22
  156.2 7.3 %collective-permute-start.28 = (f32[256,256]{1,0:T(8,128)S(1)}, f32[256,256]{1,0:T(8,128)S(1)}, u32[]{:S(2)}, u32[]{:S(2)}) collective-permute-start(f32[256,256]{1,0:T(8,128)S(1)} %get-tuple-element.195), channel_id=1, source_target_pairs={{0,4},{1,5},{2,6},{3,7},{4,0},{5,1},{6,2},{7,3},{8,12},{9,13},{10,... | collective-permute-start | bytes 786440 | tf_op jit(solution)/shard_map/ppermute | solution.py:22
  157.8 6.9 %collective-permute-start.30 = (f32[256,256]{1,0:T(8,128)S(1)}, f32[256,256]{1,0:T(8,128)S(1)}, u32[]{:S(2)}, u32[]{:S(2)}) collective-permute-start(f32[256,256]{1,0:T(8,128)S(1)} %get-tuple-element.196), channel_id=1, source_target_pairs={{0,2},{1,3},{2,0},{3,1},{4,6},{5,7},{6,4},{7,5},{8,10},{9,11},{10,... | collective-permute-start | bytes 786440 | tf_op jit(solution)/shard_map/ppermute | solution.py:22
  168.3 9.1 %collective-permute-start.34 = (f32[256,128]{1,0:T(8,128)S(1)}, f32[256,128]{1,0:T(8,128)S(1)}, u32[]{:S(2)}, u32[]{:S(2)}) collective-permute-start(f32[256,128]{1,0:T(8,128)S(1)} %fusion.63), channel_id=1, source_target_pairs={{0,16},{8,24},{16,0},{24,8},{1,17},{9,25},{17,1},{25,9},{2,18},{10... | collective-permute-start | bytes 393224 | tf_op jit(solution)/shard_map/ppermute | solution.py:22
  168.8 9.0 %collective-permute-start.33 = (f32[256,128]{1,0:T(8,128)S(1)}, f32[256,128]{1,0:T(8,128)S(1)}, u32[]{:S(2)}, u32[]{:S(2)}) collective-permute-start(f32[256,128]{1,0:T(8,128)S(1)} %fusion.66), channel_id=1, source_target_pairs={{0,8},{8,0},{16,24},{24,16},{1,9},{9,1},{17,25},{25,17},{2,10},{10... | collective-permute-start | bytes 393224 | tf_op jit(solution)/shard_map/ppermute | solution.py:22
  177.9 8.1 %collective-permute-start.38 = (f32[256,128]{1,0:T(8,128)S(1)}, f32[256,128]{1,0:T(8,128)S(1)}, u32[]{:S(2)}, u32[]{:S(2)}) collective-permute-start(f32[256,128]{1,0:T(8,128)S(1)} %add.505), channel_id=1, source_target_pairs={{0,8},{8,0},{16,24},{24,16},{1,9},{9,1},{17,25},{25,17},{2,10},{10... | collective-permute-start | bytes 393224 | tf_op jit(solution)/shard_map/ppermute | solution.py:22
  178.0 12.9 %collective-permute-start.37 = (f32[256,128]{1,0:T(8,128)S(1)}, f32[256,128]{1,0:T(8,128)S(1)}, u32[]{:S(2)}, u32[]{:S(2)}) collective-permute-start(f32[256,128]{1,0:T(8,128)S(1)} %add.504), channel_id=1, source_target_pairs={{0,16},{8,24},{16,0},{24,8},{1,17},{9,25},{17,1},{25,9},{2,18},{10... | collective-permute-start | bytes 393224 | tf_op jit(solution)/shard_map/ppermute | solution.py:22
  180.0 12.4 %collective-permute-start.36 = (f32[256,128]{1,0:T(8,128)S(1)}, f32[256,128]{1,0:T(8,128)S(1)}, u32[]{:S(2)}, u32[]{:S(2)}) collective-permute-start(f32[256,128]{1,0:T(8,128)S(1)} %fusion.65), channel_id=1, source_target_pairs={{0,16},{8,24},{16,0},{24,8},{1,17},{9,25},{17,1},{25,9},{2,18},{10... | collective-permute-start | bytes 393224 | tf_op jit(solution)/shard_map/ppermute | solution.py:22
  180.9 11.5 %collective-permute-start.35 = (f32[256,128]{1,0:T(8,128)S(1)}, f32[256,128]{1,0:T(8,128)S(1)}, u32[]{:S(2)}, u32[]{:S(2)}) collective-permute-start(f32[256,128]{1,0:T(8,128)S(1)} %fusion.64), channel_id=1, source_target_pairs={{0,8},{8,0},{16,24},{24,16},{1,9},{9,1},{17,25},{25,17},{2,10},{10... | collective-permute-start | bytes 393224 | tf_op jit(solution)/shard_map/ppermute | solution.py:22
  192.5 6.3 %collective-permute-start.40 = (f32[256,128]{1,0:T(8,128)S(1)}, f32[256,128]{1,0:T(8,128)S(1)}, u32[]{:S(2)}, u32[]{:S(2)}) collective-permute-start(f32[256,128]{1,0:T(8,128)S(1)} %add.508), channel_id=1, source_target_pairs={{0,8},{8,0},{16,24},{24,16},{1,9},{9,1},{17,25},{25,17},{2,10},{10... | collective-permute-start | bytes 393224 | tf_op jit(solution)/shard_map/ppermute | solution.py:22
  192.5 8.2 %collective-permute-start.39 = (f32[256,128]{1,0:T(8,128)S(1)}, f32[256,128]{1,0:T(8,128)S(1)}, u32[]{:S(2)}, u32[]{:S(2)}) collective-permute-start(f32[256,128]{1,0:T(8,128)S(1)} %add.507), channel_id=1, source_target_pairs={{0,16},{8,24},{16,0},{24,8},{1,17},{9,25},{17,1},{25,9},{2,18},{10... | collective-permute-start | bytes 393224 | tf_op jit(solution)/shard_map/ppermute | solution.py:22
  196.6 9.9 %collective-permute-start.45 = (f32[1024,128]{1,0:T(8,128)S(1)}, f32[1024,128]{1,0:T(8,128)S(1)}, u32[]{:S(2)}, u32[]{:S(2)}) collective-permute-start(f32[1024,128]{1,0:T(8,128)S(1)} %fusion.36), channel_id=1, source_target_pairs={{0,1},{1,0},{2,3},{3,2},{4,5},{5,4},{6,7},{7,6},{8,9},{9,8},{10,11... | collective-permute-start | bytes 1572872 | tf_op jit(solution)/shard_map/ppermute | solution.py:22
  201.8 9.3 %collective-permute-start.56 = (f32[512,128]{1,0:T(8,128)S(1)}, f32[512,128]{1,0:T(8,128)S(1)}, u32[]{:S(2)}, u32[]{:S(2)}) collective-permute-start(f32[512,128]{1,0:T(8,128)S(1)} %get-tuple-element.113), channel_id=1, source_target_pairs={{0,4},{1,5},{2,6},{3,7},{4,0},{5,1},{6,2},{7,3},{8,12},{9,13},{10,... | collective-permute-start | bytes 786440 | tf_op jit(solution)/shard_map/ppermute | solution.py:22
  202.9 13.1 %collective-permute-start.55 = (f32[512,128]{1,0:T(8,128)S(1)}, f32[512,128]{1,0:T(8,128)S(1)}, u32[]{:S(2)}, u32[]{:S(2)}) collective-permute-start(f32[512,128]{1,0:T(8,128)S(1)} %get-tuple-element.119), channel_id=1, source_target_pairs={{0,4},{1,5},{2,6},{3,7},{4,0},{5,1},{6,2},{7,3},{8,12},{9,13},{10,... | collective-permute-start | bytes 786440 | tf_op jit(solution)/shard_map/ppermute | solution.py:22
  204.5 7.3 %collective-permute-start.47 = (f32[512,128]{1,0:T(8,128)S(1)}, f32[512,128]{1,0:T(8,128)S(1)}, u32[]{:S(2)}, u32[]{:S(2)}) collective-permute-start(f32[512,128]{1,0:T(8,128)S(1)} %get-tuple-element.112), channel_id=1, source_target_pairs={{0,2},{1,3},{2,0},{3,1},{4,6},{5,7},{6,4},{7,5},{8,10},{9,11},{10,... | collective-permute-start | bytes 786440 | tf_op jit(solution)/shard_map/ppermute | solution.py:22
  205.6 6.3 %collective-permute-start.50 = (f32[1024,128]{1,0:T(8,128)S(1)}, f32[1024,128]{1,0:T(8,128)S(1)}, u32[]{:S(2)}, u32[]{:S(2)}) collective-permute-start(f32[1024,128]{1,0:T(8,128)S(1)} %fusion.42), channel_id=1, source_target_pairs={{0,1},{1,0},{2,3},{3,2},{4,5},{5,4},{6,7},{7,6},{8,9},{9,8},{10,11... | collective-permute-start | bytes 1572872 | tf_op jit(solution)/shard_map/ppermute | solution.py:22
  206.6 6.4 %collective-permute-start.44 = (f32[1024,128]{1,0:T(8,128)S(1)}, f32[1024,128]{1,0:T(8,128)S(1)}, u32[]{:S(2)}, u32[]{:S(2)}) collective-permute-start(f32[1024,128]{1,0:T(8,128)S(1)} %fusion.33), channel_id=1, source_target_pairs={{0,1},{1,0},{2,3},{3,2},{4,5},{5,4},{6,7},{7,6},{8,9},{9,8},{10,11... | collective-permute-start | bytes 1572872 | tf_op jit(solution)/shard_map/ppermute | solution.py:22
  211.1 19.3 %collective-permute-start.46 = (f32[512,128]{1,0:T(8,128)S(1)}, f32[512,128]{1,0:T(8,128)S(1)}, u32[]{:S(2)}, u32[]{:S(2)}) collective-permute-start(f32[512,128]{1,0:T(8,128)S(1)} %get-tuple-element.124), channel_id=1, source_target_pairs={{0,2},{1,3},{2,0},{3,1},{4,6},{5,7},{6,4},{7,5},{8,10},{9,11},{10,... | collective-permute-start | bytes 786440 | tf_op jit(solution)/shard_map/ppermute | solution.py:22
  211.9 11.9 %collective-permute-start.52 = (f32[1024,128]{1,0:T(8,128)S(1)}, f32[1024,128]{1,0:T(8,128)S(1)}, u32[]{:S(2)}, u32[]{:S(2)}) collective-permute-start(f32[1024,128]{1,0:T(8,128)S(1)} %fusion.45), channel_id=1, source_target_pairs={{0,1},{1,0},{2,3},{3,2},{4,5},{5,4},{6,7},{7,6},{8,9},{9,8},{10,11... | collective-permute-start | bytes 1572872 | tf_op jit(solution)/shard_map/ppermute | solution.py:22
  213.0 10.1 %collective-permute-start.57 = (f32[512,128]{1,0:T(8,128)S(1)}, f32[512,128]{1,0:T(8,128)S(1)}, u32[]{:S(2)}, u32[]{:S(2)}) collective-permute-start(f32[512,128]{1,0:T(8,128)S(1)} %add.558), channel_id=1, source_target_pairs={{0,2},{1,3},{2,0},{3,1},{4,6},{5,7},{6,4},{7,5},{8,10},{9,11},{10,... | collective-permute-start | bytes 786440 | tf_op jit(solution)/shard_map/ppermute | solution.py:22
  214.9 17.0 %collective-permute-start.48 = (f32[512,128]{1,0:T(8,128)S(1)}, f32[512,128]{1,0:T(8,128)S(1)}, u32[]{:S(2)}, u32[]{:S(2)}) collective-permute-start(f32[512,128]{1,0:T(8,128)S(1)} %add.543), channel_id=1, source_target_pairs={{0,4},{1,5},{2,6},{3,7},{4,0},{5,1},{6,2},{7,3},{8,12},{9,13},{10,... | collective-permute-start | bytes 786440 | tf_op jit(solution)/shard_map/ppermute | solution.py:22
  216.0 13.8 %collective-permute-start.59 = (f32[512,128]{1,0:T(8,128)S(1)}, f32[512,128]{1,0:T(8,128)S(1)}, u32[]{:S(2)}, u32[]{:S(2)}) collective-permute-start(f32[512,128]{1,0:T(8,128)S(1)} %get-tuple-element.143), channel_id=1, source_target_pairs={{0,4},{1,5},{2,6},{3,7},{4,0},{5,1},{6,2},{7,3},{8,12},{9,13},{10,... | collective-permute-start | bytes 786440 | tf_op jit(solution)/shard_map/ppermute | solution.py:22
  223.1 8.9 %collective-permute-start.53 = (f32[512,128]{1,0:T(8,128)S(1)}, f32[512,128]{1,0:T(8,128)S(1)}, u32[]{:S(2)}, u32[]{:S(2)}) collective-permute-start(f32[512,128]{1,0:T(8,128)S(1)} %get-tuple-element.128), channel_id=1, source_target_pairs={{0,2},{1,3},{2,0},{3,1},{4,6},{5,7},{6,4},{7,5},{8,10},{9,11},{10,... | collective-permute-start | bytes 786440 | tf_op jit(solution)/shard_map/ppermute | solution.py:22
  224.3 11.1 %collective-permute-start.58 = (f32[512,128]{1,0:T(8,128)S(1)}, f32[512,128]{1,0:T(8,128)S(1)}, u32[]{:S(2)}, u32[]{:S(2)}) collective-permute-start(f32[512,128]{1,0:T(8,128)S(1)} %get-tuple-element.141), channel_id=1, source_target_pairs={{0,4},{1,5},{2,6},{3,7},{4,0},{5,1},{6,2},{7,3},{8,12},{9,13},{10,... | collective-permute-start | bytes 786440 | tf_op jit(solution)/shard_map/ppermute | solution.py:22
  229.8 11.5 %collective-permute-start.51 = (f32[512,128]{1,0:T(8,128)S(1)}, f32[512,128]{1,0:T(8,128)S(1)}, u32[]{:S(2)}, u32[]{:S(2)}) collective-permute-start(f32[512,128]{1,0:T(8,128)S(1)} %get-tuple-element.137), channel_id=1, source_target_pairs={{0,2},{1,3},{2,0},{3,1},{4,6},{5,7},{6,4},{7,5},{8,10},{9,11},{10,... | collective-permute-start | bytes 786440 | tf_op jit(solution)/shard_map/ppermute | solution.py:22
  230.5 10.7 %collective-permute-start.60 = (f32[512,128]{1,0:T(8,128)S(1)}, f32[512,128]{1,0:T(8,128)S(1)}, u32[]{:S(2)}, u32[]{:S(2)}) collective-permute-start(f32[512,128]{1,0:T(8,128)S(1)} %add.561), channel_id=1, source_target_pairs={{0,2},{1,3},{2,0},{3,1},{4,6},{5,7},{6,4},{7,5},{8,10},{9,11},{10,... | collective-permute-start | bytes 786440 | tf_op jit(solution)/shard_map/ppermute | solution.py:22
  232.0 9.2 %collective-permute-start.54 = (f32[512,128]{1,0:T(8,128)S(1)}, f32[512,128]{1,0:T(8,128)S(1)}, u32[]{:S(2)}, u32[]{:S(2)}) collective-permute-start(f32[512,128]{1,0:T(8,128)S(1)} %add.555), channel_id=1, source_target_pairs={{0,4},{1,5},{2,6},{3,7},{4,0},{5,1},{6,2},{7,3},{8,12},{9,13},{10,... | collective-permute-start | bytes 786440 | tf_op jit(solution)/shard_map/ppermute | solution.py:22
  (45 other events, 258.7 us)

commit v5 on v4

--- a/solution.py
+++ b/solution.py
@@ -66,35 +66,33 @@
     return tuple(2 << b for b in range(n.bit_length() - 2))
 
 
-def stage_kernel(sel, c_ref, d_ref, *refs):
-    outs, sem = refs[:4], refs[4]
+def stage_kernel(dim, sel, x_ref, *refs):
+    outs, sem = refs[:2], refs[2]
+    size = outs[0].shape[dim]
     copies = []
     for side in range(2):
         half_of = sel[0] if side else 1 - sel[0]
-        rows, depth = outs[side].shape[1], outs[2 + side].shape[2]
-        sources = (c_ref.at[:, pl.ds(half_of * rows, rows), :], d_ref.at[:, :, pl.ds(half_of * depth, depth)])
-        for k, source in enumerate(sources):
-            copies.append(pltpu.make_async_copy(source, outs[2 * k + side], sem.at[2 * k + side]))
+        at = [slice(None)] * 3
+        at[dim] = pl.ds(half_of * size, size)
+        copies.append(pltpu.make_async_copy(x_ref.at[tuple(at)], outs[side], sem.at[side]))
     for copy in copies:
         copy.start()
     for copy in copies:
         copy.wait()
 
 
-def stage(bit, couple, dinv):
-    pairs, rows, depth = couple.shape
-    panels, height, width = dinv.shape
-    shapes = [(pairs, rows // 2, depth)] * 2 + [(panels, height, width // 2)] * 2
-    out = pl.pallas_call(
-        stage_kernel,
-        out_shape=[jax.ShapeDtypeStruct(shape, BF16) for shape in shapes],
-        in_specs=[SMEM, HBM, HBM],
-        out_specs=[VMEM] * 4,
-        scratch_shapes=[pltpu.SemaphoreType.DMA((4,))],
+def stage(sel, x, dim):
+    shape = list(x.shape)
+    shape[dim] //= 2
+    return pl.pallas_call(
+        functools.partial(stage_kernel, dim),
+        out_shape=[jax.ShapeDtypeStruct(shape, BF16)] * 2,
+        in_specs=[SMEM, HBM],
+        out_specs=[VMEM] * 2,
+        scratch_shapes=[pltpu.SemaphoreType.DMA((2,))],
         compiler_params=pltpu.CompilerParams(vmem_limit_bytes=44 << 20),
         name="stage",
-    )(bit, couple, dinv)
-    return out[:2], out[2:]
+    )(sel, x)
 
 
 def row_major(x):
@@ -162,9 +160,13 @@
         early[top] = row_major(early[top] + term if panel else term)
         return early[top]
 
-    def stage_step(dep):
-        store["couple"], store["dinv"] = stage(after(sel, dep), couple, dinv)
+    def couple_step(dep):
+        store["couple"] = stage(after(sel, dep), couple, 1)
         return store["couple"][0]
+
+    def dinv_step(dep):
+        store["dinv"] = stage(after(sel, dep), dinv, 2)
+        return store["dinv"][0]
 
     def last_step(dep):
         store["last"] = last_rows(after(blocks, dep), below_factor, own)
@@ -213,7 +215,7 @@
         return total
 
     solutions, solved = [], []
-    queue = [stage_step, last_step]
+    queue = [dinv_step, couple_step, last_step]
     for target in range(PANELS):
         right = rhs[target]
         if target > 0:

time: 243 us -> 241 us (level)
    pallas_call x1 -> x2, Pallas kernels: 5.79 us -> 3.57 us  [stage(): pl.pallas_call(functools.partial(stage_kernel, dim), out_shape=[jax.Shape...]
  transfers between devices with their start and end apart: 61 -> 61, of which waited for: 43 -> 44; matrix products, arithmetic and copies ran while one was open for 18% -> 18% of each run, Pallas kernels for 4% -> 3%
where the time goes in v5:
time: 241 us; the launch traced here: 240 us
  waiting for transfers between devices  115 us (48%)
  starting transfers between devices  57.5 us (24%)
  matrix products  43.7 us (18%)
  local copies, waits for them, and re-layouts  7.89 us (3%)
  Pallas kernels  7.59 us (3%)
  other arithmetic  6.35 us (3%)
    ppermute x61, waiting for transfers between devices, swap(): return lax.ppermute(x, axis, [(i, i ^ mask) for i in range(n)])  115 us
    ppermute x61, starting transfers between devices, swap(): return lax.ppermute(x, axis, [(i, i ^ mask) for i in range(n)])  57.5 us
    dot_general x6, matrix products, early_step(): term = jnp.dot(factor, after(solved, dep), preferred_element_type=F32)  23.9 us
    dot_general x16, matrix products, tail(): term = jnp.dot(store['last'][q], solved, preferred_element_type=F32)  7.15 us
    dot_general x32, matrix products, inverse_dots(): jnp.dot(block, right[side][k].astype(BF16), preferred_element_type=F32)  5.66 us
  transfers between devices with their start and end apart: 61, of which 44 were waited for; matrix products, arithmetic and copies ran while one was open for 18% of the time, Pallas kernels for 3%

profile of v5, /device:TPU:0, one launch (start us, length us, event | category | flops | bytes accessed | tf_op | source)
XLA Modules:
  0.0 240.2 jit_solution(263984200907371077)
XLA Ops:
  0.6 1.7 fusion.80
  2.3 4.1 %collective-permute-start.1 = (f32[256,256]{1,0:T(8,128)S(1)}, f32[256,256]{1,0:T(8,128)S(1)}, u32[]{:S(2)}, u32[]{:S(2)}) collective-permute-start(f32[256,256]{1,0:T(8,128)S(1)} %fusion.80), channel_id=1, source_target_pairs={{0,16},{8,24},{16,0},{24,8},{1,17},{9,25},{17,1},{25,9},{2,18},{10... | collective-permute-start | bytes 786440 | tf_op jit(solution)/shard_map/ppermute | solution.py:22
  6.4 1.7 fusion.82
  8.1 1.6 collective-permute-start
  11.3 2.2 copy-done
  15.4 3.1 %collective-permute-done.1 = f32[256,256]{1,0:T(8,128)S(1)} collective-permute-done((f32[256,256]{1,0:T(8,128)S(1)}, f32[256,256]{1,0:T(8,128)S(1)}, u32[]{:S(2)}, u32[]{:S(2)}) %collective-permute-start.1) | collective-permute-done | bytes 262176 | tf_op jit(solution)/shard_map/ppermute | solution.py:22
  18.5 1.9 collective-permute-done
  20.5 3.0 %collective-permute-start.2 = (f32[256,256]{1,0:T(8,128)S(1)}, f32[256,256]{1,0:T(8,128)S(1)}, u32[]{:S(2)}, u32[]{:S(2)}) collective-permute-start(f32[256,256]{1,0:T(8,128)S(1)} %add.432), channel_id=1, source_target_pairs={{0,16},{8,24},{16,0},{24,8},{1,17},{9,25},{17,1},{25,9},{2,18},{10... | collective-permute-start | bytes 786440 | tf_op jit(solution)/shard_map/ppermute | solution.py:22
  24.3 3.0 %stage.3 = (bf16[6,512,512]{2,1,0:T(8,128)(2,1)S(1)}, bf16[6,512,512]{2,1,0:T(8,128)(2,1)S(1)}) custom-call(s32[1]{0:T(128)} %bitcast.3.sel, bf16[6,1024,512]{2,1,0:T(8,128)(2,1)} %x_ref.3), custom_call_target="tpu_custom_call" | custom-call | tf_op jit(solution)/shard_map/stage/pallas_call | solution.py:87
  27.3 5.4 %collective-permute-done.3 = f32[256,256]{1,0:T(8,128)S(1)} collective-permute-done((f32[256,256]{1,0:T(8,128)S(1)}, f32[256,256]{1,0:T(8,128)S(1)}, u32[]{:S(2)}, u32[]{:S(2)}) %collective-permute-start.3) | collective-permute-done | bytes 262176 | tf_op jit(solution)/shard_map/ppermute | solution.py:22
  32.8 1.7 collective-permute-done.2
  40.5 5.2 %collective-permute-done.5 = f32[256,256]{1,0:T(8,128)S(1)} collective-permute-done((f32[256,256]{1,0:T(8,128)S(1)}, f32[256,256]{1,0:T(8,128)S(1)}, u32[]{:S(2)}, u32[]{:S(2)}) %collective-permute-start.5) | collective-permute-done | bytes 262176 | tf_op jit(solution)/shard_map/ppermute | solution.py:22
  47.0 1.6 collective-permute-start.6
  49.4 4.8 %collective-permute-done.6 = f32[256,256]{1,0:T(8,128)S(1)} collective-permute-done((f32[256,256]{1,0:T(8,128)S(1)}, f32[256,256]{1,0:T(8,128)S(1)}, u32[]{:S(2)}, u32[]{:S(2)}) %collective-permute-start.6) | collective-permute-done | bytes 262176 | tf_op jit(solution)/shard_map/ppermute | solution.py:22
  58.9 3.0 %collective-permute-start.11 = (f32[256,256]{1,0:T(8,128)S(1)}, f32[256,256]{1,0:T(8,128)S(1)}, u32[]{:S(2)}, u32[]{:S(2)}) collective-permute-start(f32[256,256]{1,0:T(8,128)S(1)} %fusion.60), channel_id=1, source_target_pairs={{0,8},{8,0},{16,24},{24,16},{1,9},{9,1},{17,25},{25,17},{2,10},{10... | collective-permute-start | bytes 786440 | tf_op jit(solution)/shard_map/ppermute | solution.py:22
  62.0 3.0 %fusion.9 = f32[4096,256]{1,0:T(8,128)S(1)} fusion(bf16[512,256]{1,0:T(8,128)(2,1)S(1)} %pad_maximum_fusion.5, bf16[4,8192,512]{2,1,0:T(8,128)(2,1)} %refs_0_.1, f32[4096]{0:T(1024)S(1)} %bitcast.262), kind=kOutput, calls=%fused_computation.15 | convolution fusion | flops 1074790400 | bytes 8667136 | tf_op jit(solution)/shard_map/dot_general | solution.py:158
  65.0 8.4 %collective-permute-done.12 = f32[256,256]{1,0:T(8,128)S(1)} collective-permute-done((f32[256,256]{1,0:T(8,128)S(1)}, f32[256,256]{1,0:T(8,128)S(1)}, u32[]{:S(2)}, u32[]{:S(2)}) %collective-permute-start.12) | collective-permute-done | bytes 262176 | tf_op jit(solution)/shard_map/ppermute | solution.py:22
  74.0 2.1 collective-permute-start.13
  76.0 3.2 %fusion.8 = f32[4096,256]{1,0:T(8,128)S(1)} fusion(bf16[512,256]{1,0:T(8,128)(2,1)S(1)} %pad_maximum_fusion.5, bf16[4,8192,512]{2,1,0:T(8,128)(2,1)} %refs_0_.1, f32[4096]{0:T(1024)S(1)} %bitcast.261), kind=kOutput, calls=%fused_computation.13 | convolution fusion | flops 1074790400 | bytes 8667136 | tf_op jit(solution)/shard_map/dot_general | solution.py:158
  79.3 6.9 %collective-permute-done.14 = f32[256,256]{1,0:T(8,128)S(1)} collective-permute-done((f32[256,256]{1,0:T(8,128)S(1)}, f32[256,256]{1,0:T(8,128)S(1)}, u32[]{:S(2)}, u32[]{:S(2)}) %collective-permute-start.14) | collective-permute-done | bytes 262176 | tf_op jit(solution)/shard_map/ppermute | solution.py:22
  86.2 2.2 collective-permute-done.13
  89.2 1.6 collective-permute-done.15
  92.7 6.9 %collective-permute-done.16 = f32[256,256]{1,0:T(8,128)S(1)} collective-permute-done((f32[256,256]{1,0:T(8,128)S(1)}, f32[256,256]{1,0:T(8,128)S(1)}, u32[]{:S(2)}, u32[]{:S(2)}) %collective-permute-start.16) | collective-permute-done | bytes 262176 | tf_op jit(solution)/shard_map/ppermute | solution.py:22
  102.3 4.9 %collective-permute-done.17 = f32[256,256]{1,0:T(8,128)S(1)} collective-permute-done((f32[256,256]{1,0:T(8,128)S(1)}, f32[256,256]{1,0:T(8,128)S(1)}, u32[]{:S(2)}, u32[]{:S(2)}) %collective-permute-start.17) | collective-permute-done | bytes 262176 | tf_op jit(solution)/shard_map/ppermute | solution.py:22
  111.2 1.8 collective-permute-start.22
  112.9 5.6 %fusion.7 = f32[4096,256]{1,0:T(8,128)} fusion(f32[4096,256]{1,0:T(8,128)S(1)} %fusion.9, bf16[512,256]{1,0:T(8,128)(2,1)S(1)} %pad_maximum_fusion.6, bf16[4,8192,512]{2,1,0:T(8,128)(2,1)} %refs_0_.1, f32[4096]{0:T(1024)S(1)} %bitcast.259), kind=kOutput, calls=%fused_computation.11 | convolution fusion | flops 1075838976 | bytes 12861440 | tf_op jit(solution)/shard_map/dot_general | solution.py:158
  118.5 5.9 %collective-permute-done.23 = f32[256,256]{1,0:T(8,128)S(1)} collective-permute-done((f32[256,256]{1,0:T(8,128)S(1)}, f32[256,256]{1,0:T(8,128)S(1)}, u32[]{:S(2)}, u32[]{:S(2)}) %collective-permute-start.23) | collective-permute-done | bytes 262176 | tf_op jit(solution)/shard_map/ppermute | solution.py:22
  125.1 2.8 %collective-permute-start.24 = (f32[256,256]{1,0:T(8,128)S(1)}, f32[256,256]{1,0:T(8,128)S(1)}, u32[]{:S(2)}, u32[]{:S(2)}) collective-permute-start(f32[256,256]{1,0:T(8,128)S(1)} %add.467), channel_id=1, source_target_pairs={{0,16},{8,24},{16,0},{24,8},{1,17},{9,25},{17,1},{25,9},{2,18},{10... | collective-permute-start | bytes 786440 | tf_op jit(solution)/shard_map/ppermute | solution.py:22
  127.9 5.6 %fusion.5 = f32[4096,256]{1,0:T(8,128)} fusion(f32[4096,256]{1,0:T(8,128)S(1)} %fusion.8, bf16[512,256]{1,0:T(8,128)(2,1)S(1)} %pad_maximum_fusion.6, bf16[4,8192,512]{2,1,0:T(8,128)(2,1)} %refs_0_.1, f32[4096]{0:T(1024)S(1)} %bitcast.258), kind=kOutput, calls=%fused_computation.8 | convolution fusion | flops 1075838976 | bytes 12861440 | tf_op jit(solution)/shard_map/dot_general | solution.py:158
  133.5 4.7 %collective-permute-done.25 = f32[256,256]{1,0:T(8,128)S(1)} collective-permute-done((f32[256,256]{1,0:T(8,128)S(1)}, f32[256,256]{1,0:T(8,128)S(1)}, u32[]{:S(2)}, u32[]{:S(2)}) %collective-permute-start.25) | collective-permute-done | bytes 262176 | tf_op jit(solution)/shard_map/ppermute | solution.py:22
  145.9 4.0 %last_rows.1 = (bf16[1024,512]{1,0:T(8,128)(2,1)S(1)}, bf16[1024,512]{1,0:T(8,128)(2,1)S(1)}, bf16[1024,512]{1,0:T(8,128)(2,1)S(1)}, bf16[1024,512]{1,0:T(8,128)...) custom-call(s32[8]{0:T(128)S(1)} %iota_xor_fusion.base, ...), custom_call_target="tpu_custom_call" | custom-call | tf_op jit(solution)/shard_map/last_rows/pallas_call | solution.py:118
  150.1 1.6 collective-permute-done.27
  153.9 1.6 collective-permute-start.28
  156.2 4.9 %collective-permute-done.28 = f32[256,256]{1,0:T(8,128)S(1)} collective-permute-done((f32[256,256]{1,0:T(8,128)S(1)}, f32[256,256]{1,0:T(8,128)S(1)}, u32[]{:S(2)}, u32[]{:S(2)}) %collective-permute-start.28) | collective-permute-done | bytes 262176 | tf_op jit(solution)/shard_map/ppermute | solution.py:22
  166.5 2.8 %collective-permute-start.33 = (f32[256,128]{1,0:T(8,128)S(1)}, f32[256,128]{1,0:T(8,128)S(1)}, u32[]{:S(2)}, u32[]{:S(2)}) collective-permute-start(f32[256,128]{1,0:T(8,128)S(1)} %fusion.66), channel_id=1, source_target_pairs={{0,8},{8,0},{16,24},{24,16},{1,9},{9,1},{17,25},{25,17},{2,10},{10... | collective-permute-start | bytes 393224 | tf_op jit(solution)/shard_map/ppermute | solution.py:22
  169.3 3.2 %fusion.3 = f32[4096,256]{1,0:T(8,128)S(1)} fusion(f32[4096,256]{1,0:T(8,128)S(1)} %copy-done.4, bf16[512,256]{1,0:T(8,128)(2,1)S(1)} %pad_maximum_fusion.7, bf16[4,8192,512]{2,1,0:T(8,128)(2,1)} %refs_0_.1, f32[4096]{0:T(1024)S(1)} %bitcast.257), kind=kOutput, calls=%fused_computation.5 | convolution fusion | flops 1075838976 | bytes 12861440 | tf_op jit(solution)/shard_map/dot_general | solution.py:158
  172.8 2.3 collective-permute-done.34
  175.7 2.0 collective-permute-start.37
  178.7 1.9 collective-permute-start.35
  180.6 3.3 %fusion.1 = f32[4096,256]{1,0:T(8,128)S(1)} fusion(f32[4096,256]{1,0:T(8,128)S(1)} %copy-done.3, bf16[512,256]{1,0:T(8,128)(2,1)S(1)} %pad_maximum_fusion.7, bf16[4,8192,512]{2,1,0:T(8,128)(2,1)} %refs_0_.1, f32[4096]{0:T(1024)S(1)} %bitcast.256), kind=kOutput, calls=%fused_computation.2 | convolution fusion | flops 1075838976 | bytes 12861440 | tf_op jit(solution)/shard_map/dot_general | solution.py:158
  183.9 4.6 %collective-permute-done.37 = f32[256,128]{1,0:T(8,128)S(1)} collective-permute-done((f32[256,128]{1,0:T(8,128)S(1)}, f32[256,128]{1,0:T(8,128)S(1)}, u32[]{:S(2)}, u32[]{:S(2)}) %collective-permute-start.37) | collective-permute-done | bytes 131104 | tf_op jit(solution)/shard_map/ppermute | solution.py:22
  190.3 2.0 collective-permute-start.39
  194.7 1.7 collective-permute-done.40
  196.4 2.0 collective-permute-done.39
  205.8 3.0 %collective-permute-done.56 = f32[512,128]{1,0:T(8,128)S(1)} collective-permute-done((f32[512,128]{1,0:T(8,128)S(1)}, f32[512,128]{1,0:T(8,128)S(1)}, u32[]{:S(2)}, u32[]{:S(2)}) %collective-permute-start.56) | collective-permute-done | bytes 262176 | tf_op jit(solution)/shard_map/ppermute | solution.py:22
  215.3 5.5 %collective-permute-done.57 = f32[512,128]{1,0:T(8,128)S(1)} collective-permute-done((f32[512,128]{1,0:T(8,128)S(1)}, f32[512,128]{1,0:T(8,128)S(1)}, u32[]{:S(2)}, u32[]{:S(2)}) %collective-permute-start.57) | collective-permute-done | bytes 262176 | tf_op jit(solution)/shard_map/ppermute | solution.py:22
  222.6 4.9 %collective-permute-done.59 = f32[512,128]{1,0:T(8,128)S(1)} collective-permute-done((f32[512,128]{1,0:T(8,128)S(1)}, f32[512,128]{1,0:T(8,128)S(1)}, u32[]{:S(2)}, u32[]{:S(2)}) %collective-permute-start.59) | collective-permute-done | bytes 262176 | tf_op jit(solution)/shard_map/ppermute | solution.py:22
  233.1 5.8 %collective-permute-done.60 = f32[512,128]{1,0:T(8,128)S(1)} collective-permute-done((f32[512,128]{1,0:T(8,128)S(1)}, f32[512,128]{1,0:T(8,128)S(1)}, u32[]{:S(2)}, u32[]{:S(2)}) %collective-permute-start.60) | collective-permute-done | bytes 262176 | tf_op jit(solution)/shard_map/ppermute | solution.py:22
  (277 shorter events, 71.2 us)
Async XLA Ops:
  2.3 16.1 %collective-permute-start.1 = (f32[256,256]{1,0:T(8,128)S(1)}, f32[256,256]{1,0:T(8,128)S(1)}, u32[]{:S(2)}, u32[]{:S(2)}) collective-permute-start(f32[256,256]{1,0:T(8,128)S(1)} %fusion.80), channel_id=1, source_target_pairs={{0,16},{8,24},{16,0},{24,8},{1,17},{9,25},{17,1},{25,9},{2,18},{10... | collective-permute-start | bytes 786440 | tf_op jit(solution)/shard_map/ppermute | solution.py:22
  8.1 12.3 %collective-permute-start = (f32[256,256]{1,0:T(8,128)S(1)}, f32[256,256]{1,0:T(8,128)S(1)}, u32[]{:S(2)}, u32[]{:S(2)}) collective-permute-start(f32[256,256]{1,0:T(8,128)S(1)} %fusion.82), channel_id=1, source_target_pairs={{0,8},{8,0},{16,24},{24,16},{1,9},{9,1},{17,25},{25,17},{2,10},{10... | collective-permute-start | bytes 786440 | tf_op jit(solution)/shard_map/ppermute | solution.py:22
  20.5 12.3 %collective-permute-start.3 = (f32[256,256]{1,0:T(8,128)S(1)}, f32[256,256]{1,0:T(8,128)S(1)}, u32[]{:S(2)}, u32[]{:S(2)}) collective-permute-start(f32[256,256]{1,0:T(8,128)S(1)} %add.433), channel_id=1, source_target_pairs={{0,8},{8,0},{16,24},{24,16},{1,9},{9,1},{17,25},{25,17},{2,10},{10... | collective-permute-start | bytes 786440 | tf_op jit(solution)/shard_map/ppermute | solution.py:22
  20.5 14.0 %collective-permute-start.2 = (f32[256,256]{1,0:T(8,128)S(1)}, f32[256,256]{1,0:T(8,128)S(1)}, u32[]{:S(2)}, u32[]{:S(2)}) collective-permute-start(f32[256,256]{1,0:T(8,128)S(1)} %add.432), channel_id=1, source_target_pairs={{0,16},{8,24},{16,0},{24,8},{1,17},{9,25},{17,1},{25,9},{2,18},{10... | collective-permute-start | bytes 786440 | tf_op jit(solution)/shard_map/ppermute | solution.py:22
  37.3 8.4 %collective-permute-start.5 = (f32[256,256]{1,0:T(8,128)S(1)}, f32[256,256]{1,0:T(8,128)S(1)}, u32[]{:S(2)}, u32[]{:S(2)}) collective-permute-start(f32[256,256]{1,0:T(8,128)S(1)} %get-tuple-element.207), channel_id=1, source_target_pairs={{0,2},{1,3},{2,0},{3,1},{4,6},{5,7},{6,4},{7,5},{8,10},{9,11},{10,... | collective-permute-start | bytes 786440 | tf_op jit(solution)/shard_map/ppermute | solution.py:22
  38.8 8.1 %collective-permute-start.7 = (f32[256,256]{1,0:T(8,128)S(1)}, f32[256,256]{1,0:T(8,128)S(1)}, u32[]{:S(2)}, u32[]{:S(2)}) collective-permute-start(f32[256,256]{1,0:T(8,128)S(1)} %get-tuple-element.208), channel_id=1, source_target_pairs={{0,4},{1,5},{2,6},{3,7},{4,0},{5,1},{6,2},{7,3},{8,12},{9,13},{10,... | collective-permute-start | bytes 786440 | tf_op jit(solution)/shard_map/ppermute | solution.py:22
  47.0 7.3 %collective-permute-start.6 = (f32[256,256]{1,0:T(8,128)S(1)}, f32[256,256]{1,0:T(8,128)S(1)}, u32[]{:S(2)}, u32[]{:S(2)}) collective-permute-start(f32[256,256]{1,0:T(8,128)S(1)} %get-tuple-element.205), channel_id=1, source_target_pairs={{0,4},{1,5},{2,6},{3,7},{4,0},{5,1},{6,2},{7,3},{8,12},{9,13},{10,... | collective-permute-start | bytes 786440 | tf_op jit(solution)/shard_map/ppermute | solution.py:22
  48.6 6.9 %collective-permute-start.8 = (f32[256,256]{1,0:T(8,128)S(1)}, f32[256,256]{1,0:T(8,128)S(1)}, u32[]{:S(2)}, u32[]{:S(2)}) collective-permute-start(f32[256,256]{1,0:T(8,128)S(1)} %get-tuple-element.206), channel_id=1, source_target_pairs={{0,2},{1,3},{2,0},{3,1},{4,6},{5,7},{6,4},{7,5},{8,10},{9,11},{10,... | collective-permute-start | bytes 786440 | tf_op jit(solution)/shard_map/ppermute | solution.py:22
  58.6 14.8 %collective-permute-start.12 = (f32[256,256]{1,0:T(8,128)S(1)}, f32[256,256]{1,0:T(8,128)S(1)}, u32[]{:S(2)}, u32[]{:S(2)}) collective-permute-start(f32[256,256]{1,0:T(8,128)S(1)} %fusion.62), channel_id=1, source_target_pairs={{0,16},{8,24},{16,0},{24,8},{1,17},{9,25},{17,1},{25,9},{2,18},{10... | collective-permute-start | bytes 786440 | tf_op jit(solution)/shard_map/ppermute | solution.py:22
  58.9 15.0 %collective-permute-start.11 = (f32[256,256]{1,0:T(8,128)S(1)}, f32[256,256]{1,0:T(8,128)S(1)}, u32[]{:S(2)}, u32[]{:S(2)}) collective-permute-start(f32[256,256]{1,0:T(8,128)S(1)} %fusion.60), channel_id=1, source_target_pairs={{0,8},{8,0},{16,24},{24,16},{1,9},{9,1},{17,25},{25,17},{2,10},{10... | collective-permute-start | bytes 786440 | tf_op jit(solution)/shard_map/ppermute | solution.py:22
  73.9 12.2 %collective-permute-start.14 = (f32[256,256]{1,0:T(8,128)S(1)}, f32[256,256]{1,0:T(8,128)S(1)}, u32[]{:S(2)}, u32[]{:S(2)}) collective-permute-start(f32[256,256]{1,0:T(8,128)S(1)} %add.450), channel_id=1, source_target_pairs={{0,8},{8,0},{16,24},{24,16},{1,9},{9,1},{17,25},{25,17},{2,10},{10... | collective-permute-start | bytes 786440 | tf_op jit(solution)/shard_map/ppermute | solution.py:22
  74.0 14.5 %collective-permute-start.13 = (f32[256,256]{1,0:T(8,128)S(1)}, f32[256,256]{1,0:T(8,128)S(1)}, u32[]{:S(2)}, u32[]{:S(2)}) collective-permute-start(f32[256,256]{1,0:T(8,128)S(1)} %add.449), channel_id=1, source_target_pairs={{0,16},{8,24},{16,0},{24,8},{1,17},{9,25},{17,1},{25,9},{2,18},{10... | collective-permute-start | bytes 786440 | tf_op jit(solution)/shard_map/ppermute | solution.py:22
  91.2 8.4 %collective-permute-start.16 = (f32[256,256]{1,0:T(8,128)S(1)}, f32[256,256]{1,0:T(8,128)S(1)}, u32[]{:S(2)}, u32[]{:S(2)}) collective-permute-start(f32[256,256]{1,0:T(8,128)S(1)} %get-tuple-element.203), channel_id=1, source_target_pairs={{0,2},{1,3},{2,0},{3,1},{4,6},{5,7},{6,4},{7,5},{8,10},{9,11},{10,... | collective-permute-start | bytes 786440 | tf_op jit(solution)/shard_map/ppermute | solution.py:22
  91.8 8.1 %collective-permute-start.18 = (f32[256,256]{1,0:T(8,128)S(1)}, f32[256,256]{1,0:T(8,128)S(1)}, u32[]{:S(2)}, u32[]{:S(2)}) collective-permute-start(f32[256,256]{1,0:T(8,128)S(1)} %get-tuple-element.204), channel_id=1, source_target_pairs={{0,4},{1,5},{2,6},{3,7},{4,0},{5,1},{6,2},{7,3},{8,12},{9,13},{10,... | collective-permute-start | bytes 786440 | tf_op jit(solution)/shard_map/ppermute | solution.py:22
  100.0 7.3 %collective-permute-start.17 = (f32[256,256]{1,0:T(8,128)S(1)}, f32[256,256]{1,0:T(8,128)S(1)}, u32[]{:S(2)}, u32[]{:S(2)}) collective-permute-start(f32[256,256]{1,0:T(8,128)S(1)} %get-tuple-element.201), channel_id=1, source_target_pairs={{0,4},{1,5},{2,6},{3,7},{4,0},{5,1},{6,2},{7,3},{8,12},{9,13},{10,... | collective-permute-start | bytes 786440 | tf_op jit(solution)/shard_map/ppermute | solution.py:22
  100.6 6.9 %collective-permute-start.19 = (f32[256,256]{1,0:T(8,128)S(1)}, f32[256,256]{1,0:T(8,128)S(1)}, u32[]{:S(2)}, u32[]{:S(2)}) collective-permute-start(f32[256,256]{1,0:T(8,128)S(1)} %get-tuple-element.202), channel_id=1, source_target_pairs={{0,2},{1,3},{2,0},{3,1},{4,6},{5,7},{6,4},{7,5},{8,10},{9,11},{10,... | collective-permute-start | bytes 786440 | tf_op jit(solution)/shard_map/ppermute | solution.py:22
  110.6 13.8 %collective-permute-start.23 = (f32[256,256]{1,0:T(8,128)S(1)}, f32[256,256]{1,0:T(8,128)S(1)}, u32[]{:S(2)}, u32[]{:S(2)}) collective-permute-start(f32[256,256]{1,0:T(8,128)S(1)} %fusion.58), channel_id=1, source_target_pairs={{0,16},{8,24},{16,0},{24,8},{1,17},{9,25},{17,1},{25,9},{2,18},{10... | collective-permute-start | bytes 786440 | tf_op jit(solution)/shard_map/ppermute | solution.py:22
  111.2 13.8 %collective-permute-start.22 = (f32[256,256]{1,0:T(8,128)S(1)}, f32[256,256]{1,0:T(8,128)S(1)}, u32[]{:S(2)}, u32[]{:S(2)}) collective-permute-start(f32[256,256]{1,0:T(8,128)S(1)} %fusion.56), channel_id=1, source_target_pairs={{0,8},{8,0},{16,24},{24,16},{1,9},{9,1},{17,25},{25,17},{2,10},{10... | collective-permute-start | bytes 786440 | tf_op jit(solution)/shard_map/ppermute | solution.py:22
  125.0 13.2 %collective-permute-start.25 = (f32[256,256]{1,0:T(8,128)S(1)}, f32[256,256]{1,0:T(8,128)S(1)}, u32[]{:S(2)}, u32[]{:S(2)}) collective-permute-start(f32[256,256]{1,0:T(8,128)S(1)} %add.468), channel_id=1, source_target_pairs={{0,8},{8,0},{16,24},{24,16},{1,9},{9,1},{17,25},{25,17},{2,10},{10... | collective-permute-start | bytes 786440 | tf_op jit(solution)/shard_map/ppermute | solution.py:22
  125.1 14.3 %collective-permute-start.24 = (f32[256,256]{1,0:T(8,128)S(1)}, f32[256,256]{1,0:T(8,128)S(1)}, u32[]{:S(2)}, u32[]{:S(2)}) collective-permute-start(f32[256,256]{1,0:T(8,128)S(1)} %add.467), channel_id=1, source_target_pairs={{0,16},{8,24},{16,0},{24,8},{1,17},{9,25},{17,1},{25,9},{2,18},{10... | collective-permute-start | bytes 786440 | tf_op jit(solution)/shard_map/ppermute | solution.py:22
  143.0 8.7 %collective-permute-start.27 = (f32[256,256]{1,0:T(8,128)}, f32[256,256]{1,0:T(8,128)}, u32[]{:S(2)}, u32[]{:S(2)}) collective-permute-start(f32[256,256]{1,0:T(8,128)} %get-tuple-element.199), channel_id=1, source_target_pairs={{0,2},{1,3},{2,0},{3,1},{4,6},{5,7},{6,4},{7,5},{8,10},{9,11},{10,... | collective-permute-start | bytes 786440 | tf_op jit(solution)/shard_map/ppermute | solution.py:22
  144.4 8.4 %collective-permute-start.29 = (f32[256,256]{1,0:T(8,128)}, f32[256,256]{1,0:T(8,128)}, u32[]{:S(2)}, u32[]{:S(2)}) collective-permute-start(f32[256,256]{1,0:T(8,128)} %get-tuple-element.200), channel_id=1, source_target_pairs={{0,4},{1,5},{2,6},{3,7},{4,0},{5,1},{6,2},{7,3},{8,12},{9,13},{10,... | collective-permute-start | bytes 786440 | tf_op jit(solution)/shard_map/ppermute | solution.py:22
  153.9 7.3 %collective-permute-start.28 = (f32[256,256]{1,0:T(8,128)S(1)}, f32[256,256]{1,0:T(8,128)S(1)}, u32[]{:S(2)}, u32[]{:S(2)}) collective-permute-start(f32[256,256]{1,0:T(8,128)S(1)} %get-tuple-element.197), channel_id=1, source_target_pairs={{0,4},{1,5},{2,6},{3,7},{4,0},{5,1},{6,2},{7,3},{8,12},{9,13},{10,... | collective-permute-start | bytes 786440 | tf_op jit(solution)/shard_map/ppermute | solution.py:22
  155.4 6.9 %collective-permute-start.30 = (f32[256,256]{1,0:T(8,128)S(1)}, f32[256,256]{1,0:T(8,128)S(1)}, u32[]{:S(2)}, u32[]{:S(2)}) collective-permute-start(f32[256,256]{1,0:T(8,128)S(1)} %get-tuple-element.198), channel_id=1, source_target_pairs={{0,2},{1,3},{2,0},{3,1},{4,6},{5,7},{6,4},{7,5},{8,10},{9,11},{10,... | collective-permute-start | bytes 786440 | tf_op jit(solution)/shard_map/ppermute | solution.py:22
  166.0 9.2 %collective-permute-start.34 = (f32[256,128]{1,0:T(8,128)S(1)}, f32[256,128]{1,0:T(8,128)S(1)}, u32[]{:S(2)}, u32[]{:S(2)}) collective-permute-start(f32[256,128]{1,0:T(8,128)S(1)} %fusion.63), channel_id=1, source_target_pairs={{0,16},{8,24},{16,0},{24,8},{1,17},{9,25},{17,1},{25,9},{2,18},{10... | collective-permute-start | bytes 393224 | tf_op jit(solution)/shard_map/ppermute | solution.py:22
  166.5 9.1 %collective-permute-start.33 = (f32[256,128]{1,0:T(8,128)S(1)}, f32[256,128]{1,0:T(8,128)S(1)}, u32[]{:S(2)}, u32[]{:S(2)}) collective-permute-start(f32[256,128]{1,0:T(8,128)S(1)} %fusion.66), channel_id=1, source_target_pairs={{0,8},{8,0},{16,24},{24,16},{1,9},{9,1},{17,25},{25,17},{2,10},{10... | collective-permute-start | bytes 393224 | tf_op jit(solution)/shard_map/ppermute | solution.py:22
  175.6 8.3 %collective-permute-start.38 = (f32[256,128]{1,0:T(8,128)S(1)}, f32[256,128]{1,0:T(8,128)S(1)}, u32[]{:S(2)}, u32[]{:S(2)}) collective-permute-start(f32[256,128]{1,0:T(8,128)S(1)} %add.497), channel_id=1, source_target_pairs={{0,8},{8,0},{16,24},{24,16},{1,9},{9,1},{17,25},{25,17},{2,10},{10... | collective-permute-start | bytes 393224 | tf_op jit(solution)/shard_map/ppermute | solution.py:22
  175.7 12.9 %collective-permute-start.37 = (f32[256,128]{1,0:T(8,128)S(1)}, f32[256,128]{1,0:T(8,128)S(1)}, u32[]{:S(2)}, u32[]{:S(2)}) collective-permute-start(f32[256,128]{1,0:T(8,128)S(1)} %add.496), channel_id=1, source_target_pairs={{0,16},{8,24},{16,0},{24,8},{1,17},{9,25},{17,1},{25,9},{2,18},{10... | collective-permute-start | bytes 393224 | tf_op jit(solution)/shard_map/ppermute | solution.py:22
  177.7 12.4 %collective-permute-start.36 = (f32[256,128]{1,0:T(8,128)S(1)}, f32[256,128]{1,0:T(8,128)S(1)}, u32[]{:S(2)}, u32[]{:S(2)}) collective-permute-start(f32[256,128]{1,0:T(8,128)S(1)} %fusion.65), channel_id=1, source_target_pairs={{0,16},{8,24},{16,0},{24,8},{1,17},{9,25},{17,1},{25,9},{2,18},{10... | collective-permute-start | bytes 393224 | tf_op jit(solution)/shard_map/ppermute | solution.py:22
  178.7 11.5 %collective-permute-start.35 = (f32[256,128]{1,0:T(8,128)S(1)}, f32[256,128]{1,0:T(8,128)S(1)}, u32[]{:S(2)}, u32[]{:S(2)}) collective-permute-start(f32[256,128]{1,0:T(8,128)S(1)} %fusion.64), channel_id=1, source_target_pairs={{0,8},{8,0},{16,24},{24,16},{1,9},{9,1},{17,25},{25,17},{2,10},{10... | collective-permute-start | bytes 393224 | tf_op jit(solution)/shard_map/ppermute | solution.py:22
  190.2 6.3 %collective-permute-start.40 = (f32[256,128]{1,0:T(8,128)S(1)}, f32[256,128]{1,0:T(8,128)S(1)}, u32[]{:S(2)}, u32[]{:S(2)}) collective-permute-start(f32[256,128]{1,0:T(8,128)S(1)} %add.508), channel_id=1, source_target_pairs={{0,8},{8,0},{16,24},{24,16},{1,9},{9,1},{17,25},{25,17},{2,10},{10... | collective-permute-start | bytes 393224 | tf_op jit(solution)/shard_map/ppermute | solution.py:22
  190.3 8.2 %collective-permute-start.39 = (f32[256,128]{1,0:T(8,128)S(1)}, f32[256,128]{1,0:T(8,128)S(1)}, u32[]{:S(2)}, u32[]{:S(2)}) collective-permute-start(f32[256,128]{1,0:T(8,128)S(1)} %add.507), channel_id=1, source_target_pairs={{0,16},{8,24},{16,0},{24,8},{1,17},{9,25},{17,1},{25,9},{2,18},{10... | collective-permute-start | bytes 393224 | tf_op jit(solution)/shard_map/ppermute | solution.py:22
  194.2 10.0 %collective-permute-start.45 = (f32[1024,128]{1,0:T(8,128)S(1)}, f32[1024,128]{1,0:T(8,128)S(1)}, u32[]{:S(2)}, u32[]{:S(2)}) collective-permute-start(f32[1024,128]{1,0:T(8,128)S(1)} %fusion.36), channel_id=1, source_target_pairs={{0,1},{1,0},{2,3},{3,2},{4,5},{5,4},{6,7},{7,6},{8,9},{9,8},{10,11... | collective-permute-start | bytes 1572872 | tf_op jit(solution)/shard_map/ppermute | solution.py:22
  199.5 9.3 %collective-permute-start.56 = (f32[512,128]{1,0:T(8,128)S(1)}, f32[512,128]{1,0:T(8,128)S(1)}, u32[]{:S(2)}, u32[]{:S(2)}) collective-permute-start(f32[512,128]{1,0:T(8,128)S(1)} %get-tuple-element.114), channel_id=1, source_target_pairs={{0,4},{1,5},{2,6},{3,7},{4,0},{5,1},{6,2},{7,3},{8,12},{9,13},{10,... | collective-permute-start | bytes 786440 | tf_op jit(solution)/shard_map/ppermute | solution.py:22
  200.6 13.1 %collective-permute-start.55 = (f32[512,128]{1,0:T(8,128)S(1)}, f32[512,128]{1,0:T(8,128)S(1)}, u32[]{:S(2)}, u32[]{:S(2)}) collective-permute-start(f32[512,128]{1,0:T(8,128)S(1)} %get-tuple-element.120), channel_id=1, source_target_pairs={{0,4},{1,5},{2,6},{3,7},{4,0},{5,1},{6,2},{7,3},{8,12},{9,13},{10,... | collective-permute-start | bytes 786440 | tf_op jit(solution)/shard_map/ppermute | solution.py:22
  202.1 7.3 %collective-permute-start.47 = (f32[512,128]{1,0:T(8,128)S(1)}, f32[512,128]{1,0:T(8,128)S(1)}, u32[]{:S(2)}, u32[]{:S(2)}) collective-permute-start(f32[512,128]{1,0:T(8,128)S(1)} %get-tuple-element.113), channel_id=1, source_target_pairs={{0,2},{1,3},{2,0},{3,1},{4,6},{5,7},{6,4},{7,5},{8,10},{9,11},{10,... | collective-permute-start | bytes 786440 | tf_op jit(solution)/shard_map/ppermute | solution.py:22
  203.2 6.3 %collective-permute-start.50 = (f32[1024,128]{1,0:T(8,128)S(1)}, f32[1024,128]{1,0:T(8,128)S(1)}, u32[]{:S(2)}, u32[]{:S(2)}) collective-permute-start(f32[1024,128]{1,0:T(8,128)S(1)} %fusion.42), channel_id=1, source_target_pairs={{0,1},{1,0},{2,3},{3,2},{4,5},{5,4},{6,7},{7,6},{8,9},{9,8},{10,11... | collective-permute-start | bytes 1572872 | tf_op jit(solution)/shard_map/ppermute | solution.py:22
  204.2 6.4 %collective-permute-start.44 = (f32[1024,128]{1,0:T(8,128)S(1)}, f32[1024,128]{1,0:T(8,128)S(1)}, u32[]{:S(2)}, u32[]{:S(2)}) collective-permute-start(f32[1024,128]{1,0:T(8,128)S(1)} %fusion.33), channel_id=1, source_target_pairs={{0,1},{1,0},{2,3},{3,2},{4,5},{5,4},{6,7},{7,6},{8,9},{9,8},{10,11... | collective-permute-start | bytes 1572872 | tf_op jit(solution)/shard_map/ppermute | solution.py:22
  208.8 19.3 %collective-permute-start.46 = (f32[512,128]{1,0:T(8,128)S(1)}, f32[512,128]{1,0:T(8,128)S(1)}, u32[]{:S(2)}, u32[]{:S(2)}) collective-permute-start(f32[512,128]{1,0:T(8,128)S(1)} %get-tuple-element.125), channel_id=1, source_target_pairs={{0,2},{1,3},{2,0},{3,1},{4,6},{5,7},{6,4},{7,5},{8,10},{9,11},{10,... | collective-permute-start | bytes 786440 | tf_op jit(solution)/shard_map/ppermute | solution.py:22
  209.6 11.9 %collective-permute-start.52 = (f32[1024,128]{1,0:T(8,128)S(1)}, f32[1024,128]{1,0:T(8,128)S(1)}, u32[]{:S(2)}, u32[]{:S(2)}) collective-permute-start(f32[1024,128]{1,0:T(8,128)S(1)} %fusion.45), channel_id=1, source_target_pairs={{0,1},{1,0},{2,3},{3,2},{4,5},{5,4},{6,7},{7,6},{8,9},{9,8},{10,11... | collective-permute-start | bytes 1572872 | tf_op jit(solution)/shard_map/ppermute | solution.py:22
  210.6 10.2 %collective-permute-start.57 = (f32[512,128]{1,0:T(8,128)S(1)}, f32[512,128]{1,0:T(8,128)S(1)}, u32[]{:S(2)}, u32[]{:S(2)}) collective-permute-start(f32[512,128]{1,0:T(8,128)S(1)} %add.558), channel_id=1, source_target_pairs={{0,2},{1,3},{2,0},{3,1},{4,6},{5,7},{6,4},{7,5},{8,10},{9,11},{10,... | collective-permute-start | bytes 786440 | tf_op jit(solution)/shard_map/ppermute | solution.py:22
  212.6 17.0 %collective-permute-start.48 = (f32[512,128]{1,0:T(8,128)S(1)}, f32[512,128]{1,0:T(8,128)S(1)}, u32[]{:S(2)}, u32[]{:S(2)}) collective-permute-start(f32[512,128]{1,0:T(8,128)S(1)} %add.543), channel_id=1, source_target_pairs={{0,4},{1,5},{2,6},{3,7},{4,0},{5,1},{6,2},{7,3},{8,12},{9,13},{10,... | collective-permute-start | bytes 786440 | tf_op jit(solution)/shard_map/ppermute | solution.py:22
  213.7 13.7 %collective-permute-start.59 = (f32[512,128]{1,0:T(8,128)S(1)}, f32[512,128]{1,0:T(8,128)S(1)}, u32[]{:S(2)}, u32[]{:S(2)}) collective-permute-start(f32[512,128]{1,0:T(8,128)S(1)} %get-tuple-element.145), channel_id=1, source_target_pairs={{0,4},{1,5},{2,6},{3,7},{4,0},{5,1},{6,2},{7,3},{8,12},{9,13},{10,... | collective-permute-start | bytes 786440 | tf_op jit(solution)/shard_map/ppermute | solution.py:22
  220.8 8.9 %collective-permute-start.53 = (f32[512,128]{1,0:T(8,128)S(1)}, f32[512,128]{1,0:T(8,128)S(1)}, u32[]{:S(2)}, u32[]{:S(2)}) collective-permute-start(f32[512,128]{1,0:T(8,128)S(1)} %get-tuple-element.129), channel_id=1, source_target_pairs={{0,2},{1,3},{2,0},{3,1},{4,6},{5,7},{6,4},{7,5},{8,10},{9,11},{10,... | collective-permute-start | bytes 786440 | tf_op jit(solution)/shard_map/ppermute | solution.py:22
  222.0 11.1 %collective-permute-start.58 = (f32[512,128]{1,0:T(8,128)S(1)}, f32[512,128]{1,0:T(8,128)S(1)}, u32[]{:S(2)}, u32[]{:S(2)}) collective-permute-start(f32[512,128]{1,0:T(8,128)S(1)} %get-tuple-element.143), channel_id=1, source_target_pairs={{0,4},{1,5},{2,6},{3,7},{4,0},{5,1},{6,2},{7,3},{8,12},{9,13},{10,... | collective-permute-start | bytes 786440 | tf_op jit(solution)/shard_map/ppermute | solution.py:22
  227.5 11.5 %collective-permute-start.51 = (f32[512,128]{1,0:T(8,128)S(1)}, f32[512,128]{1,0:T(8,128)S(1)}, u32[]{:S(2)}, u32[]{:S(2)}) collective-permute-start(f32[512,128]{1,0:T(8,128)S(1)} %get-tuple-element.139), channel_id=1, source_target_pairs={{0,2},{1,3},{2,0},{3,1},{4,6},{5,7},{6,4},{7,5},{8,10},{9,11},{10,... | collective-permute-start | bytes 786440 | tf_op jit(solution)/shard_map/ppermute | solution.py:22
  228.1 10.8 %collective-permute-start.60 = (f32[512,128]{1,0:T(8,128)S(1)}, f32[512,128]{1,0:T(8,128)S(1)}, u32[]{:S(2)}, u32[]{:S(2)}) collective-permute-start(f32[512,128]{1,0:T(8,128)S(1)} %add.561), channel_id=1, source_target_pairs={{0,2},{1,3},{2,0},{3,1},{4,6},{5,7},{6,4},{7,5},{8,10},{9,11},{10,... | collective-permute-start | bytes 786440 | tf_op jit(solution)/shard_map/ppermute | solution.py:22
  229.7 9.3 %collective-permute-start.54 = (f32[512,128]{1,0:T(8,128)S(1)}, f32[512,128]{1,0:T(8,128)S(1)}, u32[]{:S(2)}, u32[]{:S(2)}) collective-permute-start(f32[512,128]{1,0:T(8,128)S(1)} %add.555), channel_id=1, source_target_pairs={{0,4},{1,5},{2,6},{3,7},{4,0},{5,1},{6,2},{7,3},{8,12},{9,13},{10,... | collective-permute-start | bytes 786440 | tf_op jit(solution)/shard_map/ppermute | solution.py:22
  (37 other events, 206.1 us)

commit v6 on v5

--- a/solution.py
+++ b/solution.py
@@ -41,7 +41,7 @@
         got = [swap(p, axis, masks[(step + j) % len(masks)]) for j, p in enumerate(parts)]
         new = [p + g for p, g in zip(parts, got)]
         if queue:
-            new = lax.optimization_barrier((*new, queue.pop(0)(parts[-1])))[: len(new)]
+            new = lax.optimization_barrier((*new, *jax.tree.leaves(queue.pop(0)(parts[-1]))))[: len(new)]
         parts = list(new)
     return parts
 
@@ -146,7 +146,6 @@
     blocks = me ^ jnp.arange(n, dtype=jnp.int32)
     gain = jnp.repeat(window_mask.astype(F32), BLK, axis=1)
     gains = [half(gain, s, 1) for s in sides]
-    rhs = [None] + [[halves(half(rhs_window[t], s, 0)) for s in sides] for t in range(1, PANELS)]
     own = rhs_below.shape[0]
     rows = below_factor.shape[1] // 2
     below_gain = jnp.repeat(below_mask.astype(F32), BLK, axis=1)
@@ -162,7 +161,17 @@
 
     def couple_step(dep):
         store["couple"] = stage(after(sel, dep), couple, 1)
-        return store["couple"][0]
+        key = after(bit, dep)
+        rows_of = rhs_window.shape[1] // 2
+        cuts = [
+            lax.dynamic_slice(rhs_window, (t, s * rows_of, 0), (1, rows_of, rhs_window.shape[2]))[0]
+            for t in range(1, PANELS)
+            for s in (1 - key, key)
+        ]
+        cuts = lax.optimization_barrier(tuple(cuts))
+        for t in range(1, PANELS):
+            store["rhs", t] = [halves(x) for x in cuts[2 * t - 2 : 2 * t]]
+        return (store["couple"][0], *cuts)
 
     def dinv_step(dep):
         store["dinv"] = stage(after(sel, dep), dinv, 2)
@@ -217,12 +226,13 @@
     solutions, solved = [], []
     queue = [dinv_step, couple_step, last_step]
     for target in range(PANELS):
-        right = rhs[target]
+        rhs = store.get(("rhs", target))
+        right = rhs
         if target > 0:
             away = swap(update(target, 0, solved), "col", 1)
             home = sum_parts(halves(update(target, 1, solved) + away), "col", col_masks(), [])
             back = [swap(h, "col", 1) for h in home]
-            right = [[r - b for r, b in zip(rhs[target][0], back)], [r - h for r, h in zip(rhs[target][1], home)]]
+            right = [[r - b for r, b in zip(rhs[0], back)], [r - h for r, h in zip(rhs[1], home)]]
         if target == PANELS - 1:
             break
         if target == 0:

time: 241 us -> 241 us (level)
  waiting for transfers between devices: 115 us -> 111 us
  local copies, waits for them, and re-layouts: 7.89 us -> 11.8 us
    ppermute x61, waiting for transfers between devices: 115 us -> 111 us  [swap(): return lax.ppermute(x, axis, [(i, i ^ mask) for i in range(n)])]
    squeeze x0 -> x1, local copies, waits for them, and re-layouts: none -> 3 us  [couple_step(): lax.dynamic_slice(rhs_window, (t, s * rows_of, 0), (1, rows_of, rhs_windo...]
  transfers between devices with their start and end apart: 61 -> 61, of which waited for: 44 -> 44; matrix products, arithmetic and copies ran while one was open for 18% -> 20% of each run, Pallas kernels for 3% -> 3%
where the time goes in v6:
time: 241 us; the launch traced here: 240 us
  waiting for transfers between devices  111 us (46%)
  starting transfers between devices  57.4 us (24%)
  matrix products  43.7 us (18%)
  local copies, waits for them, and re-layouts  11.8 us (5%)
  Pallas kernels  7.59 us (3%)
  other arithmetic  7.35 us (3%)
    ppermute x61, waiting for transfers between devices, swap(): return lax.ppermute(x, axis, [(i, i ^ mask) for i in range(n)])  111 us
    ppermute x61, starting transfers between devices, swap(): return lax.ppermute(x, axis, [(i, i ^ mask) for i in range(n)])  57.4 us
    dot_general x6, matrix products, early_step(): term = jnp.dot(factor, after(solved, dep), preferred_element_type=F32)  23.8 us
    dot_general x16, matrix products, tail(): term = jnp.dot(store['last'][q], solved, preferred_element_type=F32)  7.15 us
    dot_general x32, matrix products, inverse_dots(): jnp.dot(block, right[side][k].astype(BF16), preferred_element_type=F32)  5.67 us
  transfers between devices with their start and end apart: 61, of which 44 were waited for; matrix products, arithmetic and copies ran while one was open for 20% of the time, Pallas kernels for 3%

profile of v6, /device:TPU:0, one launch (start us, length us, event | category | flops | bytes accessed | tf_op | source)
XLA Modules:
  0.0 240.3 jit_solution(6345337253246406919)
XLA Ops:
  0.6 1.7 fusion.80
  2.3 4.1 %collective-permute-start.1 = (f32[256,256]{1,0:T(8,128)S(1)}, f32[256,256]{1,0:T(8,128)S(1)}, u32[]{:S(2)}, u32[]{:S(2)}) collective-permute-start(f32[256,256]{1,0:T(8,128)S(1)} %fusion.80), channel_id=1, source_target_pairs={{0,16},{8,24},{16,0},{24,8},{1,17},{9,25},{17,1},{25,9},{2,18},{10... | collective-permute-start | bytes 786440 | tf_op jit(solution)/shard_map/ppermute | solution.py:22
  6.4 1.7 fusion.82
  8.1 1.6 collective-permute-start
  10.6 2.2 copy-done
  15.5 3.0 %collective-permute-done.1 = f32[256,256]{1,0:T(8,128)S(1)} collective-permute-done((f32[256,256]{1,0:T(8,128)S(1)}, f32[256,256]{1,0:T(8,128)S(1)}, u32[]{:S(2)}, u32[]{:S(2)}) %collective-permute-start.1) | collective-permute-done | bytes 262176 | tf_op jit(solution)/shard_map/ppermute | solution.py:22
  18.5 1.9 collective-permute-done
  20.6 3.0 %collective-permute-start.2 = (f32[256,256]{1,0:T(8,128)S(1)}, f32[256,256]{1,0:T(8,128)S(1)}, u32[]{:S(2)}, u32[]{:S(2)}) collective-permute-start(f32[256,256]{1,0:T(8,128)S(1)} %add.436), channel_id=1, source_target_pairs={{0,16},{8,24},{16,0},{24,8},{1,17},{9,25},{17,1},{25,9},{2,18},{10... | collective-permute-start | bytes 786440 | tf_op jit(solution)/shard_map/ppermute | solution.py:22
  25.1 3.0 %dynamic-slice_bitcast_fusion = (f32[512,256]{1,0:T(8,128)}, f32[512,256]{1,0:T(8,128)S(1)}, f32[512,256]{1,0:T(8,128)S(1)}, f32[512,256]{1,0:T(8,128)S(1)}, f32[512,256]{1,0:T(8,128)S(1)}, /*index=5*/f32[512,256]{1,0:T(8,128)}) fusion(f32[4,1024,256]{2,1,0:T(8,128)} %param.7, s32[]{:T(128)S(6)} %select_n.222, s32[]{:T(128)S(6)} %select_n.221), kind=kLoop, calls=%fused_computation.157 | loop fusion | bytes 6291464 | tf_op jit(solution)/shard_map/squeeze | solution.py:167
  28.1 3.0 %stage.3 = (bf16[6,512,512]{2,1,0:T(8,128)(2,1)S(1)}, bf16[6,512,512]{2,1,0:T(8,128)(2,1)S(1)}) custom-call(s32[1]{0:T(128)} %bitcast.3.sel, bf16[6,1024,512]{2,1,0:T(8,128)(2,1)} %x_ref.3), custom_call_target="tpu_custom_call" | custom-call | tf_op jit(solution)/shard_map/stage/pallas_call | solution.py:87
  31.1 1.8 collective-permute-done.3
  40.5 5.2 %collective-permute-done.5 = f32[256,256]{1,0:T(8,128)S(1)} collective-permute-done((f32[256,256]{1,0:T(8,128)S(1)}, f32[256,256]{1,0:T(8,128)S(1)}, u32[]{:S(2)}, u32[]{:S(2)}) %collective-permute-start.5) | collective-permute-done | bytes 262176 | tf_op jit(solution)/shard_map/ppermute | solution.py:22
  49.4 4.8 %collective-permute-done.6 = f32[256,256]{1,0:T(8,128)S(1)} collective-permute-done((f32[256,256]{1,0:T(8,128)S(1)}, f32[256,256]{1,0:T(8,128)S(1)}, u32[]{:S(2)}, u32[]{:S(2)}) %collective-permute-start.6) | collective-permute-done | bytes 262176 | tf_op jit(solution)/shard_map/ppermute | solution.py:22
  58.9 3.0 %collective-permute-start.11 = (f32[256,256]{1,0:T(8,128)S(1)}, f32[256,256]{1,0:T(8,128)S(1)}, u32[]{:S(2)}, u32[]{:S(2)}) collective-permute-start(f32[256,256]{1,0:T(8,128)S(1)} %fusion.60), channel_id=1, source_target_pairs={{0,8},{8,0},{16,24},{24,16},{1,9},{9,1},{17,25},{25,17},{2,10},{10... | collective-permute-start | bytes 786440 | tf_op jit(solution)/shard_map/ppermute | solution.py:22
  62.0 3.0 %fusion.9 = f32[4096,256]{1,0:T(8,128)S(1)} fusion(bf16[512,256]{1,0:T(8,128)(2,1)S(1)} %pad_maximum_fusion.5, bf16[4,8192,512]{2,1,0:T(8,128)(2,1)} %refs_0_.1, f32[4096]{0:T(1024)S(1)} %bitcast.202), kind=kOutput, calls=%fused_computation.15 | convolution fusion | flops 1074790400 | bytes 8667136 | tf_op jit(solution)/shard_map/dot_general | solution.py:157
  65.0 8.4 %collective-permute-done.12 = f32[256,256]{1,0:T(8,128)S(1)} collective-permute-done((f32[256,256]{1,0:T(8,128)S(1)}, f32[256,256]{1,0:T(8,128)S(1)}, u32[]{:S(2)}, u32[]{:S(2)}) %collective-permute-start.12) | collective-permute-done | bytes 262176 | tf_op jit(solution)/shard_map/ppermute | solution.py:22
  74.0 2.1 collective-permute-start.13
  76.1 3.2 %fusion.8 = f32[4096,256]{1,0:T(8,128)S(1)} fusion(bf16[512,256]{1,0:T(8,128)(2,1)S(1)} %pad_maximum_fusion.5, bf16[4,8192,512]{2,1,0:T(8,128)(2,1)} %refs_0_.1, f32[4096]{0:T(1024)S(1)} %bitcast.201), kind=kOutput, calls=%fused_computation.13 | convolution fusion | flops 1074790400 | bytes 8667136 | tf_op jit(solution)/shard_map/dot_general | solution.py:157
  79.3 6.9 %collective-permute-done.14 = f32[256,256]{1,0:T(8,128)S(1)} collective-permute-done((f32[256,256]{1,0:T(8,128)S(1)}, f32[256,256]{1,0:T(8,128)S(1)}, u32[]{:S(2)}, u32[]{:S(2)}) %collective-permute-start.14) | collective-permute-done | bytes 262176 | tf_op jit(solution)/shard_map/ppermute | solution.py:22
  86.2 2.3 collective-permute-done.13
  92.7 6.9 %collective-permute-done.16 = f32[256,256]{1,0:T(8,128)S(1)} collective-permute-done((f32[256,256]{1,0:T(8,128)S(1)}, f32[256,256]{1,0:T(8,128)S(1)}, u32[]{:S(2)}, u32[]{:S(2)}) %collective-permute-start.16) | collective-permute-done | bytes 262176 | tf_op jit(solution)/shard_map/ppermute | solution.py:22
  102.3 5.0 %collective-permute-done.17 = f32[256,256]{1,0:T(8,128)S(1)} collective-permute-done((f32[256,256]{1,0:T(8,128)S(1)}, f32[256,256]{1,0:T(8,128)S(1)}, u32[]{:S(2)}, u32[]{:S(2)}) %collective-permute-start.17) | collective-permute-done | bytes 262176 | tf_op jit(solution)/shard_map/ppermute | solution.py:22
  111.2 1.8 collective-permute-start.22
  113.0 5.5 %fusion.7 = f32[4096,256]{1,0:T(8,128)} fusion(f32[4096,256]{1,0:T(8,128)S(1)} %fusion.9, bf16[512,256]{1,0:T(8,128)(2,1)S(1)} %pad_maximum_fusion.6, bf16[4,8192,512]{2,1,0:T(8,128)(2,1)} %refs_0_.1, f32[4096]{0:T(1024)S(1)} %bitcast.199), kind=kOutput, calls=%fused_computation.11 | convolution fusion | flops 1075838976 | bytes 12861440 | tf_op jit(solution)/shard_map/dot_general | solution.py:157
  118.5 6.0 %collective-permute-done.23 = f32[256,256]{1,0:T(8,128)S(1)} collective-permute-done((f32[256,256]{1,0:T(8,128)S(1)}, f32[256,256]{1,0:T(8,128)S(1)}, u32[]{:S(2)}, u32[]{:S(2)}) %collective-permute-start.23) | collective-permute-done | bytes 262176 | tf_op jit(solution)/shard_map/ppermute | solution.py:22
  125.1 2.8 %collective-permute-start.24 = (f32[256,256]{1,0:T(8,128)S(1)}, f32[256,256]{1,0:T(8,128)S(1)}, u32[]{:S(2)}, u32[]{:S(2)}) collective-permute-start(f32[256,256]{1,0:T(8,128)S(1)} %add.473), channel_id=1, source_target_pairs={{0,16},{8,24},{16,0},{24,8},{1,17},{9,25},{17,1},{25,9},{2,18},{10... | collective-permute-start | bytes 786440 | tf_op jit(solution)/shard_map/ppermute | solution.py:22
  128.0 5.5 %fusion.5 = f32[4096,256]{1,0:T(8,128)} fusion(f32[4096,256]{1,0:T(8,128)S(1)} %fusion.8, bf16[512,256]{1,0:T(8,128)(2,1)S(1)} %pad_maximum_fusion.6, bf16[4,8192,512]{2,1,0:T(8,128)(2,1)} %refs_0_.1, f32[4096]{0:T(1024)S(1)} %bitcast.198), kind=kOutput, calls=%fused_computation.8 | convolution fusion | flops 1075838976 | bytes 12861440 | tf_op jit(solution)/shard_map/dot_general | solution.py:157
  133.5 4.7 %collective-permute-done.25 = f32[256,256]{1,0:T(8,128)S(1)} collective-permute-done((f32[256,256]{1,0:T(8,128)S(1)}, f32[256,256]{1,0:T(8,128)S(1)}, u32[]{:S(2)}, u32[]{:S(2)}) %collective-permute-start.25) | collective-permute-done | bytes 262176 | tf_op jit(solution)/shard_map/ppermute | solution.py:22
  146.0 4.0 %last_rows.1 = (bf16[1024,512]{1,0:T(8,128)(2,1)S(1)}, bf16[1024,512]{1,0:T(8,128)(2,1)S(1)}, bf16[1024,512]{1,0:T(8,128)(2,1)S(1)}, bf16[1024,512]{1,0:T(8,128)...) custom-call(s32[8]{0:T(128)S(1)} %iota_xor_fusion.base, ...), custom_call_target="tpu_custom_call" | custom-call | tf_op jit(solution)/shard_map/last_rows/pallas_call | solution.py:118
  150.1 1.6 collective-permute-done.27
  153.9 1.6 collective-permute-start.28
  156.2 4.9 %collective-permute-done.28 = f32[256,256]{1,0:T(8,128)S(1)} collective-permute-done((f32[256,256]{1,0:T(8,128)S(1)}, f32[256,256]{1,0:T(8,128)S(1)}, u32[]{:S(2)}, u32[]{:S(2)}) %collective-permute-start.28) | collective-permute-done | bytes 262176 | tf_op jit(solution)/shard_map/ppermute | solution.py:22
  166.5 2.8 %collective-permute-start.33 = (f32[256,128]{1,0:T(8,128)S(1)}, f32[256,128]{1,0:T(8,128)S(1)}, u32[]{:S(2)}, u32[]{:S(2)}) collective-permute-start(f32[256,128]{1,0:T(8,128)S(1)} %fusion.66), channel_id=1, source_target_pairs={{0,8},{8,0},{16,24},{24,16},{1,9},{9,1},{17,25},{25,17},{2,10},{10... | collective-permute-start | bytes 393224 | tf_op jit(solution)/shard_map/ppermute | solution.py:22
  169.4 3.2 %fusion.3 = f32[4096,256]{1,0:T(8,128)S(1)} fusion(f32[4096,256]{1,0:T(8,128)S(1)} %copy-done.4, bf16[512,256]{1,0:T(8,128)(2,1)S(1)} %pad_maximum_fusion.7, bf16[4,8192,512]{2,1,0:T(8,128)(2,1)} %refs_0_.1, f32[4096]{0:T(1024)S(1)} %bitcast.197), kind=kOutput, calls=%fused_computation.5 | convolution fusion | flops 1075838976 | bytes 12861440 | tf_op jit(solution)/shard_map/dot_general | solution.py:157
  172.9 2.3 collective-permute-done.34
  175.7 2.1 collective-permute-start.37
  178.7 1.9 collective-permute-start.35
  180.7 3.3 %fusion.1 = f32[4096,256]{1,0:T(8,128)S(1)} fusion(f32[4096,256]{1,0:T(8,128)S(1)} %copy-done.3, bf16[512,256]{1,0:T(8,128)(2,1)S(1)} %pad_maximum_fusion.7, bf16[4,8192,512]{2,1,0:T(8,128)(2,1)} %refs_0_.1, f32[4096]{0:T(1024)S(1)} %bitcast.196), kind=kOutput, calls=%fused_computation.2 | convolution fusion | flops 1075838976 | bytes 12861440 | tf_op jit(solution)/shard_map/dot_general | solution.py:157
  184.0 4.6 %collective-permute-done.37 = f32[256,128]{1,0:T(8,128)S(1)} collective-permute-done((f32[256,128]{1,0:T(8,128)S(1)}, f32[256,128]{1,0:T(8,128)S(1)}, u32[]{:S(2)}, u32[]{:S(2)}) %collective-permute-start.37) | collective-permute-done | bytes 131104 | tf_op jit(solution)/shard_map/ppermute | solution.py:22
  190.3 1.9 collective-permute-start.39
  194.8 1.7 collective-permute-done.40
  196.5 2.0 collective-permute-done.39
  200.6 1.6 collective-permute-start.55
  205.9 3.0 %collective-permute-done.56 = f32[512,128]{1,0:T(8,128)S(1)} collective-permute-done((f32[512,128]{1,0:T(8,128)S(1)}, f32[512,128]{1,0:T(8,128)S(1)}, u32[]{:S(2)}, u32[]{:S(2)}) %collective-permute-start.56) | collective-permute-done | bytes 262176 | tf_op jit(solution)/shard_map/ppermute | solution.py:22
  213.8 1.6 collective-permute-start.59
  215.4 5.5 %collective-permute-done.57 = f32[512,128]{1,0:T(8,128)S(1)} collective-permute-done((f32[512,128]{1,0:T(8,128)S(1)}, f32[512,128]{1,0:T(8,128)S(1)}, u32[]{:S(2)}, u32[]{:S(2)}) %collective-permute-start.57) | collective-permute-done | bytes 262176 | tf_op jit(solution)/shard_map/ppermute | solution.py:22
  222.6 5.0 %collective-permute-done.59 = f32[512,128]{1,0:T(8,128)S(1)} collective-permute-done((f32[512,128]{1,0:T(8,128)S(1)}, f32[512,128]{1,0:T(8,128)S(1)}, u32[]{:S(2)}, u32[]{:S(2)}) %collective-permute-start.59) | collective-permute-done | bytes 262176 | tf_op jit(solution)/shard_map/ppermute | solution.py:22
  233.2 5.8 %collective-permute-done.60 = f32[512,128]{1,0:T(8,128)S(1)} collective-permute-done((f32[512,128]{1,0:T(8,128)S(1)}, f32[512,128]{1,0:T(8,128)S(1)}, u32[]{:S(2)}, u32[]{:S(2)}) %collective-permute-start.60) | collective-permute-done | bytes 262176 | tf_op jit(solution)/shard_map/ppermute | solution.py:22
  (263 shorter events, 73.6 us)
Async XLA Ops:
  2.3 16.1 %collective-permute-start.1 = (f32[256,256]{1,0:T(8,128)S(1)}, f32[256,256]{1,0:T(8,128)S(1)}, u32[]{:S(2)}, u32[]{:S(2)}) collective-permute-start(f32[256,256]{1,0:T(8,128)S(1)} %fusion.80), channel_id=1, source_target_pairs={{0,16},{8,24},{16,0},{24,8},{1,17},{9,25},{17,1},{25,9},{2,18},{10... | collective-permute-start | bytes 786440 | tf_op jit(solution)/shard_map/ppermute | solution.py:22
  8.1 12.3 %collective-permute-start = (f32[256,256]{1,0:T(8,128)S(1)}, f32[256,256]{1,0:T(8,128)S(1)}, u32[]{:S(2)}, u32[]{:S(2)}) collective-permute-start(f32[256,256]{1,0:T(8,128)S(1)} %fusion.82), channel_id=1, source_target_pairs={{0,8},{8,0},{16,24},{24,16},{1,9},{9,1},{17,25},{25,17},{2,10},{10... | collective-permute-start | bytes 786440 | tf_op jit(solution)/shard_map/ppermute | solution.py:22
  20.5 12.4 %collective-permute-start.3 = (f32[256,256]{1,0:T(8,128)S(1)}, f32[256,256]{1,0:T(8,128)}, u32[]{:S(2)}, u32[]{:S(2)}) collective-permute-start(f32[256,256]{1,0:T(8,128)S(1)} %add.437), channel_id=1, source_target_pairs={{0,8},{8,0},{16,24},{24,16},{1,9},{9,1},{17,25},{25,17},{2,10},{10... | collective-permute-start | bytes 786440 | tf_op jit(solution)/shard_map/ppermute | solution.py:22
  20.6 14.0 %collective-permute-start.2 = (f32[256,256]{1,0:T(8,128)S(1)}, f32[256,256]{1,0:T(8,128)S(1)}, u32[]{:S(2)}, u32[]{:S(2)}) collective-permute-start(f32[256,256]{1,0:T(8,128)S(1)} %add.436), channel_id=1, source_target_pairs={{0,16},{8,24},{16,0},{24,8},{1,17},{9,25},{17,1},{25,9},{2,18},{10... | collective-permute-start | bytes 786440 | tf_op jit(solution)/shard_map/ppermute | solution.py:22
  37.3 8.4 %collective-permute-start.5 = (f32[256,256]{1,0:T(8,128)S(1)}, f32[256,256]{1,0:T(8,128)S(1)}, u32[]{:S(2)}, u32[]{:S(2)}) collective-permute-start(f32[256,256]{1,0:T(8,128)S(1)} %get-tuple-element.224), channel_id=1, source_target_pairs={{0,2},{1,3},{2,0},{3,1},{4,6},{5,7},{6,4},{7,5},{8,10},{9,11},{10,... | collective-permute-start | bytes 786440 | tf_op jit(solution)/shard_map/ppermute | solution.py:22
  38.8 8.1 %collective-permute-start.7 = (f32[256,256]{1,0:T(8,128)S(1)}, f32[256,256]{1,0:T(8,128)S(1)}, u32[]{:S(2)}, u32[]{:S(2)}) collective-permute-start(f32[256,256]{1,0:T(8,128)S(1)} %get-tuple-element.225), channel_id=1, source_target_pairs={{0,4},{1,5},{2,6},{3,7},{4,0},{5,1},{6,2},{7,3},{8,12},{9,13},{10,... | collective-permute-start | bytes 786440 | tf_op jit(solution)/shard_map/ppermute | solution.py:22
  47.0 7.3 %collective-permute-start.6 = (f32[256,256]{1,0:T(8,128)S(1)}, f32[256,256]{1,0:T(8,128)S(1)}, u32[]{:S(2)}, u32[]{:S(2)}) collective-permute-start(f32[256,256]{1,0:T(8,128)S(1)} %get-tuple-element.222), channel_id=1, source_target_pairs={{0,4},{1,5},{2,6},{3,7},{4,0},{5,1},{6,2},{7,3},{8,12},{9,13},{10,... | collective-permute-start | bytes 786440 | tf_op jit(solution)/shard_map/ppermute | solution.py:22
  48.6 6.9 %collective-permute-start.8 = (f32[256,256]{1,0:T(8,128)S(1)}, f32[256,256]{1,0:T(8,128)S(1)}, u32[]{:S(2)}, u32[]{:S(2)}) collective-permute-start(f32[256,256]{1,0:T(8,128)S(1)} %get-tuple-element.223), channel_id=1, source_target_pairs={{0,2},{1,3},{2,0},{3,1},{4,6},{5,7},{6,4},{7,5},{8,10},{9,11},{10,... | collective-permute-start | bytes 786440 | tf_op jit(solution)/shard_map/ppermute | solution.py:22
  58.6 14.8 %collective-permute-start.12 = (f32[256,256]{1,0:T(8,128)S(1)}, f32[256,256]{1,0:T(8,128)S(1)}, u32[]{:S(2)}, u32[]{:S(2)}) collective-permute-start(f32[256,256]{1,0:T(8,128)S(1)} %fusion.62), channel_id=1, source_target_pairs={{0,16},{8,24},{16,0},{24,8},{1,17},{9,25},{17,1},{25,9},{2,18},{10... | collective-permute-start | bytes 786440 | tf_op jit(solution)/shard_map/ppermute | solution.py:22
  58.9 15.0 %collective-permute-start.11 = (f32[256,256]{1,0:T(8,128)S(1)}, f32[256,256]{1,0:T(8,128)S(1)}, u32[]{:S(2)}, u32[]{:S(2)}) collective-permute-start(f32[256,256]{1,0:T(8,128)S(1)} %fusion.60), channel_id=1, source_target_pairs={{0,8},{8,0},{16,24},{24,16},{1,9},{9,1},{17,25},{25,17},{2,10},{10... | collective-permute-start | bytes 786440 | tf_op jit(solution)/shard_map/ppermute | solution.py:22
  73.9 12.2 %collective-permute-start.14 = (f32[256,256]{1,0:T(8,128)S(1)}, f32[256,256]{1,0:T(8,128)S(1)}, u32[]{:S(2)}, u32[]{:S(2)}) collective-permute-start(f32[256,256]{1,0:T(8,128)S(1)} %add.456), channel_id=1, source_target_pairs={{0,8},{8,0},{16,24},{24,16},{1,9},{9,1},{17,25},{25,17},{2,10},{10... | collective-permute-start | bytes 786440 | tf_op jit(solution)/shard_map/ppermute | solution.py:22
  74.0 14.5 %collective-permute-start.13 = (f32[256,256]{1,0:T(8,128)S(1)}, f32[256,256]{1,0:T(8,128)S(1)}, u32[]{:S(2)}, u32[]{:S(2)}) collective-permute-start(f32[256,256]{1,0:T(8,128)S(1)} %add.455), channel_id=1, source_target_pairs={{0,16},{8,24},{16,0},{24,8},{1,17},{9,25},{17,1},{25,9},{2,18},{10... | collective-permute-start | bytes 786440 | tf_op jit(solution)/shard_map/ppermute | solution.py:22
  91.2 8.4 %collective-permute-start.16 = (f32[256,256]{1,0:T(8,128)S(1)}, f32[256,256]{1,0:T(8,128)S(1)}, u32[]{:S(2)}, u32[]{:S(2)}) collective-permute-start(f32[256,256]{1,0:T(8,128)S(1)} %get-tuple-element.216), channel_id=1, source_target_pairs={{0,2},{1,3},{2,0},{3,1},{4,6},{5,7},{6,4},{7,5},{8,10},{9,11},{10,... | collective-permute-start | bytes 786440 | tf_op jit(solution)/shard_map/ppermute | solution.py:22
  91.9 8.1 %collective-permute-start.18 = (f32[256,256]{1,0:T(8,128)S(1)}, f32[256,256]{1,0:T(8,128)S(1)}, u32[]{:S(2)}, u32[]{:S(2)}) collective-permute-start(f32[256,256]{1,0:T(8,128)S(1)} %get-tuple-element.217), channel_id=1, source_target_pairs={{0,4},{1,5},{2,6},{3,7},{4,0},{5,1},{6,2},{7,3},{8,12},{9,13},{10,... | collective-permute-start | bytes 786440 | tf_op jit(solution)/shard_map/ppermute | solution.py:22
  100.0 7.3 %collective-permute-start.17 = (f32[256,256]{1,0:T(8,128)S(1)}, f32[256,256]{1,0:T(8,128)S(1)}, u32[]{:S(2)}, u32[]{:S(2)}) collective-permute-start(f32[256,256]{1,0:T(8,128)S(1)} %get-tuple-element.214), channel_id=1, source_target_pairs={{0,4},{1,5},{2,6},{3,7},{4,0},{5,1},{6,2},{7,3},{8,12},{9,13},{10,... | collective-permute-start | bytes 786440 | tf_op jit(solution)/shard_map/ppermute | solution.py:22
  100.6 6.9 %collective-permute-start.19 = (f32[256,256]{1,0:T(8,128)S(1)}, f32[256,256]{1,0:T(8,128)S(1)}, u32[]{:S(2)}, u32[]{:S(2)}) collective-permute-start(f32[256,256]{1,0:T(8,128)S(1)} %get-tuple-element.215), channel_id=1, source_target_pairs={{0,2},{1,3},{2,0},{3,1},{4,6},{5,7},{6,4},{7,5},{8,10},{9,11},{10,... | collective-permute-start | bytes 786440 | tf_op jit(solution)/shard_map/ppermute | solution.py:22
  110.7 13.8 %collective-permute-start.23 = (f32[256,256]{1,0:T(8,128)S(1)}, f32[256,256]{1,0:T(8,128)S(1)}, u32[]{:S(2)}, u32[]{:S(2)}) collective-permute-start(f32[256,256]{1,0:T(8,128)S(1)} %fusion.58), channel_id=1, source_target_pairs={{0,16},{8,24},{16,0},{24,8},{1,17},{9,25},{17,1},{25,9},{2,18},{10... | collective-permute-start | bytes 786440 | tf_op jit(solution)/shard_map/ppermute | solution.py:22
  111.2 13.8 %collective-permute-start.22 = (f32[256,256]{1,0:T(8,128)S(1)}, f32[256,256]{1,0:T(8,128)S(1)}, u32[]{:S(2)}, u32[]{:S(2)}) collective-permute-start(f32[256,256]{1,0:T(8,128)S(1)} %fusion.56), channel_id=1, source_target_pairs={{0,8},{8,0},{16,24},{24,16},{1,9},{9,1},{17,25},{25,17},{2,10},{10... | collective-permute-start | bytes 786440 | tf_op jit(solution)/shard_map/ppermute | solution.py:22
  125.0 13.2 %collective-permute-start.25 = (f32[256,256]{1,0:T(8,128)S(1)}, f32[256,256]{1,0:T(8,128)S(1)}, u32[]{:S(2)}, u32[]{:S(2)}) collective-permute-start(f32[256,256]{1,0:T(8,128)S(1)} %add.474), channel_id=1, source_target_pairs={{0,8},{8,0},{16,24},{24,16},{1,9},{9,1},{17,25},{25,17},{2,10},{10... | collective-permute-start | bytes 786440 | tf_op jit(solution)/shard_map/ppermute | solution.py:22
  125.1 14.3 %collective-permute-start.24 = (f32[256,256]{1,0:T(8,128)S(1)}, f32[256,256]{1,0:T(8,128)S(1)}, u32[]{:S(2)}, u32[]{:S(2)}) collective-permute-start(f32[256,256]{1,0:T(8,128)S(1)} %add.473), channel_id=1, source_target_pairs={{0,16},{8,24},{16,0},{24,8},{1,17},{9,25},{17,1},{25,9},{2,18},{10... | collective-permute-start | bytes 786440 | tf_op jit(solution)/shard_map/ppermute | solution.py:22
  143.0 8.7 %collective-permute-start.27 = (f32[256,256]{1,0:T(8,128)}, f32[256,256]{1,0:T(8,128)}, u32[]{:S(2)}, u32[]{:S(2)}) collective-permute-start(f32[256,256]{1,0:T(8,128)} %get-tuple-element.208), channel_id=1, source_target_pairs={{0,2},{1,3},{2,0},{3,1},{4,6},{5,7},{6,4},{7,5},{8,10},{9,11},{10,... | collective-permute-start | bytes 786440 | tf_op jit(solution)/shard_map/ppermute | solution.py:22
  144.4 8.4 %collective-permute-start.29 = (f32[256,256]{1,0:T(8,128)}, f32[256,256]{1,0:T(8,128)}, u32[]{:S(2)}, u32[]{:S(2)}) collective-permute-start(f32[256,256]{1,0:T(8,128)} %get-tuple-element.209), channel_id=1, source_target_pairs={{0,4},{1,5},{2,6},{3,7},{4,0},{5,1},{6,2},{7,3},{8,12},{9,13},{10,... | collective-permute-start | bytes 786440 | tf_op jit(solution)/shard_map/ppermute | solution.py:22
  153.9 7.3 %collective-permute-start.28 = (f32[256,256]{1,0:T(8,128)S(1)}, f32[256,256]{1,0:T(8,128)S(1)}, u32[]{:S(2)}, u32[]{:S(2)}) collective-permute-start(f32[256,256]{1,0:T(8,128)S(1)} %get-tuple-element.206), channel_id=1, source_target_pairs={{0,4},{1,5},{2,6},{3,7},{4,0},{5,1},{6,2},{7,3},{8,12},{9,13},{10,... | collective-permute-start | bytes 786440 | tf_op jit(solution)/shard_map/ppermute | solution.py:22
  155.5 6.9 %collective-permute-start.30 = (f32[256,256]{1,0:T(8,128)S(1)}, f32[256,256]{1,0:T(8,128)S(1)}, u32[]{:S(2)}, u32[]{:S(2)}) collective-permute-start(f32[256,256]{1,0:T(8,128)S(1)} %get-tuple-element.207), channel_id=1, source_target_pairs={{0,2},{1,3},{2,0},{3,1},{4,6},{5,7},{6,4},{7,5},{8,10},{9,11},{10,... | collective-permute-start | bytes 786440 | tf_op jit(solution)/shard_map/ppermute | solution.py:22
  166.0 9.2 %collective-permute-start.34 = (f32[256,128]{1,0:T(8,128)S(1)}, f32[256,128]{1,0:T(8,128)S(1)}, u32[]{:S(2)}, u32[]{:S(2)}) collective-permute-start(f32[256,128]{1,0:T(8,128)S(1)} %fusion.63), channel_id=1, source_target_pairs={{0,16},{8,24},{16,0},{24,8},{1,17},{9,25},{17,1},{25,9},{2,18},{10... | collective-permute-start | bytes 393224 | tf_op jit(solution)/shard_map/ppermute | solution.py:22
  166.5 9.1 %collective-permute-start.33 = (f32[256,128]{1,0:T(8,128)S(1)}, f32[256,128]{1,0:T(8,128)S(1)}, u32[]{:S(2)}, u32[]{:S(2)}) collective-permute-start(f32[256,128]{1,0:T(8,128)S(1)} %fusion.66), channel_id=1, source_target_pairs={{0,8},{8,0},{16,24},{24,16},{1,9},{9,1},{17,25},{25,17},{2,10},{10... | collective-permute-start | bytes 393224 | tf_op jit(solution)/shard_map/ppermute | solution.py:22
  175.7 8.3 %collective-permute-start.38 = (f32[256,128]{1,0:T(8,128)S(1)}, f32[256,128]{1,0:T(8,128)S(1)}, u32[]{:S(2)}, u32[]{:S(2)}) collective-permute-start(f32[256,128]{1,0:T(8,128)S(1)} %add.503), channel_id=1, source_target_pairs={{0,8},{8,0},{16,24},{24,16},{1,9},{9,1},{17,25},{25,17},{2,10},{10... | collective-permute-start | bytes 393224 | tf_op jit(solution)/shard_map/ppermute | solution.py:22
  175.7 12.9 %collective-permute-start.37 = (f32[256,128]{1,0:T(8,128)S(1)}, f32[256,128]{1,0:T(8,128)S(1)}, u32[]{:S(2)}, u32[]{:S(2)}) collective-permute-start(f32[256,128]{1,0:T(8,128)S(1)} %add.502), channel_id=1, source_target_pairs={{0,16},{8,24},{16,0},{24,8},{1,17},{9,25},{17,1},{25,9},{2,18},{10... | collective-permute-start | bytes 393224 | tf_op jit(solution)/shard_map/ppermute | solution.py:22
  177.8 12.4 %collective-permute-start.36 = (f32[256,128]{1,0:T(8,128)S(1)}, f32[256,128]{1,0:T(8,128)S(1)}, u32[]{:S(2)}, u32[]{:S(2)}) collective-permute-start(f32[256,128]{1,0:T(8,128)S(1)} %fusion.65), channel_id=1, source_target_pairs={{0,16},{8,24},{16,0},{24,8},{1,17},{9,25},{17,1},{25,9},{2,18},{10... | collective-permute-start | bytes 393224 | tf_op jit(solution)/shard_map/ppermute | solution.py:22
  178.7 11.5 %collective-permute-start.35 = (f32[256,128]{1,0:T(8,128)S(1)}, f32[256,128]{1,0:T(8,128)S(1)}, u32[]{:S(2)}, u32[]{:S(2)}) collective-permute-start(f32[256,128]{1,0:T(8,128)S(1)} %fusion.64), channel_id=1, source_target_pairs={{0,8},{8,0},{16,24},{24,16},{1,9},{9,1},{17,25},{25,17},{2,10},{10... | collective-permute-start | bytes 393224 | tf_op jit(solution)/shard_map/ppermute | solution.py:22
  190.3 6.3 %collective-permute-start.40 = (f32[256,128]{1,0:T(8,128)S(1)}, f32[256,128]{1,0:T(8,128)S(1)}, u32[]{:S(2)}, u32[]{:S(2)}) collective-permute-start(f32[256,128]{1,0:T(8,128)S(1)} %add.514), channel_id=1, source_target_pairs={{0,8},{8,0},{16,24},{24,16},{1,9},{9,1},{17,25},{25,17},{2,10},{10... | collective-permute-start | bytes 393224 | tf_op jit(solution)/shard_map/ppermute | solution.py:22
  190.3 8.2 %collective-permute-start.39 = (f32[256,128]{1,0:T(8,128)S(1)}, f32[256,128]{1,0:T(8,128)S(1)}, u32[]{:S(2)}, u32[]{:S(2)}) collective-permute-start(f32[256,128]{1,0:T(8,128)S(1)} %add.513), channel_id=1, source_target_pairs={{0,16},{8,24},{16,0},{24,8},{1,17},{9,25},{17,1},{25,9},{2,18},{10... | collective-permute-start | bytes 393224 | tf_op jit(solution)/shard_map/ppermute | solution.py:22
  194.3 10.0 %collective-permute-start.45 = (f32[1024,128]{1,0:T(8,128)S(1)}, f32[1024,128]{1,0:T(8,128)S(1)}, u32[]{:S(2)}, u32[]{:S(2)}) collective-permute-start(f32[1024,128]{1,0:T(8,128)S(1)} %fusion.36), channel_id=1, source_target_pairs={{0,1},{1,0},{2,3},{3,2},{4,5},{5,4},{6,7},{7,6},{8,9},{9,8},{10,11... | collective-permute-start | bytes 1572872 | tf_op jit(solution)/shard_map/ppermute | solution.py:22
  199.6 9.3 %collective-permute-start.56 = (f32[512,128]{1,0:T(8,128)S(1)}, f32[512,128]{1,0:T(8,128)S(1)}, u32[]{:S(2)}, u32[]{:S(2)}) collective-permute-start(f32[512,128]{1,0:T(8,128)S(1)} %get-tuple-element.128), channel_id=1, source_target_pairs={{0,4},{1,5},{2,6},{3,7},{4,0},{5,1},{6,2},{7,3},{8,12},{9,13},{10,... | collective-permute-start | bytes 786440 | tf_op jit(solution)/shard_map/ppermute | solution.py:22
  200.6 13.1 %collective-permute-start.55 = (f32[512,128]{1,0:T(8,128)S(1)}, f32[512,128]{1,0:T(8,128)S(1)}, u32[]{:S(2)}, u32[]{:S(2)}) collective-permute-start(f32[512,128]{1,0:T(8,128)S(1)} %get-tuple-element.134), channel_id=1, source_target_pairs={{0,4},{1,5},{2,6},{3,7},{4,0},{5,1},{6,2},{7,3},{8,12},{9,13},{10,... | collective-permute-start | bytes 786440 | tf_op jit(solution)/shard_map/ppermute | solution.py:22
  202.2 7.3 %collective-permute-start.47 = (f32[512,128]{1,0:T(8,128)S(1)}, f32[512,128]{1,0:T(8,128)S(1)}, u32[]{:S(2)}, u32[]{:S(2)}) collective-permute-start(f32[512,128]{1,0:T(8,128)S(1)} %get-tuple-element.127), channel_id=1, source_target_pairs={{0,2},{1,3},{2,0},{3,1},{4,6},{5,7},{6,4},{7,5},{8,10},{9,11},{10,... | collective-permute-start | bytes 786440 | tf_op jit(solution)/shard_map/ppermute | solution.py:22
  203.3 6.3 %collective-permute-start.50 = (f32[1024,128]{1,0:T(8,128)S(1)}, f32[1024,128]{1,0:T(8,128)S(1)}, u32[]{:S(2)}, u32[]{:S(2)}) collective-permute-start(f32[1024,128]{1,0:T(8,128)S(1)} %fusion.42), channel_id=1, source_target_pairs={{0,1},{1,0},{2,3},{3,2},{4,5},{5,4},{6,7},{7,6},{8,9},{9,8},{10,11... | collective-permute-start | bytes 1572872 | tf_op jit(solution)/shard_map/ppermute | solution.py:22
  204.3 6.4 %collective-permute-start.44 = (f32[1024,128]{1,0:T(8,128)S(1)}, f32[1024,128]{1,0:T(8,128)S(1)}, u32[]{:S(2)}, u32[]{:S(2)}) collective-permute-start(f32[1024,128]{1,0:T(8,128)S(1)} %fusion.33), channel_id=1, source_target_pairs={{0,1},{1,0},{2,3},{3,2},{4,5},{5,4},{6,7},{7,6},{8,9},{9,8},{10,11... | collective-permute-start | bytes 1572872 | tf_op jit(solution)/shard_map/ppermute | solution.py:22
  208.9 19.3 %collective-permute-start.46 = (f32[512,128]{1,0:T(8,128)S(1)}, f32[512,128]{1,0:T(8,128)S(1)}, u32[]{:S(2)}, u32[]{:S(2)}) collective-permute-start(f32[512,128]{1,0:T(8,128)S(1)} %get-tuple-element.139), channel_id=1, source_target_pairs={{0,2},{1,3},{2,0},{3,1},{4,6},{5,7},{6,4},{7,5},{8,10},{9,11},{10,... | collective-permute-start | bytes 786440 | tf_op jit(solution)/shard_map/ppermute | solution.py:22
  209.7 11.9 %collective-permute-start.52 = (f32[1024,128]{1,0:T(8,128)S(1)}, f32[1024,128]{1,0:T(8,128)S(1)}, u32[]{:S(2)}, u32[]{:S(2)}) collective-permute-start(f32[1024,128]{1,0:T(8,128)S(1)} %fusion.45), channel_id=1, source_target_pairs={{0,1},{1,0},{2,3},{3,2},{4,5},{5,4},{6,7},{7,6},{8,9},{9,8},{10,11... | collective-permute-start | bytes 1572872 | tf_op jit(solution)/shard_map/ppermute | solution.py:22
  210.7 10.1 %collective-permute-start.57 = (f32[512,128]{1,0:T(8,128)S(1)}, f32[512,128]{1,0:T(8,128)S(1)}, u32[]{:S(2)}, u32[]{:S(2)}) collective-permute-start(f32[512,128]{1,0:T(8,128)S(1)} %add.564), channel_id=1, source_target_pairs={{0,2},{1,3},{2,0},{3,1},{4,6},{5,7},{6,4},{7,5},{8,10},{9,11},{10,... | collective-permute-start | bytes 786440 | tf_op jit(solution)/shard_map/ppermute | solution.py:22
  212.7 17.0 %collective-permute-start.48 = (f32[512,128]{1,0:T(8,128)S(1)}, f32[512,128]{1,0:T(8,128)S(1)}, u32[]{:S(2)}, u32[]{:S(2)}) collective-permute-start(f32[512,128]{1,0:T(8,128)S(1)} %add.549), channel_id=1, source_target_pairs={{0,4},{1,5},{2,6},{3,7},{4,0},{5,1},{6,2},{7,3},{8,12},{9,13},{10,... | collective-permute-start | bytes 786440 | tf_op jit(solution)/shard_map/ppermute | solution.py:22
  213.8 13.8 %collective-permute-start.59 = (f32[512,128]{1,0:T(8,128)S(1)}, f32[512,128]{1,0:T(8,128)S(1)}, u32[]{:S(2)}, u32[]{:S(2)}) collective-permute-start(f32[512,128]{1,0:T(8,128)S(1)} %get-tuple-element.159), channel_id=1, source_target_pairs={{0,4},{1,5},{2,6},{3,7},{4,0},{5,1},{6,2},{7,3},{8,12},{9,13},{10,... | collective-permute-start | bytes 786440 | tf_op jit(solution)/shard_map/ppermute | solution.py:22
  220.9 8.9 %collective-permute-start.53 = (f32[512,128]{1,0:T(8,128)S(1)}, f32[512,128]{1,0:T(8,128)S(1)}, u32[]{:S(2)}, u32[]{:S(2)}) collective-permute-start(f32[512,128]{1,0:T(8,128)S(1)} %get-tuple-element.143), channel_id=1, source_target_pairs={{0,2},{1,3},{2,0},{3,1},{4,6},{5,7},{6,4},{7,5},{8,10},{9,11},{10,... | collective-permute-start | bytes 786440 | tf_op jit(solution)/shard_map/ppermute | solution.py:22
  222.1 11.1 %collective-permute-start.58 = (f32[512,128]{1,0:T(8,128)S(1)}, f32[512,128]{1,0:T(8,128)S(1)}, u32[]{:S(2)}, u32[]{:S(2)}) collective-permute-start(f32[512,128]{1,0:T(8,128)S(1)} %get-tuple-element.157), channel_id=1, source_target_pairs={{0,4},{1,5},{2,6},{3,7},{4,0},{5,1},{6,2},{7,3},{8,12},{9,13},{10,... | collective-permute-start | bytes 786440 | tf_op jit(solution)/shard_map/ppermute | solution.py:22
  227.6 11.5 %collective-permute-start.51 = (f32[512,128]{1,0:T(8,128)S(1)}, f32[512,128]{1,0:T(8,128)S(1)}, u32[]{:S(2)}, u32[]{:S(2)}) collective-permute-start(f32[512,128]{1,0:T(8,128)S(1)} %get-tuple-element.153), channel_id=1, source_target_pairs={{0,2},{1,3},{2,0},{3,1},{4,6},{5,7},{6,4},{7,5},{8,10},{9,11},{10,... | collective-permute-start | bytes 786440 | tf_op jit(solution)/shard_map/ppermute | solution.py:22
  228.2 10.8 %collective-permute-start.60 = (f32[512,128]{1,0:T(8,128)S(1)}, f32[512,128]{1,0:T(8,128)S(1)}, u32[]{:S(2)}, u32[]{:S(2)}) collective-permute-start(f32[512,128]{1,0:T(8,128)S(1)} %add.567), channel_id=1, source_target_pairs={{0,2},{1,3},{2,0},{3,1},{4,6},{5,7},{6,4},{7,5},{8,10},{9,11},{10,... | collective-permute-start | bytes 786440 | tf_op jit(solution)/shard_map/ppermute | solution.py:22
  229.8 9.2 %collective-permute-start.54 = (f32[512,128]{1,0:T(8,128)S(1)}, f32[512,128]{1,0:T(8,128)S(1)}, u32[]{:S(2)}, u32[]{:S(2)}) collective-permute-start(f32[512,128]{1,0:T(8,128)S(1)} %add.561), channel_id=1, source_target_pairs={{0,4},{1,5},{2,6},{3,7},{4,0},{5,1},{6,2},{7,3},{8,12},{9,13},{10,... | collective-permute-start | bytes 786440 | tf_op jit(solution)/shard_map/ppermute | solution.py:22
  (30 other events, 172.6 us)
